TPU v7x, 32 devices: a whole 2x2x4 slice. The times are simulated.
32 devices in a mesh: band: 4 (over x, core), space: 8 (over z, y).
Axes of the slice: x: 2, y: 2, z: 4, core: 2. Of those that a mesh axis runs over, the one named last changes fastest.
Arguments:
- orbitals: bfloat16 [96, 128, 16, 128], P('band', 'space'), may hold values from -0.796875 to 0.796875
- occupations: float32 [96], P('band'), may hold values from 0.5 to 2
- potential_in: float32 [128, 16, 128], P('space'), may hold values from -6 to 6
- ionic_potential: float32 [128, 16, 128], P('space'), may hold values from -6 to 6
- hartree_prev: float32 [128, 16, 128], P('space'), may hold values from -6 to 6
- projectors: bfloat16 [64, 13, 16, 256], P('space'), may hold values from -0.375 to 0.375
- box_start: int32 [3, 64], replicated, may hold values from 0 to 127, as said below
- coupling: float32 [13, 13], replicated, may hold values from -6 to 6
Outputs:
- applied: bfloat16 [96, 128, 16, 128], P('band', 'space')
- potential: float32 [128, 16, 128], P('space')
Inputs may be any that keep to these rules, and one draw needn't show every extreme that they name: `box_start`: column a holds the first plane, row and column of atom a's box. The plane lies among the 16 planes that begin at (a // 8) * 16; the row is at most 0 and the column at most 112. Atom 0's box begins at plane, row and column 0, and the last atom's box begins on plane 128 - 1.
All inputs are finite; a program needn't handle non-finite values.
Results may differ from a plain program's by a relative error of at most 0.013.
Values may be sent and summed in bfloat16 or wider, within the bound.
No kernel may reach another device: no remote copies, remote signals or barrier semaphores. Data moves between devices by JAX's collectives and lax.ppermute only.
A program may use at most 128 MiB of HBM per device.

v0:
```python
import math

import jax
import jax.numpy as jnp
from jax import lax
from jax.sharding import PartitionSpec as P

SWEEPS = 2


screening = 0.25
four_pi = 4.0 * math.pi
stencil_far = ((1, 4.0 / 3.0), (2, -1.0 / 12.0))


def padded(cells, sides, width):
    for axis, dim in sides:
        count = lax.axis_size(axis)
        head = lax.slice_in_dim(cells, 0, width, axis=dim)
        tail = lax.slice_in_dim(cells, cells.shape[dim] - width, cells.shape[dim], axis=dim)
        cells = jnp.concatenate(
            [
                lax.ppermute(tail, axis, [(i, (i + 1) % count) for i in range(count)]),
                cells,
                lax.ppermute(head, axis, [((i + 1) % count, i) for i in range(count)]),
            ],
            axis=dim,
        )
    return cells


def from_behind(block, axis, distance):
    devices = range(lax.axis_size(axis))
    route = [((i - distance) % len(devices), i) for i in devices]
    return lax.ppermute(block, axis, route)


def embed_atom(beta_atom, row, column, rows_y, cols_z):
    nproj_here, width, square = beta_atom.shape
    steps_box = jnp.arange(width, dtype=jnp.int32)
    row_hot = (jnp.arange(rows_y, dtype=jnp.int32)[None, :] == (row + steps_box)[:, None]).astype(
        jnp.float32
    )
    col_hot = (
        jnp.arange(cols_z, dtype=jnp.int32)[None, :] == (column + steps_box)[:, None]
    ).astype(jnp.float32)
    cube = beta_atom.astype(jnp.float32).reshape(nproj_here, width, width, width)
    placed = jnp.einsum("pijk,kz->pijz", cube, col_hot, precision=lax.Precision.HIGHEST)
    placed = jnp.einsum("pijz,jy->piyz", placed, row_hot, precision=lax.Precision.HIGHEST)
    return placed.astype(jnp.bfloat16)


def gather_coefficients(field, beta_block, starts, row_start, col_start):
    rows_y = field.shape[2]
    cols_z = field.shape[3]
    width = beta_block.shape[2]

    def per_atom(inputs):
        beta_atom, plane, row, column = inputs
        placed = embed_atom(beta_atom, row, column, rows_y, cols_z)
        slab = lax.dynamic_slice_in_dim(field, plane, width, 1)
        return jnp.einsum("piyz,oiyz->po", placed, slab, preferred_element_type=jnp.float32)

    return lax.map(per_atom, (beta_block, starts, row_start, col_start))


def weigh(coupling, coefficients):
    return jnp.einsum(
        "pq,aqo->apo", coupling, coefficients, precision=lax.Precision.HIGHEST
    ).astype(jnp.bfloat16)


def deposit(buffer, beta_block, weighted, starts, row_start, col_start):
    rows_y = buffer.shape[2]
    cols_z = buffer.shape[3]
    width = beta_block.shape[2]

    def add_atom(atom_index, summed):
        placed = embed_atom(
            beta_block[atom_index], row_start[atom_index], col_start[atom_index], rows_y, cols_z
        )
        update = jnp.einsum(
            "piyz,po->oiyz", placed, weighted[atom_index], preferred_element_type=jnp.float32
        )
        plane = starts[atom_index]
        current = lax.dynamic_slice_in_dim(summed, plane, width, 1)
        return lax.dynamic_update_slice_in_dim(summed, current + update, plane, 1)

    return lax.fori_loop(0, beta_block.shape[0], add_atom, buffer)


def relax_slab(field, source_ext, margin):
    inner = field[1:-1]
    neighbours = field[2:] + field[:-2]
    neighbours = neighbours + jnp.roll(inner, 1, 1) + jnp.roll(inner, -1, 1)
    neighbours = neighbours + jnp.roll(inner, 1, 2) + jnp.roll(inner, -1, 2)
    total = source_ext.shape[0]
    cropped = source_ext[margin : total - margin]
    return (neighbours + cropped) / (6.0 + screening)


def local(
    orbitals,
    occupations,
    potential_in,
    ionic_potential,
    hartree_prev,
    projectors,
    box_start,
    coupling,
):
    orbit_count, planes, rows_y, cols_z = orbitals.shape
    atoms_dev = projectors.shape[0]
    n_space = lax.axis_size("space")
    domain = lax.axis_index("space")
    center = orbitals.astype(jnp.float32)
    extended = padded(orbitals, (("space", 1),), 2)
    laplacian = -7.5 * center
    for distance, weight in stencil_far:
        upper = extended[:, 2 + distance : 2 + distance + planes].astype(jnp.float32)
        lower = extended[:, 2 - distance : 2 - distance + planes].astype(jnp.float32)
        laplacian = laplacian + weight * (upper + lower)
        for dimension in (2, 3):
            laplacian = laplacian + weight * (
                jnp.roll(center, distance, dimension) + jnp.roll(center, -distance, dimension)
            )
    local_cols = lax.dynamic_slice_in_dim(box_start, domain * atoms_dev, atoms_dev, 1)
    local_offset = local_cols[0] % planes
    following = from_behind(orbitals, "space", -1)
    joined = jnp.concatenate([orbitals, following], axis=1)
    coefficients = gather_coefficients(
        joined, projectors, local_offset, local_cols[1], local_cols[2]
    )
    weighted = weigh(coupling, coefficients)
    buffer = jnp.zeros((orbit_count, 2 * planes, rows_y, cols_z), jnp.float32)
    buffer = deposit(buffer, projectors, weighted, local_offset, local_cols[1], local_cols[2])
    carried = from_behind(buffer[:, planes:], "space", 1)
    nonlocal_part = buffer[:, :planes] + carried
    applied = (-0.5 * laplacian + potential_in[None] * center + nonlocal_part).astype(jnp.bfloat16)
    partial_density = jnp.sum(occupations[:, None, None, None] * center * center, axis=0)
    cell_count = planes * rows_y * cols_z * n_space
    density = lax.psum(partial_density.astype(jnp.bfloat16), "band").astype(jnp.float32)
    charge_total = lax.psum(jnp.sum(partial_density), ("band", "space"))
    source = four_pi * (density - charge_total / cell_count)
    hartree = hartree_prev
    stacked = jnp.stack([hartree, source])
    wide = padded(stacked.astype(jnp.bfloat16), (("space", 1),), SWEEPS).astype(stacked.dtype)
    field = wide[0]
    source_ext = wide[1]
    for sweep_index in range(SWEEPS):
        field = relax_slab(field, source_ext, sweep_index + 1)
    hartree = field
    potential = ionic_potential + hartree - jnp.cbrt(3.0 * density / math.pi)
    return (applied, potential)


def solution(mesh):
    placed = (
        P("band", "space", None, None),
        P("band"),
        P("space", None, None),
        P("space", None, None),
        P("space", None, None),
        P("space", None, None, None),
        P(),
        P(),
    )
    return jax.shard_map(
        local,
        mesh=mesh,
        in_specs=placed,
        out_specs=(P("band", "space", None, None), P("space", None, None)),
        check_vma=False,
    )
```

profile of v0, /device:TPU:0, one launch (start us, length us, event | category | flops | bytes accessed | tf_op | source)
XLA Modules:
  0.0 411.0 jit_solution(4972142981431228359)
XLA Ops:
  7.2 3.2 fusion.45
  12.3 6.0 %collective-permute-start = (bf16[24,2,16,128]{3,2,1,0:T(8,128)(2,1)}, bf16[24,2,16,128]{3,2,1,0:T(8,128)(2,1)}, u32[]{:S(2)}, u32[]{:S(2)}) collective-permute-start(bf16[24,2,16,128]{3,2,1,0:T(8,128)(2,1)} %get-tuple-element.195), channel_id=1, source_target_pairs={{1,0},{2,1},{3,2},{4,3},{5,4},{6,5},{7,6},{0,7},{9,8},{10,9},{11,1... | collective-permute-start | bytes 589832 | tf_op jit(solution)/shard_map/ppermute | solution.py:25
  19.3 4.8 %collective-permute-start.2 = (bf16[24,16,16,128]{3,0,2,1:T(8,128)(2,1)S(1)}, bf16[24,16,16,128]{3,0,2,1:T(8,128)(2,1)}, u32[]{:S(2)}, u32[]{:S(2)}) collective-permute-start(bf16[24,16,16,128]{3,0,2,1:T(8,128)(2,1)S(1)} %copy.11), channel_id=1, source_target_pairs={{1,0},{2,1},{3,2},{4,3},{5,4},{6,5},{7,6},{0,7},{9,8},{10,9},{11,1... | collective-permute-start | bytes 4718600 | tf_op jit(solution)/shard_map/ppermute | solution.py:35
  25.4 3.5 fusion.76
  28.9 3.3 fusion.75
  32.2 3.3 fusion.74
  35.5 3.5 fusion.72
  39.2 3.4 fusion.70
  42.5 3.4 fusion.71
  45.9 47.4 %psum.15 = f32[]{:T(128)} all-reduce(f32[]{:T(128)} %get-tuple-element.165), channel_id=1, replica_groups=mesh['band'=4,'space'=8] {'band','space'}, use_global_device_ids=true, to_apply=%region_7.8 | all-reduce | flops 1 | bytes 8 | tf_op jit(solution)/shard_map/psum | solution.py:143
  100.2 3.3 pad_maximum_fusion
  103.5 72.8 %while.23 = (s32[]{:T(128)}, f32[8,13,24]{2,1,0:T(8,128)S(1)}, s32[8]{0:T(128)S(1)}, bf16[8,13,16,256]{3,2,1,0:T(8,128)(2,1)}, s32[8]{0:T(128)S(1)}, /*index=5*/...) while((s32[]{:T(128)}, f32[8,13,24]{2,1,0:T(8,128)S(1)}, ...), condition=%wide.region_1.2_spmd, body=%wide.region_0.1_spmd.sunk | while | flops 115869984 | bytes 19808740 | solution.py:64
  176.5 3.3 broadcast_in_dim.28.clone
  179.8 132.7 %while.24 = (s32[]{:T(128)}, f32[24,32,16,128]{3,2,1,0:T(8,128)}, s32[8]{0:T(128)S(1)}, bf16[8,13,24]{2,1,0:T(8,128)(2,1)S(1)}, s32[8]{0:T(128)S(1)}, /*index=5*...) while((s32[]{:T(128)}, f32[24,32,16,128]{3,2,1,0:T(8,128)}, ...), condition=%wide.region_3.4_spmd, body=%wide.region_2.3_spmd.sunk | while | flops 116656416 | bytes 68563480 | solution.py:89
  193.8 2.6 copy-done.3
  210.4 2.6 copy-done.3
  227.0 2.6 copy-done.3
  243.6 2.6 copy-done.3
  260.2 2.6 copy-done.3
  276.8 2.6 copy-done.3
  293.3 2.6 copy-done.3
  309.9 2.6 copy-done.3
  321.0 65.7 %collective-permute-done.3 = f32[24,16,16,128]{3,2,1,0:T(8,128)S(1)} collective-permute-done((f32[24,16,16,128]{3,2,1,0:T(8,128)S(1)}, f32[24,16,16,128]{3,2,1,0:T(8,128)S(1)}, u32[]{:S(2)}, u32[]{:S(2)}) %collective-permute-start.3) | collective-permute-done | bytes 3145760 | tf_op jit(solution)/shard_map/ppermute | solution.py:35
  388.4 15.7 %fusion.41 = bf16[24,16,16,128]{3,2,1,0:T(8,128)(2,1)} fusion(f32[24,16,15,128]{3,2,1,0:T(8,128)S(1)} %copy-done.6, f32[24,16,1,128]{3,2,1,0:T(1,128)} %get-tuple-element.214, f32[24,16,1,128]{3,2,1,0:T(1,128)S(1)} %get-tuple-element.213, f32[24,16,15,128]{3,2,1,0:T(8,128)S(1)} %copy-done.5, f32[24,16,16,127]{3,2,1,0:T(8,128)} %get-tuple-element.208, ...), kind=kLoop, calls=%fused_computation.48 | loop fusion | flops 29884416 | bytes 41025536 | tf_op jit(solution)/shard_map/convert_element_type | solution.py:139
  (307 shorter events, 173.9 us)
Async XLA Ops:
  7.2 169.1 %copy-start = (f32[13,13]{1,0:T(8,128)S(1)}, f32[13,13]{1,0:T(8,128)}, u32[]{:S(2)}) copy-start(f32[13,13]{1,0:T(8,128)} %param.19) | copy-start | bytes 2032
  7.2 11.1 %copy-start.2 = (bf16[24,16,16,128]{3,2,1,0:T(8,128)(2,1)S(1)}, bf16[24,16,16,128]{3,2,1,0:T(8,128)(2,1)}, u32[]{:S(2)}) copy-start(bf16[24,16,16,128]{3,2,1,0:T(8,128)(2,1)} %param.12) | copy-start | bytes 4718596
  7.2 86.8 %all-reduce.2.cloned.1.call-start = ((), (), s32[]{:S(2)}) async-start(), calls=%async_computation | async-start | bytes 131072 | tf_op jit(solution)/shard_map/psum | solution.py:142
  12.3 307.5 %collective-permute-start = (bf16[24,2,16,128]{3,2,1,0:T(8,128)(2,1)}, bf16[24,2,16,128]{3,2,1,0:T(8,128)(2,1)}, u32[]{:S(2)}, u32[]{:S(2)}) collective-permute-start(bf16[24,2,16,128]{3,2,1,0:T(8,128)(2,1)} %get-tuple-element.195), channel_id=1, source_target_pairs={{1,0},{2,1},{3,2},{4,3},{5,4},{6,5},{7,6},{0,7},{9,8},{10,9},{11,1... | collective-permute-start | bytes 589832 | tf_op jit(solution)/shard_map/ppermute | solution.py:25
  18.3 299.5 %collective-permute-start.1 = (bf16[24,2,16,128]{3,2,1,0:T(8,128)(2,1)}, bf16[24,2,16,128]{3,2,1,0:T(8,128)(2,1)}, u32[]{:S(2)}, u32[]{:S(2)}) collective-permute-start(bf16[24,2,16,128]{3,2,1,0:T(8,128)(2,1)} %get-tuple-element.196), channel_id=1, source_target_pairs={{0,1},{1,2},{2,3},{3,4},{4,5},{5,6},{6,7},{7,0},{8,9},{9,10},{10,1... | collective-permute-start | bytes 589832 | tf_op jit(solution)/shard_map/ppermute | solution.py:23
  19.3 80.9 %collective-permute-start.2 = (bf16[24,16,16,128]{3,0,2,1:T(8,128)(2,1)S(1)}, bf16[24,16,16,128]{3,0,2,1:T(8,128)(2,1)}, u32[]{:S(2)}, u32[]{:S(2)}) collective-permute-start(bf16[24,16,16,128]{3,0,2,1:T(8,128)(2,1)S(1)} %copy.11), channel_id=1, source_target_pairs={{1,0},{2,1},{3,2},{4,3},{5,4},{6,5},{7,6},{0,7},{9,8},{10,9},{11,1... | collective-permute-start | bytes 4718600 | tf_op jit(solution)/shard_map/ppermute | solution.py:35
  95.5 220.7 %collective-permute-start.4 = (bf16[2,2,16,128]{3,2,1,0:T(8,128)(2,1)}, bf16[2,2,16,128]{3,2,1,0:T(8,128)(2,1)S(1)}, u32[]{:S(2)}, u32[]{:S(2)}) collective-permute-start(bf16[2,2,16,128]{3,2,1,0:T(8,128)(2,1)} %get-tuple-element.231), channel_id=1, source_target_pairs={{0,1},{1,2},{2,3},{3,4},{4,5},{5,6},{6,7},{7,0},{8,9},{9,10},{10,1... | collective-permute-start | bytes 49160 | tf_op jit(solution)/shard_map/ppermute | solution.py:23
  98.0 218.1 %collective-permute-start.5 = (bf16[2,2,16,128]{3,2,1,0:T(8,128)(2,1)S(1)}, bf16[2,2,16,128]{3,2,1,0:T(8,128)(2,1)S(1)}, u32[]{:S(2)}, u32[]{:S(2)}) collective-permute-start(bf16[2,2,16,128]{3,2,1,0:T(8,128)(2,1)S(1)} %get-tuple-element.232), channel_id=1, source_target_pairs={{1,0},{2,1},{3,2},{4,3},{5,4},{6,5},{7,6},{0,7},{9,8},{10,9},{11,1... | collective-permute-start | bytes 49160 | tf_op jit(solution)/shard_map/ppermute | solution.py:25
  186.8 5.9 %slice-start = ((s8[6291456]{0:T(1024)(128)(4,1)}), s8[4194304]{0:T(1024)(128)(4,1)S(1)}, s32[]{:S(2)}) async-start(s8[6291456]{0:T(1024)(128)(4,1)} %bitcast.137), calls=%async_computation.1 | async-start | bytes 8388608 | tf_op jit(solution)/shard_map/while
  187.8 4.8 %slice-start.1 = ((s8[6291456]{0:T(1024)(128)(4,1)}), s8[2097152]{0:T(1024)(128)(4,1)S(1)}, s32[]{:S(2)}) async-start(s8[6291456]{0:T(1024)(128)(4,1)} %bitcast.137), calls=%async_computation.2 | async-start | bytes 4194304 | tf_op jit(solution)/shard_map/while
  203.4 5.9 %slice-start = ((s8[6291456]{0:T(1024)(128)(4,1)}), s8[4194304]{0:T(1024)(128)(4,1)S(1)}, s32[]{:S(2)}) async-start(s8[6291456]{0:T(1024)(128)(4,1)} %bitcast.137), calls=%async_computation.1 | async-start | bytes 8388608 | tf_op jit(solution)/shard_map/while
  204.4 4.8 %slice-start.1 = ((s8[6291456]{0:T(1024)(128)(4,1)}), s8[2097152]{0:T(1024)(128)(4,1)S(1)}, s32[]{:S(2)}) async-start(s8[6291456]{0:T(1024)(128)(4,1)} %bitcast.137), calls=%async_computation.2 | async-start | bytes 4194304 | tf_op jit(solution)/shard_map/while
  220.0 5.9 %slice-start = ((s8[6291456]{0:T(1024)(128)(4,1)}), s8[4194304]{0:T(1024)(128)(4,1)S(1)}, s32[]{:S(2)}) async-start(s8[6291456]{0:T(1024)(128)(4,1)} %bitcast.137), calls=%async_computation.1 | async-start | bytes 8388608 | tf_op jit(solution)/shard_map/while
  236.6 5.9 %slice-start = ((s8[6291456]{0:T(1024)(128)(4,1)}), s8[4194304]{0:T(1024)(128)(4,1)S(1)}, s32[]{:S(2)}) async-start(s8[6291456]{0:T(1024)(128)(4,1)} %bitcast.137), calls=%async_computation.1 | async-start | bytes 8388608 | tf_op jit(solution)/shard_map/while
  253.2 5.9 %slice-start = ((s8[6291456]{0:T(1024)(128)(4,1)}), s8[4194304]{0:T(1024)(128)(4,1)S(1)}, s32[]{:S(2)}) async-start(s8[6291456]{0:T(1024)(128)(4,1)} %bitcast.137), calls=%async_computation.1 | async-start | bytes 8388608 | tf_op jit(solution)/shard_map/while
  269.7 5.9 %slice-start = ((s8[6291456]{0:T(1024)(128)(4,1)}), s8[4194304]{0:T(1024)(128)(4,1)S(1)}, s32[]{:S(2)}) async-start(s8[6291456]{0:T(1024)(128)(4,1)} %bitcast.137), calls=%async_computation.1 | async-start | bytes 8388608 | tf_op jit(solution)/shard_map/while
  286.3 5.9 %slice-start = ((s8[6291456]{0:T(1024)(128)(4,1)}), s8[4194304]{0:T(1024)(128)(4,1)S(1)}, s32[]{:S(2)}) async-start(s8[6291456]{0:T(1024)(128)(4,1)} %bitcast.137), calls=%async_computation.1 | async-start | bytes 8388608 | tf_op jit(solution)/shard_map/while
  302.9 5.9 %slice-start = ((s8[6291456]{0:T(1024)(128)(4,1)}), s8[4194304]{0:T(1024)(128)(4,1)S(1)}, s32[]{:S(2)}) async-start(s8[6291456]{0:T(1024)(128)(4,1)} %bitcast.137), calls=%async_computation.1 | async-start | bytes 8388608 | tf_op jit(solution)/shard_map/while
  312.6 75.8 %slice-start.2 = ((s8[6291456]{0:T(1024)(128)(4,1)}), s8[4194304]{0:T(1024)(128)(4,1)S(1)}, s32[]{:S(2)}) async-start(s8[6291456]{0:T(1024)(128)(4,1)} %bitcast.139), calls=%async_computation.3 | async-start | bytes 8388608
  314.9 71.7 %collective-permute-start.3 = (f32[24,16,16,128]{3,2,1,0:T(8,128)S(1)}, f32[24,16,16,128]{3,2,1,0:T(8,128)S(1)}, u32[]{:S(2)}, u32[]{:S(2)}) collective-permute-start(f32[24,16,16,128]{3,2,1,0:T(8,128)S(1)} %slice.247), channel_id=1, source_target_pairs={{7,0},{0,1},{1,2},{2,3},{3,4},{4,5},{5,6},{6,7},{15,8},{8,9},{9,10... | collective-permute-start | bytes 9437192 | tf_op jit(solution)/shard_map/ppermute | solution.py:35
  316.5 71.9 %slice-start.3 = ((s8[6291456]{0:T(1024)(128)(4,1)}), s8[2097152]{0:T(1024)(128)(4,1)S(1)}, s32[]{:S(2)}) async-start(s8[6291456]{0:T(1024)(128)(4,1)} %bitcast.139), calls=%async_computation.4 | async-start | bytes 4194304
  316.9 71.5 %copy-start.6 = (f32[24,16,15,128]{3,2,1,0:T(8,128)S(1)}, f32[24,16,15,128]{3,2,1,0:T(8,128)}, u32[]{:S(2)}) copy-start(f32[24,16,15,128]{3,2,1,0:T(8,128)} %get-tuple-element.212) | copy-start | bytes 8847364
  317.8 70.6 %copy-start.5 = (f32[24,16,15,128]{3,2,1,0:T(8,128)S(1)}, f32[24,16,15,128]{3,2,1,0:T(8,128)}, u32[]{:S(2)}) copy-start(f32[24,16,15,128]{3,2,1,0:T(8,128)} %get-tuple-element.211) | copy-start | bytes 8847364
  388.4 15.8 %copy-start.1 = (f32[13,13]{1,0:T(8,128)S(1)}, f32[13,13]{1,0:T(8,128)}, u32[]{:S(2)}) copy-start(f32[13,13]{1,0:T(8,128)} %param.19) | copy-start | bytes 2032
  (28 other events, 79.2 us)
Sparse Core Ops, SparseCore 0:
  10.9 34.2 all-reduce.1
where the time goes:
time: 413 us; the launch traced here: 411 us
  local copies, waits for them, and re-layouts  143 us (35%)
  waiting for transfers between devices  65.7 us (16%)
  blocking collectives  47.4 us (11%)
  matrix products  47.1 us (11%)
  other arithmetic  45.4 us (11%)
  loops' own time  31.3 us (8%)
  starting transfers between devices  15.8 us (4%)
  between operations  15 us (4%)
    ppermute x2, waiting for transfers between devices, from_behind(): return lax.ppermute(block, axis, route)  65.7 us
    psum x1, blocking collectives, local(): charge_total = lax.psum(jnp.sum(partial_density), ('band', 'space'))  47.4 us
    while x64, local copies, waits for them, and re-layouts  24.6 us
    slice x8, local copies, waits for them, and re-layouts, local(): jnp.roll(center, -distance, dimension)  22.6 us
    dynamic_slice x32, local copies, waits for them, and re-layouts, gather_coefficients(): return lax.map(per_atom, (beta_block, starts, row_start, col_start))  22.2 us
    dynamic_slice x8, local copies, waits for them, and re-layouts, add_atom(): current = lax.dynamic_slice_in_dim(summed, plane, width, 1)  19.6 us
    dot_general x8, matrix products, add_atom(): jnp.einsum('piyz,po->oiyz', placed, weighted[atom_index], preferred_eleme...  18.8 us
    dot_general x16, matrix products, embed_atom(): jnp.einsum('pijz,jy->piyz', placed, row_hot, precision=lax.Precision.HIGH...  16.2 us
  transfers between devices with their start and end apart: 7, of which 1 were waited for; matrix products, arithmetic and copies ran while one was open for 46% of the time, Pallas kernels for 0%

commit v1 on v0

v1 whole, which is shorter than its diff:
```python
import functools
import math

import jax
import jax.numpy as jnp
import numpy as np
from jax import lax
from jax.experimental import pallas as pl
from jax.experimental.pallas import tpu as pltpu
from jax.sharding import PartitionSpec as P

SWEEPS = 2
LANES = 128
SLOT = 16

screening = 0.25
four_pi = 4.0 * math.pi
f32 = jnp.float32
bf16 = jnp.bfloat16


def vmem():
    return pl.BlockSpec(memory_space=pltpu.VMEM)


def smem():
    return pl.BlockSpec(memory_space=pltpu.SMEM)


def hbm():
    return pl.BlockSpec(memory_space=pl.ANY)


def spread_projectors(raw, atom, rows_ref):
    nproj, box, square = raw.shape
    flat = raw.reshape(nproj * box, square).astype(f32)
    for tile in range(square // LANES):
        rows_ref[atom, tile, : nproj * box] = flat[:, tile * LANES : (tile + 1) * LANES]
        rows_ref[atom, tile, nproj * box :] = jnp.zeros(
            (rows_ref.shape[2] - nproj * box, LANES), f32
        )


def place_plane(rows_ref, starts, plane, placed_ref, carried):
    atoms = rows_ref.shape[0]
    box = rows_ref.shape[2] // SLOT
    per_tile = LANES // box
    lane = lax.broadcasted_iota(jnp.int32, (SLOT, LANES), 1)

    def one(atom, _):
        offset = starts[0, atom]
        column = starts[1, atom]
        j = plane - offset
        if carried:
            j = j + box
        valid = jnp.logical_and(j >= 0, j < box)
        j = jnp.clip(j, 0, box - 1)
        low = jnp.where(valid, column, LANES)
        inside = jnp.logical_and(lane >= low, lane < low + box)
        for tile in range(box // per_tile):
            cells = rows_ref[atom, tile, pl.ds(j, SLOT, stride=box), :]
            for row in range(per_tile):
                shift = lax.rem(column + (LANES - box * row), LANES)
                moved = pltpu.roll(cells, shift, 1)
                placed_ref[
                    pl.ds(pl.multiple_of(atom * SLOT, SLOT), SLOT),
                    pl.ds((tile * per_tile + row) * LANES, LANES),
                ] = jnp.where(inside, moved, 0.0).astype(bf16)
        return 0

    lax.fori_loop(0, atoms, one, 0)


def turn_plane(field_ref, plane, wide_ref):
    count, _, rows, _ = field_ref.shape
    cells = field_ref[:, plane].astype(f32)
    wide_ref[...] = cells.reshape(count * rows, LANES)
    return jnp.concatenate(
        [wide_ref[pl.ds(r, count, stride=rows), :] for r in range(rows)], axis=1
    ).astype(bf16)


NT = (((1,), (1,)), ((), ()))


def density_kernel(occ, field_ref, out_ref):
    total = jnp.zeros(out_ref.shape, f32)
    for o in range(field_ref.shape[0]):
        cells = field_ref[o].astype(f32)
        total = total + (occ[o] * cells) * cells
    out_ref[...] = total


def coefficient_kernel(carried, starts, core, field_ref, *rest):
    if carried:
        mine_ref, other_ref, out_ref, rows_ref, placed_ref, wide_ref = rest
        half = mine_ref.shape[0]
        for q in range(half):
            spread_projectors(mine_ref[q], core[0] * half + q, rows_ref)
            spread_projectors(other_ref[q], (1 - core[0]) * half + q, rows_ref)
    else:
        proj_ref, out_ref, rows_ref, placed_ref, wide_ref = rest
        for q in range(proj_ref.shape[0]):
            spread_projectors(proj_ref[q], q, rows_ref)
    planes = field_ref.shape[1]
    out_ref[...] = jnp.zeros(out_ref.shape, f32)

    def one(plane, _):
        place_plane(rows_ref, starts, plane, placed_ref, carried)
        turned = turn_plane(field_ref, plane, wide_ref)
        out_ref[...] += lax.dot_general(
            turned, placed_ref[...], NT, preferred_element_type=f32
        )
        return 0

    lax.fori_loop(0, planes, one, 0)


def weigh(coef, coupling_ref):
    return lax.dot_general(
        coef, coupling_ref[...], (((1,), (0,)), ((), ())),
        precision=lax.Precision.HIGHEST, preferred_element_type=f32,
    ).astype(bf16)


def deposit(rows_ref, starts, weighted, placed_ref, sum_ref, planes, carried):
    count = weighted.shape[0]
    rows = placed_ref.shape[1] // LANES

    def one(plane, _):
        place_plane(rows_ref, starts, plane, placed_ref, carried)
        update = jnp.dot(weighted, placed_ref[...], preferred_element_type=f32)
        for r in range(rows):
            sum_ref[pl.ds(plane * rows + r, count, stride=planes * rows), :] = update[
                :, r * LANES : (r + 1) * LANES
            ]
        return 0

    lax.fori_loop(0, planes, one, 0)


def local_kernel(
    starts, core, field_ref, low_ref, high_ref, mine_ref, other_ref, part_ref, far_ref,
    coupling_ref, along_ref, across_ref, pot_ref, out_ref,
    rows_ref, placed_ref, sum_ref, ext_ref, sems,
):
    count, planes, rows, _ = field_ref.shape
    copies = [
        pltpu.make_async_copy(low_ref, ext_ref.at[:, 0:2], sems.at[0]),
        pltpu.make_async_copy(field_ref, ext_ref.at[:, 2 : 2 + planes], sems.at[1]),
        pltpu.make_async_copy(high_ref, ext_ref.at[:, 2 + planes : 4 + planes], sems.at[2]),
    ]
    for copy in copies:
        copy.start()
    half = mine_ref.shape[0]
    for q in range(half):
        spread_projectors(mine_ref[q], core[0] * half + q, rows_ref)
        spread_projectors(other_ref[q], (1 - core[0]) * half + q, rows_ref)
    weighted = weigh(part_ref[...] + far_ref[...], coupling_ref)
    deposit(rows_ref, starts, weighted, placed_ref, sum_ref, planes, True)
    for copy in copies:
        copy.wait()
    cells = planes * rows

    def one(o, _):
        ext = ext_ref[o].reshape((planes + 4) * rows, LANES)
        center = ext[2 * rows : 2 * rows + cells]
        stencil = jnp.dot(across_ref[...], ext, preferred_element_type=f32)
        stencil = stencil + jnp.dot(center, along_ref[...], preferred_element_type=f32)
        value = stencil * (-1.0 / 24.0) + pot_ref[...].reshape(cells, LANES) * center.astype(f32)
        nonlocal_part = sum_ref[pl.ds(pl.multiple_of(o * cells, cells), cells), :]
        out_ref[o] = (value + nonlocal_part).reshape(planes, rows, LANES)
        return 0

    lax.fori_loop(0, count, one, 0)


def final_kernel(
    starts, charge, acc_ref, proj_ref, part_ref, far_ref, coupling_ref,
    dens_ref, hart_ref, ionic_ref, below_ref, above_ref,
    out_ref, pot_ref, rows_ref, placed_ref, sum_ref,
):
    count, planes, rows, _ = out_ref.shape
    cells = planes * rows
    for q in range(proj_ref.shape[0]):
        spread_projectors(proj_ref[q], q, rows_ref)
    weighted = weigh(part_ref[...] + far_ref[:count], coupling_ref)
    deposit(rows_ref, starts, weighted, placed_ref, sum_ref, planes, False)

    def one(o, _):
        nonlocal_part = sum_ref[pl.ds(pl.multiple_of(o * cells, cells), cells), :]
        out_ref[o] = (acc_ref[o].reshape(cells, LANES) + nonlocal_part).reshape(
            planes, rows, LANES
        ).astype(bf16)
        return 0

    lax.fori_loop(0, count, one, 0)

    wide = planes + 4
    field = jnp.concatenate(
        [
            below_ref[count : count + 2 * rows].reshape(2, rows, LANES),
            hart_ref[...],
            above_ref[count : count + 2 * rows].reshape(2, rows, LANES),
        ],
        axis=0,
    )
    dens = jnp.concatenate(
        [
            below_ref[count + 2 * rows :].reshape(1, rows, LANES),
            dens_ref[...],
            above_ref[count + 2 * rows :].reshape(1, rows, LANES),
        ],
        axis=0,
    )
    source = four_pi * dens
    scale = 1.0 / (6.0 + screening)

    def relax(h, s):
        inner = h[1:-1]
        size = inner.shape
        flat = inner.reshape(size[0] * rows, LANES)
        across = pltpu.roll(flat, 1, 1) + pltpu.roll(flat, LANES - 1, 1)
        total = h[2:] + h[:-2] + across.reshape(size)
        total = total + pltpu.roll(inner, 1, 1) + pltpu.roll(inner, rows - 1, 1)
        return (total + s) * scale

    once = relax(field, source)
    twice = relax(once, source[1:-1])
    shift = charge[0] * (four_pi * scale * (1.0 + 6.0 * scale))
    third = (3.0 / math.pi) * dens_ref[...]
    root = jnp.exp(jnp.log(jnp.maximum(third, 1e-37)) * (1.0 / 3.0))
    root = (2.0 * root + third / jnp.maximum(root * root, 1e-30)) * (1.0 / 3.0)
    root = jnp.where(third > 0.0, root, 0.0)
    pot_ref[...] = ionic_ref[...] + twice - shift - root


def stencils(planes, rows):
    across = np.zeros((planes * rows, (planes + 4) * rows), np.float32)
    index = np.arange(planes * rows)
    plane, row = index // rows, index % rows
    for step, weight in ((1, 16.0), (2, -1.0)):
        for sign in (1, -1):
            np.add.at(across, (index, (plane + 2 + sign * step) * rows + row), weight)
            np.add.at(across, (index, (plane + 2) * rows + (row + sign * step) % rows), weight)
    along = np.zeros((LANES, LANES), np.float32)
    lane = np.arange(LANES)
    along[lane, lane] = -90.0
    for step, weight in ((1, 16.0), (2, -1.0)):
        for sign in (1, -1):
            np.add.at(along, ((lane + sign * step) % LANES, lane), weight)
    return jnp.asarray(across, bf16), jnp.asarray(along, bf16)


def around(block, axis, distance):
    count = lax.axis_size(axis)
    return lax.ppermute(block, axis, [(i, (i + distance) % count) for i in range(count)])


def swap(block, axis, mask):
    return lax.ppermute(block, axis, [(i, i ^ mask) for i in range(lax.axis_size(axis))])


def local(
    orbitals, occupations, potential_in, ionic_potential, hartree_prev, projectors, box_start, coupling
):
    count, planes, rows, lanes = orbitals.shape
    atoms, nproj, box, square = projectors.shape
    n_space = lax.axis_size("space")
    n_band = lax.axis_size("band")
    domain = lax.axis_index("space")
    core = lax.axis_index("band") % 2
    half = atoms // 2
    slots = atoms * SLOT
    params = functools.partial(pltpu.CompilerParams, vmem_limit_bytes=48 << 20)

    mine = around(lax.dynamic_slice_in_dim(projectors, core * half, half, 0), "space", 1)
    other = swap(mine, "band", 1)
    low = around(orbitals[:, planes - 2 :], "space", 1)
    high = around(orbitals[:, :2], "space", -1)

    behind = (domain + n_space - 1) % n_space
    own_starts = lax.dynamic_slice_in_dim(box_start, domain * atoms, atoms, 1)
    own_starts = jnp.stack([own_starts[0] % planes, own_starts[2]])
    prev_starts = lax.dynamic_slice_in_dim(box_start, behind * atoms, atoms, 1)
    prev_starts = jnp.stack([prev_starts[0] % planes, prev_starts[2]])
    core_scalar = core.reshape(1).astype(jnp.int32)
    padded = jnp.zeros((SLOT, SLOT), f32).at[:nproj, :nproj].set(coupling.T)
    coupling_wide = jnp.kron(jnp.eye(atoms, dtype=f32), padded)
    across, along = stencils(planes, rows)

    steps = 4
    partial = pl.pallas_call(
        density_kernel,
        grid=(steps,),
        in_specs=[
            smem(),
            pl.BlockSpec((count, planes // steps, rows, lanes), lambda i: (0, i, 0, 0)),
        ],
        out_specs=pl.BlockSpec((planes // steps, rows, lanes), lambda i: (i, 0, 0)),
        out_shape=jax.ShapeDtypeStruct((planes, rows, lanes), f32),
        compiler_params=params(),
        name="density",
    )(occupations, orbitals)

    scratch = [
        pltpu.VMEM((atoms, square // lanes, SLOT * box, lanes), f32),
        pltpu.VMEM((slots, rows * lanes), bf16),
    ]
    own_part = pl.pallas_call(
        functools.partial(coefficient_kernel, False),
        in_specs=[smem(), smem(), vmem(), vmem()],
        out_specs=vmem(),
        out_shape=jax.ShapeDtypeStruct((count, slots), f32),
        scratch_shapes=scratch + [pltpu.VMEM((count * rows, lanes), f32)],
        compiler_params=params(),
        name="own_coefficients",
    )(own_starts, core_scalar, orbitals, projectors)

    pair = partial + swap(partial, "band", 1)
    density = pair.astype(bf16)
    mask = 2
    while mask < n_band:
        density = density.astype(f32) + swap(density, "band", mask).astype(f32)
        mask *= 2
        if mask < n_band:
            density = density.astype(bf16)
    density = density.astype(f32)
    charge = jnp.full((8, lanes), jnp.sum(density), f32)
    mask = 1
    while mask < n_space:
        charge = charge + swap(charge, "space", mask)
        mask *= 2
    mean = charge[0, :1] / (planes * rows * lanes * n_space)

    def message(part, planes_h, planes_d):
        return jnp.concatenate(
            [part, planes_h.reshape(2 * rows, lanes), planes_d.reshape(rows, lanes)], axis=0
        )

    below = around(message(own_part, hartree_prev[planes - 2 :], density[planes - 1 :]), "space", 1)

    prev_part = pl.pallas_call(
        functools.partial(coefficient_kernel, True),
        in_specs=[smem(), smem(), vmem(), vmem(), vmem()],
        out_specs=vmem(),
        out_shape=jax.ShapeDtypeStruct((count, slots), f32),
        scratch_shapes=scratch + [pltpu.VMEM((count * rows, lanes), f32)],
        compiler_params=params(),
        name="carried_coefficients",
    )(prev_starts, core_scalar, orbitals, mine, other)

    above = around(message(prev_part, hartree_prev[:2], density[:1]), "space", -1)

    acc = pl.pallas_call(
        local_kernel,
        in_specs=[smem(), smem(), hbm(), hbm(), hbm()] + [vmem()] * 8,
        out_specs=vmem(),
        out_shape=jax.ShapeDtypeStruct((count, planes, rows, lanes), f32),
        scratch_shapes=scratch
        + [
            pltpu.VMEM((count * planes * rows, lanes), f32),
            pltpu.VMEM((count, planes + 4, rows, lanes), bf16),
            pltpu.SemaphoreType.DMA((3,)),
        ],
        compiler_params=params(),
        name="local_part",
    )(
        prev_starts, core_scalar, orbitals, low, high, mine, other, prev_part, below[:count],
        coupling_wide, along, across, potential_in,
    )

    applied, potential = pl.pallas_call(
        final_kernel,
        in_specs=[smem(), smem()] + [vmem()] * 10,
        out_specs=(vmem(), vmem()),
        out_shape=(
            jax.ShapeDtypeStruct((count, planes, rows, lanes), bf16),
            jax.ShapeDtypeStruct((planes, rows, lanes), f32),
        ),
        scratch_shapes=scratch + [pltpu.VMEM((count * planes * rows, lanes), f32)],
        compiler_params=params(),
        name="final_part",
    )(
        own_starts, mean, acc, projectors, own_part, above, coupling_wide,
        density, hartree_prev, ionic_potential, below, above,
    )
    return applied, potential


def solution(mesh):
    placed = (
        P("band", "space", None, None),
        P("band"),
        P("space", None, None),
        P("space", None, None),
        P("space", None, None),
        P("space", None, None, None),
        P(),
        P(),
    )
    return jax.shard_map(
        local,
        mesh=mesh,
        in_specs=placed,
        out_specs=(P("band", "space", None, None), P("space", None, None)),
        check_vma=False,
    )
```

time: 413 us -> 124 us (0.30)
  local copies, waits for them, and re-layouts: 143 us -> 11.4 us
  Pallas kernels: 0 us -> 81.9 us
  waiting for transfers between devices: 65.7 us -> 6.85 us
  blocking collectives: 47.4 us -> 0 us
  matrix products: 47.1 us -> 0 us
  other arithmetic: 45.4 us -> 5.06 us
  loops' own time: 31.3 us -> 0 us
  between operations: 15 us -> 1.49 us
    pallas_call x0 -> x5, Pallas kernels: none -> 81.9 us  [the longest x1 24.9 us: local(): pl.pallas_call(local_kernel, in_specs=[smem(), smem(), hbm(), hbm(), hbm(...]
    dynamic_slice x73 -> x2, local copies, waits for them, and re-layouts: 64 us -> 0.1 us  [the longest x1 0.07 us: local(): prev_starts = lax.dynamic_slice_in_dim(box_start, behind * atoms, atoms, 1)]
    ppermute x6 -> x11, waiting for transfers between devices: 65.7 us -> 6.85 us  [the longest x6 6.84 us: swap(): lax.ppermute(block, axis, [(i, i ^ mask) for i in range(lax.axis_size(axi...]
    psum x1 -> x0, blocking collectives: 47.4 us -> none  [local(): charge_total = lax.psum(jnp.sum(partial_density), ('band', 'space'))]
    dot_general x49 -> x0, matrix products: 47.1 us -> none  [the longest x8 18.8 us: add_atom(): jnp.einsum('piyz,po->oiyz', placed, weighted[atom_index], preferred_eleme...]
    another operation x2 -> x0, loops' own time: 31.3 us -> none  [the longest x1 15.7 us: deposit(): return lax.fori_loop(0, beta_block.shape[0], add_atom, buffer)]
    while x64 -> x0, local copies, waits for them, and re-layouts: 24.6 us -> none
    slice x19 -> x4, local copies, waits for them, and re-layouts: 27.2 us -> 2.75 us  [the longest x1 0.78 us: local(): high = around(orbitals[:, :2], 'space', -1)]
  transfers between devices with their start and end apart: 7 -> 11, of which waited for: 1 -> 3; matrix products, arithmetic and copies ran while one was open for 46% -> 8% of each run, Pallas kernels for 0% -> 49%
where the time goes in v1:
time: 124 us
  Pallas kernels  81.9 us (66%)
  starting transfers between devices  17.1 us (14%)
  local copies, waits for them, and re-layouts  11.4 us (9%)
  waiting for transfers between devices  6.85 us (6%)
  other arithmetic  5.06 us (4%)
  between operations  1.49 us (1%)
    pallas_call x1, Pallas kernels, local(): pl.pallas_call(local_kernel, in_specs=[smem(), smem(), hbm(), hbm(), hbm(...  24.9 us
    pallas_call x1, Pallas kernels, local(): pl.pallas_call(final_kernel, in_specs=[smem(), smem()] + [vmem()] * 10, o...  19.5 us
    pallas_call x1, Pallas kernels, local(): pl.pallas_call(functools.partial(coefficient_kernel, True), in_specs=[sme...  18.2 us
    pallas_call x1, Pallas kernels, local(): pl.pallas_call(functools.partial(coefficient_kernel, False), in_specs=[sm...  18.1 us
    ppermute x5, starting transfers between devices, around(): lax.ppermute(block, axis, [(i, (i + distance) % count) for i in range(cou...  9.1 us
    ppermute x6, starting transfers between devices, swap(): lax.ppermute(block, axis, [(i, i ^ mask) for i in range(lax.axis_size(axi...  8 us
    ppermute x6, waiting for transfers between devices, swap(): lax.ppermute(block, axis, [(i, i ^ mask) for i in range(lax.axis_size(axi...  6.84 us
    unnamed x25, local copies, waits for them, and re-layouts  6.67 us
  transfers between devices with their start and end apart: 11, of which 3 were waited for; matrix products, arithmetic and copies ran while one was open for 8% of the time, Pallas kernels for 49%

profile of v1, /device:TPU:0, one launch (start us, length us, event | category | flops | bytes accessed | tf_op | source)
XLA Modules:
  0.0 123.8 jit_solution(14603114834649197036)
XLA Ops:
  0.6 1.4 %copy-done = bf16[24,16,16,128]{3,2,1,0:T(8,128)(2,1)S(1)} copy-done((bf16[24,16,16,128]{3,2,1,0:T(8,128)(2,1)S(1)}, bf16[24,16,16,128]{3,2,1,0:T(8,128)(2,1)}, u32[]{:S(2)}) %copy-start) | copy-done | bytes 1572888
  2.7 1.2 density.1
  4.5 0.8 fusion.4
  5.2 5.6 %collective-permute-start.6 = (bf16[24,2,16,128]{3,2,1,0:T(8,128)(2,1)}, bf16[24,2,16,128]{3,2,1,0:T(8,128)(2,1)}, u32[]{:S(2)}, u32[]{:S(2)}) collective-permute-start(bf16[24,2,16,128]{3,2,1,0:T(8,128)(2,1)} %get-tuple-element.14), channel_id=1, source_target_pairs={{0,7},{1,0},{2,1},{3,2},{4,3},{5,4},{6,5},{7,6},{8,15},{9,8},{10,9... | collective-permute-start | bytes 589832 | tf_op jit(solution)/shard_map/ppermute | solution.py:257
  10.9 0.7 fusion.5
  11.9 18.1 %own_coefficients.1.part_ref = f32[24,128]{1,0:T(8,128)S(1)} custom-call(s32[2,8]{1,0:T(2,128)S(1)} %pad_add_fusion.starts, s32[1]{0:T(128)} %bitcast.1.core, bf16[24,16,16,128]{3,2,1,0:T(8,128)(2,1)S(1)} %copy-done.1, bf16[8,13,16,256]{3,2,1,0:T(8,128)(2,1)S(1)} %copy-done.3), custom_call_target="tpu_custom_call" | custom-call | tf_op jit(solution)/shard_map/own_coefficients/pallas_call | solution.py:310
  30.1 0.9 add_convert_fusion
  31.0 1.6 %collective-permute-start.1 = (bf16[16,16,128]{2,1,0:T(8,128)(2,1)S(1)}, bf16[16,16,128]{2,1,0:T(8,128)(2,1)S(1)}, u32[]{:S(2)}, u32[]{:S(2)}) collective-permute-start(bf16[16,16,128]{2,1,0:T(8,128)(2,1)S(1)} %add_convert_fusion), channel_id=1, source_target_pairs={{0,16},{8,24},{16,0},{24,8},{1,17},{9,25},{17,1},{25,9},{2,18},{10... | collective-permute-start | bytes 196616 | tf_op jit(solution)/shard_map/ppermute | solution.py:261
  32.6 2.8 %collective-permute-done.1 = bf16[16,16,128]{2,1,0:T(8,128)(2,1)S(1)} collective-permute-done((bf16[16,16,128]{2,1,0:T(8,128)(2,1)S(1)}, bf16[16,16,128]{2,1,0:T(8,128)(2,1)S(1)}, u32[]{:S(2)}, u32[]{:S(2)}) %collective-permute-start.1) | collective-permute-done | bytes 65568 | tf_op jit(solution)/shard_map/ppermute | solution.py:261
  37.2 3.1 %collective-permute-done.2 = f32[8,128]{1,0:T(8,128)S(1)} collective-permute-done((f32[8,128]{1,0:T(8,128)S(1)}, f32[8,128]{1,0:T(8,128)S(1)}, u32[]{:S(2)}, u32[]{:S(2)}) %collective-permute-start.2) | collective-permute-done | bytes 4128 | tf_op jit(solution)/shard_map/ppermute | solution.py:261
  40.9 1.5 %collective-permute-start.3 = (f32[8,128]{1,0:T(8,128)S(1)}, f32[8,128]{1,0:T(8,128)S(1)}, u32[]{:S(2)}, u32[]{:S(2)}) collective-permute-start(f32[8,128]{1,0:T(8,128)S(1)} %broadcast_add_fusion), channel_id=1, source_target_pairs={{0,2},{1,3},{2,0},{3,1},{4,6},{5,7},{6,4},{7,5},{8,10},{9,11},{10,... | collective-permute-start | bytes 12296 | tf_op jit(solution)/shard_map/ppermute | solution.py:261
  43.7 0.9 collective-permute-done.3
  45.3 3.9 %collective-permute-start.4 = (f32[8,128]{1,0:T(8,128)S(1)}, f32[8,128]{1,0:T(8,128)S(1)}, u32[]{:S(2)}, u32[]{:S(2)}) collective-permute-start(f32[8,128]{1,0:T(8,128)S(1)} %fusion.6), channel_id=1, source_target_pairs={{0,4},{1,5},{2,6},{3,7},{4,0},{5,1},{6,2},{7,3},{8,12},{9,13},{10,... | collective-permute-start | bytes 12296 | tf_op jit(solution)/shard_map/ppermute | solution.py:261
  49.1 18.2 %carried_coefficients.1.part_ref = f32[24,128]{1,0:T(8,128)S(1)} custom-call(s32[2,8]{1,0:T(2,128)S(1)} %pad_add_fusion.1.starts, s32[1]{0:T(128)} %bitcast.1.core, bf16[24,16,16,128]{3,2,1,0:T(8,128)(2,1)S(1)} %copy-done.1, bf16[4,13,16,256]{3,2,1,0:T(8,128)(2,1)S(1)} %collective-permute-done.7.rest_0_.mine_ref, ...), custom_call_target="tpu_custom_call" | custom-call | tf_op jit(solution)/shard_map/carried_coefficients/pallas_call | solution.py:343
  67.9 2.9 %collective-permute-start.10 = (f32[72,128]{1,0:T(8,128)}, f32[72,128]{1,0:T(8,128)S(1)}, u32[]{:S(2)}, u32[]{:S(2)}) collective-permute-start(f32[72,128]{1,0:T(8,128)} %pad_maximum_fusion.1), channel_id=1, source_target_pairs={{0,7},{1,0},{2,1},{3,2},{4,3},{5,4},{6,5},{7,6},{8,15},{9,8},{10,9... | collective-permute-start | bytes 110600 | tf_op jit(solution)/shard_map/ppermute | solution.py:257
  70.8 0.9 broadcast_multiply_fusion
  71.7 1.2 mul.42.coupling_ref
  74.1 0.7 slice.69.far_ref
  74.9 1.0 copy-done.5
  75.8 0.9 copy-done.6
  76.7 0.8 copy-done.8
  77.5 24.9 %local_part.1.acc_ref = f32[24,16,16,128]{3,2,1,0:T(8,128)} custom-call(s32[2,8]{1,0:T(2,128)S(1)} %pad_add_fusion.1.starts, s32[1]{0:T(128)} %bitcast.1.core, bf16[24,16,16,128]{3,2,1,0:T(8,128)(2,1)S(1)} %copy-done.1, bf16[24,2,16,128]{3,2,1,0:T(8,128)(2,1)} %collective-permute-done.5.low_ref, bf16[24,2,16,128]{3,2,1,0:T(8,128)(2,1)} %collective-permute-done.6.high_ref, ...), custom_call_target="tpu_custom_call" | custom-call | tf_op jit(solution)/shard_map/local_part/pallas_call | solution.py:355
  102.4 1.9 %copy-done.2 = f32[24,16,16,128]{3,2,1,0:T(8,128)S(1)} copy-done((f32[24,16,16,128]{3,2,1,0:T(8,128)S(1)}, f32[24,16,16,128]{3,2,1,0:T(8,128)}, u32[]{:S(2)}) %copy-start.2) | copy-done | bytes 3145752
  104.3 19.5 %final_part.1 = (bf16[24,16,16,128]{3,2,1,0:T(8,128)(2,1)}, f32[16,16,128]{2,1,0:T(8,128)}) custom-call(s32[2,8]{1,0:T(2,128)S(1)} %pad_add_fusion.starts, f32[1]{0:T(128)} %bitcast.charge, f32[24,16,16,128]{3,2,1,0:T(8,128)S(1)} %copy-done.2, bf16[8,13,16,256]{3,2,1,0:T(8,128)(2,1)S(1)} %copy-done.3, f32[24,128]{1,0:T(8,128)S(1)} %own_coefficients.1.part_ref, ...), custom_call_target="tpu_custom_call" | custom-call | tf_op jit(solution)/shard_map/final_part/pallas_call | solution.py:373
  (50 shorter events, 7.1 us)
Async XLA Ops:
  0.6 1.4 %copy-start = (bf16[24,16,16,128]{3,2,1,0:T(8,128)(2,1)S(1)}, bf16[24,16,16,128]{3,2,1,0:T(8,128)(2,1)}, u32[]{:S(2)}) copy-start(bf16[24,16,16,128]{3,2,1,0:T(8,128)(2,1)} %field_ref.7) | copy-start | bytes 4718596
  2.0 0.7 copy-start.9
  2.7 8.1 %copy-start.3 = (bf16[8,13,16,256]{3,2,1,0:T(8,128)(2,1)S(1)}, bf16[8,13,16,256]{3,2,1,0:T(8,128)(2,1)}, u32[]{:S(2)}) copy-start(bf16[8,13,16,256]{3,2,1,0:T(8,128)(2,1)} %proj_ref.1) | copy-start | bytes 2555908
  2.7 9.0 %copy-start.11 = (s32[3,64]{1,0:T(4,128)S(1)}, s32[3,64]{1,0:T(4,128)}, u32[]{:S(2)}) copy-start(s32[3,64]{1,0:T(4,128)} %param.18) | copy-start | bytes 2308
  2.7 9.1 %copy-start.10 = (f32[13,13]{1,0:T(8,128)S(1)}, f32[13,13]{1,0:T(8,128)}, u32[]{:S(2)}) copy-start(f32[13,13]{1,0:T(8,128)} %param.19) | copy-start | bytes 2032
  2.7 9.2 %copy-start.1 = (bf16[24,16,16,128]{3,2,1,0:T(8,128)(2,1)S(1)}, bf16[24,16,16,128]{3,2,1,0:T(8,128)(2,1)}, u32[]{:S(2)}) copy-start(bf16[24,16,16,128]{3,2,1,0:T(8,128)(2,1)} %field_ref.7) | copy-start | bytes 4718596
  3.9 26.2 %collective-permute-start = (f32[16,16,128]{2,1,0:T(8,128)S(1)}, f32[16,16,128]{2,1,0:T(8,128)}, u32[]{:S(2)}, u32[]{:S(2)}) collective-permute-start(f32[16,16,128]{2,1,0:T(8,128)S(1)} %density.1), channel_id=1, source_target_pairs={{0,8},{8,0},{16,24},{24,16},{1,9},{9,1},{17,25},{25,17},{2,10},{10... | collective-permute-start | bytes 393224 | tf_op jit(solution)/shard_map/ppermute | solution.py:261
  5.2 69.6 %collective-permute-start.6 = (bf16[24,2,16,128]{3,2,1,0:T(8,128)(2,1)}, bf16[24,2,16,128]{3,2,1,0:T(8,128)(2,1)}, u32[]{:S(2)}, u32[]{:S(2)}) collective-permute-start(bf16[24,2,16,128]{3,2,1,0:T(8,128)(2,1)} %get-tuple-element.14), channel_id=1, source_target_pairs={{0,7},{1,0},{2,1},{3,2},{4,3},{5,4},{6,5},{7,6},{8,15},{9,8},{10,9... | collective-permute-start | bytes 589832 | tf_op jit(solution)/shard_map/ppermute | solution.py:257
  10.8 64.0 %collective-permute-start.5 = (bf16[24,2,16,128]{3,2,1,0:T(8,128)(2,1)}, bf16[24,2,16,128]{3,2,1,0:T(8,128)(2,1)}, u32[]{:S(2)}, u32[]{:S(2)}) collective-permute-start(bf16[24,2,16,128]{3,2,1,0:T(8,128)(2,1)} %get-tuple-element.15), channel_id=1, source_target_pairs={{0,1},{1,2},{2,3},{3,4},{4,5},{5,6},{6,7},{7,0},{8,9},{9,10},{10,1... | collective-permute-start | bytes 589832 | tf_op jit(solution)/shard_map/ppermute | solution.py:257
  10.8 26.3 %collective-permute-start.7 = (bf16[4,13,16,256]{3,2,1,0:T(8,128)(2,1)S(1)}, bf16[4,13,16,256]{3,2,1,0:T(8,128)(2,1)S(1)}, u32[]{:S(2)}, u32[]{:S(2)}) collective-permute-start(bf16[4,13,16,256]{3,2,1,0:T(8,128)(2,1)S(1)} %constant_dynamic-slice_fusion), channel_id=1, source_target_pairs={{0,1},{1,2},{2,3},{3,4},{4,5},{5,6},{6,7},{7,0},{8,9},{9,10},{10,1... | collective-permute-start | bytes 1277960 | tf_op jit(solution)/shard_map/ppermute | solution.py:257
  31.0 4.3 %collective-permute-start.1 = (bf16[16,16,128]{2,1,0:T(8,128)(2,1)S(1)}, bf16[16,16,128]{2,1,0:T(8,128)(2,1)S(1)}, u32[]{:S(2)}, u32[]{:S(2)}) collective-permute-start(bf16[16,16,128]{2,1,0:T(8,128)(2,1)S(1)} %add_convert_fusion), channel_id=1, source_target_pairs={{0,16},{8,24},{16,0},{24,8},{1,17},{9,25},{17,1},{25,9},{2,18},{10... | collective-permute-start | bytes 196616 | tf_op jit(solution)/shard_map/ppermute | solution.py:261
  36.6 3.7 %collective-permute-start.2 = (f32[8,128]{1,0:T(8,128)S(1)}, f32[8,128]{1,0:T(8,128)S(1)}, u32[]{:S(2)}, u32[]{:S(2)}) collective-permute-start(f32[8,128]{1,0:T(8,128)S(1)} %broadcast_in_dim.8), channel_id=1, source_target_pairs={{0,1},{1,0},{2,3},{3,2},{4,5},{5,4},{6,7},{7,6},{8,9},{9,8},{10,11... | collective-permute-start | bytes 12296 | tf_op jit(solution)/shard_map/ppermute | solution.py:261
  37.2 12.0 %collective-permute-start.8 = (bf16[4,13,16,256]{3,2,1,0:T(8,128)(2,1)S(1)}, bf16[4,13,16,256]{3,2,1,0:T(8,128)(2,1)S(1)}, u32[]{:S(2)}, u32[]{:S(2)}) collective-permute-start(bf16[4,13,16,256]{3,2,1,0:T(8,128)(2,1)S(1)} %collective-permute-done.7.rest_0_.mine_ref), channel_id=1, source_target_pairs={{0,8},{8,0},{16,24},{24,16},{1,9},{9,1},{17,25},{25,17},{2,10},{10... | collective-permute-start | bytes 1277960 | tf_op jit(solution)/shard_map/ppermute | solution.py:261
  40.9 3.7 %collective-permute-start.3 = (f32[8,128]{1,0:T(8,128)S(1)}, f32[8,128]{1,0:T(8,128)S(1)}, u32[]{:S(2)}, u32[]{:S(2)}) collective-permute-start(f32[8,128]{1,0:T(8,128)S(1)} %broadcast_add_fusion), channel_id=1, source_target_pairs={{0,2},{1,3},{2,0},{3,1},{4,6},{5,7},{6,4},{7,5},{8,10},{9,11},{10,... | collective-permute-start | bytes 12296 | tf_op jit(solution)/shard_map/ppermute | solution.py:261
  43.1 31.1 %collective-permute-start.9 = (f32[72,128]{1,0:T(8,128)}, f32[72,128]{1,0:T(8,128)}, u32[]{:S(2)}, u32[]{:S(2)}) collective-permute-start(f32[72,128]{1,0:T(8,128)} %pad_maximum_fusion), channel_id=1, source_target_pairs={{0,1},{1,2},{2,3},{3,4},{4,5},{5,6},{6,7},{7,0},{8,9},{9,10},{10,1... | collective-permute-start | bytes 110600 | tf_op jit(solution)/shard_map/ppermute | solution.py:257
  45.3 27.7 %collective-permute-start.4 = (f32[8,128]{1,0:T(8,128)S(1)}, f32[8,128]{1,0:T(8,128)S(1)}, u32[]{:S(2)}, u32[]{:S(2)}) collective-permute-start(f32[8,128]{1,0:T(8,128)S(1)} %fusion.6), channel_id=1, source_target_pairs={{0,4},{1,5},{2,6},{3,7},{4,0},{5,1},{6,2},{7,3},{8,12},{9,13},{10,... | collective-permute-start | bytes 12296 | tf_op jit(solution)/shard_map/ppermute | solution.py:261
  67.9 34.4 %collective-permute-start.10 = (f32[72,128]{1,0:T(8,128)}, f32[72,128]{1,0:T(8,128)S(1)}, u32[]{:S(2)}, u32[]{:S(2)}) collective-permute-start(f32[72,128]{1,0:T(8,128)} %pad_maximum_fusion.1), channel_id=1, source_target_pairs={{0,7},{1,0},{2,1},{3,2},{4,3},{5,4},{6,5},{7,6},{8,15},{9,8},{10,9... | collective-permute-start | bytes 110600 | tf_op jit(solution)/shard_map/ppermute | solution.py:257
  74.8 27.6 %copy-start.4 = (f32[16,16,128]{2,1,0:T(8,128)S(1)}, f32[16,16,128]{2,1,0:T(8,128)}, u32[]{:S(2)}) copy-start(f32[16,16,128]{2,1,0:T(8,128)} %hart_ref.1) | copy-start | bytes 393220
  74.8 1.0 copy-start.5
  75.8 0.9 copy-start.6
  76.7 0.8 copy-start.8
  77.5 24.9 %copy-start.7 = (f32[16,16,128]{2,1,0:T(8,128)S(1)}, f32[16,16,128]{2,1,0:T(8,128)}, u32[]{:S(2)}) copy-start(f32[16,16,128]{2,1,0:T(8,128)} %ionic_ref.1) | copy-start | bytes 393220
  102.4 1.9 %copy-start.2 = (f32[24,16,16,128]{3,2,1,0:T(8,128)S(1)}, f32[24,16,16,128]{3,2,1,0:T(8,128)}, u32[]{:S(2)}) copy-start(f32[24,16,16,128]{3,2,1,0:T(8,128)} %local_part.1.acc_ref) | copy-start | bytes 9437188

commit v2 on v1

v2 whole, which is shorter than its diff:
```python
import functools
import math

import jax
import jax.numpy as jnp
from jax import lax
from jax.experimental import pallas as pl
from jax.experimental.pallas import tpu as pltpu
from jax.sharding import PartitionSpec as P

SWEEPS = 2
LANES = 128
SLOT = 16
LIMIT = 24

screening = 0.25
four_pi = 4.0 * math.pi
f32 = jnp.float32
bf16 = jnp.bfloat16


def vmem():
    return pl.BlockSpec(memory_space=pltpu.VMEM)


def smem():
    return pl.BlockSpec(memory_space=pltpu.SMEM)


def hbm():
    return pl.BlockSpec(memory_space=pl.ANY)


NT = (((1,), (1,)), ((), ()))


def prepare_kernel(occ, field_ref, density_ref, turned_ref, first_ref, last_ref, wide_ref):
    step = pl.program_id(0)
    count, planes, rows, _ = field_ref.shape
    stride = rows + 1

    @pl.when(step == 0)
    def _():
        first_ref[...] = field_ref[:, :2]

    @pl.when(step == pl.num_programs(0) - 1)
    def _():
        last_ref[...] = field_ref[:, planes - 2 :]

    for i in range(planes):
        total = jnp.zeros((rows, LANES), f32)
        for o in range(count):
            cells = field_ref[o, i].astype(f32)
            total = total + (occ[o] * cells) * cells
            wide_ref[i, o * stride : o * stride + rows, :] = cells
        density_ref[i] = total
        turned_ref[i] = jnp.concatenate(
            [
                pltpu.roll(
                    wide_ref[i, pl.ds(r, count, stride=stride), :], (SLOT * r) % LANES, 1
                )
                for r in range(rows)
            ],
            axis=1,
        ).astype(bf16)


def shift_projectors(raw_ref, index, atom, column, rows_ref, shifted_ref):
    nproj, box, square = raw_ref.shape[1:]
    stride = box + 1
    tiles = square // LANES
    for p in range(SLOT):
        if p < nproj:
            cells = raw_ref[index, p].astype(f32)
        else:
            cells = jnp.zeros((box, square), f32)
        for t in range(tiles):
            rows_ref[t, p * stride : p * stride + box, :] = cells[:, t * LANES : (t + 1) * LANES]
    for j in range(box):
        for t in range(tiles):
            cells = rows_ref[t, pl.ds(j, SLOT, stride=stride), :].astype(bf16)
            k = j * tiles + t
            shifted_ref[atom, :, k * LANES : (k + 1) * LANES] = pltpu.roll(cells, column, 1)


def lane_group(column, height):
    lane = lax.broadcasted_iota(jnp.int32, (height, LANES), 1)
    return lax.shift_right_logical(jnp.bitwise_and(lane - column + LANES, LANES - 1), 4)


def gather_atom(turned_ref, shifted_ref, atom, offset, column, lift, boxed_ref):
    planes, count, _ = turned_ref.shape
    box = SLOT
    tiles = shifted_ref.shape[2] // (box * LANES)
    per_tile = LANES // box
    group = lane_group(column, count)
    masks = [group == r for r in range(per_tile)]
    for j in range(box):
        plane = offset + j - lift
        valid = jnp.logical_and(plane >= 0, plane < planes)
        plane = jnp.clip(plane, 0, planes - 1)
        for t in range(tiles):
            base = t * per_tile * LANES
            cells = turned_ref[plane, :, base : base + LANES]
            for r in range(1, per_tile):
                low = base + r * LANES
                cells = jnp.where(masks[r], turned_ref[plane, :, low : low + LANES], cells)
            k = j * tiles + t
            boxed_ref[:, k * LANES : (k + 1) * LANES] = jnp.where(valid, cells, jnp.zeros_like(cells))
    return lax.dot_general(boxed_ref[...], shifted_ref[atom], NT, preferred_element_type=f32)


def own_kernel(
    starts, turned_ref, proj_ref, coupling_ref,
    part_ref, shifted_ref, wide_coupling_ref, rows_ref, boxed_ref,
):
    atoms, nproj = proj_ref.shape[:2]
    for a in range(atoms):
        shift_projectors(proj_ref, a, a, starts[1, a], rows_ref.at[a % 2], shifted_ref)
    for a in range(atoms):
        part_ref[:, a * SLOT : (a + 1) * SLOT] = gather_atom(
            turned_ref, shifted_ref, a, starts[0, a], starts[1, a], 0, boxed_ref.at[a % 2]
        )
    slots = atoms * SLOT
    spread = (
        lax.broadcasted_iota(jnp.int32, (nproj, slots), 0)
        == lax.broadcasted_iota(jnp.int32, (nproj, slots), 1) % SLOT
    ).astype(f32)
    exact = dict(precision=lax.Precision.HIGHEST, preferred_element_type=f32)
    right = lax.dot_general(coupling_ref[...], spread, (((0,), (0,)), ((), ())), **exact)
    both = lax.dot_general(spread, right, (((0,), (0,)), ((), ())), **exact)
    same = (
        lax.broadcasted_iota(jnp.int32, (slots, slots), 0) // SLOT
        == lax.broadcasted_iota(jnp.int32, (slots, slots), 1) // SLOT
    )
    wide_coupling_ref[...] = jnp.where(same, both, 0.0)


def carried_kernel(
    starts, core, turned_ref, mine_ref, other_ref, hart_ref, dens_ref,
    message_ref, shifted_ref, rows_ref, boxed_ref,
):
    half = mine_ref.shape[0]
    count = turned_ref.shape[1]
    rows = hart_ref.shape[1]
    for q in range(half):
        a = core[0] * half + q
        shift_projectors(mine_ref, q, a, starts[1, a], rows_ref.at[0], shifted_ref)
        a = (1 - core[0]) * half + q
        shift_projectors(other_ref, q, a, starts[1, a], rows_ref.at[1], shifted_ref)
    for a in range(2 * half):
        message_ref[:count, a * SLOT : (a + 1) * SLOT] = gather_atom(
            turned_ref, shifted_ref, a, starts[0, a], starts[1, a],
            turned_ref.shape[0], boxed_ref.at[a % 2],
        )
    message_ref[count : count + 2 * rows] = hart_ref[:2].reshape(2 * rows, LANES)
    message_ref[count + 2 * rows :] = dens_ref[0]


def weigh(coef, coupling_ref):
    return lax.dot_general(
        coef, coupling_ref[...], (((1,), (0,)), ((), ())),
        precision=lax.Precision.HIGHEST, preferred_element_type=f32,
    ).astype(bf16)


def deposit_plane(starts, shifted_ref, weighted, plane, lift, placed_ref, wide_ref):
    atoms = shifted_ref.shape[0]
    count = weighted.shape[0]
    box = SLOT
    tiles = shifted_ref.shape[2] // (box * LANES)
    per_tile = LANES // box
    for a in range(atoms):
        group = lane_group(starts[1, a], SLOT)
        j = plane - starts[0, a] + lift
        valid = jnp.logical_and(j >= 0, j < box)
        group = jnp.where(valid, group, -1)
        j = jnp.clip(j, 0, box - 1)
        for t in range(tiles):
            low = pl.multiple_of((j * tiles + t) * LANES, LANES)
            cells = shifted_ref[a, :, pl.ds(low, LANES)]
            for r in range(per_tile):
                row = t * per_tile + r
                placed_ref[a * SLOT : (a + 1) * SLOT, row * LANES : (row + 1) * LANES] = jnp.where(
                    group == r, cells, jnp.zeros_like(cells)
                )
    update = jnp.dot(weighted, placed_ref[...], preferred_element_type=f32)
    rows = tiles * per_tile
    for r in range(rows):
        wide_ref[pl.ds(r, count, stride=rows + 1), :] = pltpu.roll(
            update[:, r * LANES : (r + 1) * LANES], (-SLOT * r) % LANES, 1
        )


def local_kernel(
    starts, field_ref, low_ref, high_ref, shifted_ref, message_ref, below_ref,
    coupling_ref, pot_ref, acc_ref, placed_ref, wide_ref,
):
    count, planes, rows, _ = field_ref.shape
    weighted = weigh(message_ref[:count] + below_ref[:count], coupling_ref)

    def one(o, _):
        cells = (
            [low_ref[o, i].astype(f32) for i in range(2)]
            + [field_ref[o, i].astype(f32) for i in range(planes)]
            + [high_ref[o, i].astype(f32) for i in range(2)]
        )
        for i in range(planes):
            c = cells[i + 2]
            near = cells[i + 1] + cells[i + 3]
            near = near + pltpu.roll(c, 1, 0) + pltpu.roll(c, rows - 1, 0)
            near = near + pltpu.roll(c, 1, 1) + pltpu.roll(c, LANES - 1, 1)
            far = cells[i] + cells[i + 4]
            far = far + pltpu.roll(c, 2, 0) + pltpu.roll(c, rows - 2, 0)
            far = far + pltpu.roll(c, 2, 1) + pltpu.roll(c, LANES - 2, 1)
            acc_ref[o, i] = (
                (pot_ref[i] + 3.75) * c - (2.0 / 3.0) * near + (1.0 / 24.0) * far
            )
        return 0

    lax.fori_loop(0, count, one, 0)

    def two(plane, _):
        deposit_plane(starts, shifted_ref, weighted, plane, planes, placed_ref, wide_ref)
        for o in range(count):
            low = o * (rows + 1)
            acc_ref[o, plane] += wide_ref[low : low + rows, :]
        return 0

    lax.fori_loop(0, planes, two, 0)


def final_kernel(
    starts, acc_ref, shifted_ref, part_ref, above_ref, coupling_ref,
    dens_ref, hart_ref, ionic_ref, below_ref, charge_ref,
    out_ref, pot_ref, placed_ref, wide_ref, done_ref, sems, *, cells_total,
):
    count, planes, rows, _ = done_ref.shape
    weighted = weigh(part_ref[...] + above_ref[:count], coupling_ref)
    groups = sems.shape[0]
    size = planes // groups
    copies = []
    for group in range(groups):
        def two(i, _):
            plane = group * size + i
            deposit_plane(starts, shifted_ref, weighted, plane, 0, placed_ref, wide_ref)
            for o in range(count):
                low = o * (rows + 1)
                done_ref[o, plane] = (acc_ref[o, plane] + wide_ref[low : low + rows, :]).astype(bf16)
            return 0

        lax.fori_loop(0, size, two, 0)
        part = pl.ds(group * size, size)
        copies.append(
            pltpu.make_async_copy(done_ref.at[:, part], out_ref.at[:, part], sems.at[group])
        )
        copies[-1].start()

    field = jnp.concatenate(
        [
            below_ref[count : count + 2 * rows].reshape(2, rows, LANES),
            hart_ref[...],
            above_ref[count : count + 2 * rows].reshape(2, rows, LANES),
        ],
        axis=0,
    )
    dens = jnp.concatenate(
        [
            below_ref[count + 2 * rows :].reshape(1, rows, LANES),
            dens_ref[...],
            above_ref[count + 2 * rows :].reshape(1, rows, LANES),
        ],
        axis=0,
    )
    source = four_pi * dens
    scale = 1.0 / (6.0 + screening)

    def relax(h, s):
        inner = h[1:-1]
        size = inner.shape
        flat = inner.reshape(size[0] * rows, LANES)
        across = pltpu.roll(flat, 1, 1) + pltpu.roll(flat, LANES - 1, 1)
        total = h[2:] + h[:-2] + across.reshape(size)
        total = total + pltpu.roll(inner, 1, 1) + pltpu.roll(inner, rows - 1, 1)
        return (total + s) * scale

    once = relax(field, source)
    twice = relax(once, source[1:-1])
    shift = charge_ref[0:1, 0:1] * (four_pi * scale * (1.0 + 6.0 * scale) / cells_total)
    third = (3.0 / math.pi) * dens_ref[...]
    root = jnp.exp(jnp.log(jnp.maximum(third, 1e-37)) * (1.0 / 3.0))
    root = (2.0 * root + third / jnp.maximum(root * root, 1e-30)) * (1.0 / 3.0)
    root = jnp.where(third > 0.0, root, 0.0)
    pot_ref[...] = ionic_ref[...] + twice - shift[None] - root
    for copy in copies:
        copy.wait()


def around(block, axis, distance):
    count = lax.axis_size(axis)
    return lax.ppermute(block, axis, [(i, (i + distance) % count) for i in range(count)])


def swap(block, axis, mask):
    return lax.ppermute(block, axis, [(i, i ^ mask) for i in range(lax.axis_size(axis))])


def local(
    orbitals, occupations, potential_in, ionic_potential, hartree_prev, projectors, box_start, coupling
):
    count, planes, rows, lanes = orbitals.shape
    atoms, nproj, box, square = projectors.shape
    n_space = lax.axis_size("space")
    n_band = lax.axis_size("band")
    domain = lax.axis_index("space")
    core = lax.axis_index("band") % 2
    half = atoms // 2
    slots = atoms * SLOT
    cells = planes * rows * lanes
    params = pltpu.CompilerParams(vmem_limit_bytes=LIMIT << 20)

    def call(kernel, name, work, **kwargs):
        cost = pl.CostEstimate(flops=work * 500000, bytes_accessed=work * 1000000, transcendentals=0)
        return pl.pallas_call(kernel, name=name, compiler_params=params, cost_estimate=cost, **kwargs)

    mine = around(lax.dynamic_slice_in_dim(projectors, core * half, half, 0), "space", 1)
    other = swap(mine, "band", 1)

    behind = (domain + n_space - 1) % n_space
    own_starts = lax.dynamic_slice_in_dim(box_start, domain * atoms, atoms, 1)
    own_starts = jnp.stack([own_starts[0] % planes, own_starts[2]])
    prev_starts = lax.dynamic_slice_in_dim(box_start, behind * atoms, atoms, 1)
    prev_starts = jnp.stack([prev_starts[0] % planes, prev_starts[2]])
    core_scalar = core.reshape(1).astype(jnp.int32)

    steps = 4
    step = planes // steps
    stride = rows + 1
    partial, turned, first, last = call(
        prepare_kernel, "prepare", 2,
        grid=(steps,),
        in_specs=[smem(), pl.BlockSpec((count, step, rows, lanes), lambda i: (0, i, 0, 0))],
        out_specs=(
            pl.BlockSpec((step, rows, lanes), lambda i: (i, 0, 0)),
            pl.BlockSpec((step, count, rows * lanes), lambda i: (i, 0, 0)),
            pl.BlockSpec((count, 2, rows, lanes), lambda i: (0, 0, 0, 0)),
            pl.BlockSpec((count, 2, rows, lanes), lambda i: (0, 0, 0, 0)),
        ),
        out_shape=(
            jax.ShapeDtypeStruct((planes, rows, lanes), f32),
            jax.ShapeDtypeStruct((planes, count, rows * lanes), bf16),
            jax.ShapeDtypeStruct((count, 2, rows, lanes), bf16),
            jax.ShapeDtypeStruct((count, 2, rows, lanes), bf16),
        ),
        scratch_shapes=[pltpu.VMEM((step, count * stride, lanes), f32)],
    )(occupations, orbitals)
    low = around(last, "space", 1)
    high = around(first, "space", -1)

    shifted_shape = jax.ShapeDtypeStruct((atoms, SLOT, box * square), bf16)
    gather_scratch = [
        pltpu.VMEM((2, square // lanes, SLOT * (box + 1), lanes), f32),
        pltpu.VMEM((2, count, box * square), bf16),
    ]
    own_part, own_shifted, wide_coupling = call(
        own_kernel, "own_part", 4,
        in_specs=[smem()] + [vmem()] * 3,
        out_specs=(vmem(), vmem(), vmem()),
        out_shape=(
            jax.ShapeDtypeStruct((count, slots), f32),
            shifted_shape,
            jax.ShapeDtypeStruct((slots, slots), f32),
        ),
        scratch_shapes=gather_scratch,
    )(own_starts, turned, projectors, coupling)

    pair = partial + swap(partial, "band", 1)
    density = pair.astype(bf16)
    mask = 2
    while mask < n_band:
        density = density.astype(f32) + swap(density, "band", mask).astype(f32)
        mask *= 2
        if mask < n_band:
            density = density.astype(bf16)
    density = density.astype(f32)
    charge = jnp.full((8, lanes), jnp.sum(density), f32)
    mask = 1
    while mask < n_space:
        charge = charge + swap(charge, "space", mask)
        mask *= 2

    below = around(
        jnp.concatenate(
            [
                own_part,
                hartree_prev[planes - 2 :].reshape(2 * rows, lanes),
                density[planes - 1],
            ],
            axis=0,
        ),
        "space",
        1,
    )

    message, prev_shifted = call(
        carried_kernel, "carried_part", 4,
        in_specs=[smem(), smem()] + [vmem()] * 5,
        out_specs=(vmem(), vmem()),
        out_shape=(jax.ShapeDtypeStruct((count + 3 * rows, slots), f32), shifted_shape),
        scratch_shapes=gather_scratch,
    )(prev_starts, core_scalar, turned, mine, other, hartree_prev, density)

    above = around(message, "space", -1)

    deposit_scratch = [
        pltpu.VMEM((slots, rows * lanes), bf16),
        pltpu.VMEM((count * stride, lanes), f32),
    ]
    acc = call(
        local_kernel, "local_part", 6,
        in_specs=[smem()] + [vmem()] * 8,
        out_specs=vmem(),
        out_shape=jax.ShapeDtypeStruct((count, planes, rows, lanes), f32),
        scratch_shapes=deposit_scratch,
    )(
        prev_starts, orbitals, low, high, prev_shifted, message, below, wide_coupling, potential_in
    )

    applied, potential = call(
        functools.partial(final_kernel, cells_total=float(cells * n_space)), "final_part", 4,
        in_specs=[smem()] + [vmem()] * 10,
        out_specs=(hbm(), vmem()),
        out_shape=(
            jax.ShapeDtypeStruct((count, planes, rows, lanes), bf16),
            jax.ShapeDtypeStruct((planes, rows, lanes), f32),
        ),
        scratch_shapes=deposit_scratch
        + [
            pltpu.VMEM((count, planes, rows, lanes), bf16),
            pltpu.SemaphoreType.DMA((4,)),
        ],
    )(
        own_starts, acc, own_shifted, own_part, above, wide_coupling,
        density, hartree_prev, ionic_potential, below, charge,
    )
    return applied, potential


def solution(mesh):
    placed = (
        P("band", "space", None, None),
        P("band"),
        P("space", None, None),
        P("space", None, None),
        P("space", None, None),
        P("space", None, None, None),
        P(),
        P(),
    )
    return jax.shard_map(
        local,
        mesh=mesh,
        in_specs=placed,
        out_specs=(P("band", "space", None, None), P("space", None, None)),
        check_vma=False,
    )
```

time: 124 us -> 59.6 us (0.48)
  Pallas kernels: 81.9 us -> 26.7 us
  local copies, waits for them, and re-layouts: 11.4 us -> 4.68 us
  waiting for transfers between devices: 6.85 us -> 10.3 us
  other arithmetic: 5.06 us -> 1.99 us
  starting transfers between devices: 17.1 us -> 14.9 us
    pallas_call x5, Pallas kernels: 81.9 us -> 26.7 us  [the longest x1 10 us: local(): call(local_kernel, 'local_part', 6, in_specs=[smem()] + [vmem()] * 8, out...]
    ppermute x6, starting transfers between devices: 8 us -> 2.32 us  [swap(): lax.ppermute(block, axis, [(i, i ^ mask) for i in range(lax.axis_size(axi...]
    unnamed x25 -> x18, local copies, waits for them, and re-layouts: 6.67 us -> 2.1 us
    ppermute x6, waiting for transfers between devices: 6.84 us -> 10.3 us  [swap(): lax.ppermute(block, axis, [(i, i ^ mask) for i in range(lax.axis_size(axi...]
    ppermute x5, starting transfers between devices: 9.1 us -> 12.5 us  [around(): lax.ppermute(block, axis, [(i, (i + distance) % count) for i in range(cou...]
    slice x4 -> x2, local copies, waits for them, and re-layouts: 2.75 us -> 0.01 us  [local(): hartree_prev[planes - 2:].reshape(2 * rows, lanes)]
    dynamic_slice x1, local copies, waits for them, and re-layouts: 0.03 us -> 1.86 us  [local(): lax.dynamic_slice_in_dim(projectors, core * half, half, 0)]
    concatenate x2 -> x1, other arithmetic: 1.26 us -> 0.01 us  [local(): jnp.concatenate([own_part, hartree_prev[planes - 2:].reshape(2 * rows, la...]
  transfers between devices with their start and end apart: 11 -> 11, of which waited for: 3 -> 3; matrix products, arithmetic and copies ran while one was open for 8% -> 5% of each run, Pallas kernels for 49% -> 31%
where the time goes in v2:
time: 59.6 us; the launch traced here: 59.4 us
  Pallas kernels  26.7 us (45%)
  starting transfers between devices  14.9 us (25%)
  waiting for transfers between devices  10.3 us (17%)
  local copies, waits for them, and re-layouts  4.68 us (8%)
  other arithmetic  1.99 us (3%)
  between operations  0.89 us (1%)
    ppermute x5, starting transfers between devices, around(): lax.ppermute(block, axis, [(i, (i + distance) % count) for i in range(cou...  12.5 us
    ppermute x6, waiting for transfers between devices, swap(): lax.ppermute(block, axis, [(i, i ^ mask) for i in range(lax.axis_size(axi...  10.3 us
    pallas_call x1, Pallas kernels, local(): call(local_kernel, 'local_part', 6, in_specs=[smem()] + [vmem()] * 8, out...  10 us
    pallas_call x1, Pallas kernels, local(): call(functools.partial(final_kernel, cells_total=float(cells * n_space)),...  8.39 us
    pallas_call x1, Pallas kernels, local(): call(carried_kernel, 'carried_part', 4, in_specs=[smem(), smem()] + [vmem...  2.98 us
    pallas_call x1, Pallas kernels, local(): call(own_kernel, 'own_part', 4, in_specs=[smem()] + [vmem()] * 3, out_spe...  2.94 us
    pallas_call x1, Pallas kernels, local(): call(prepare_kernel, 'prepare', 2, grid=(steps,), in_specs=[smem(), pl.Bl...  2.33 us
    ppermute x6, starting transfers between devices, swap(): lax.ppermute(block, axis, [(i, i ^ mask) for i in range(lax.axis_size(axi...  2.32 us
  transfers between devices with their start and end apart: 11, of which 3 were waited for; matrix products, arithmetic and copies ran while one was open for 5% of the time, Pallas kernels for 31%

profile of v2, /device:TPU:0, one launch (start us, length us, event | category | flops | bytes accessed | tf_op | source)
XLA Modules:
  0.0 59.4 jit_solution(9225411564207364008)
XLA Ops:
  0.7 1.9 %constant_dynamic-slice_fusion = bf16[4,13,16,256]{3,2,1,0:T(8,128)(2,1)} fusion(bf16[8,13,16,256]{3,2,1,0:T(8,128)(2,1)} %proj_ref.1, s32[]{:T(128)S(6)} %select_n.38), kind=kLoop, calls=%fused_computation.13 | loop fusion | bytes 851972 | tf_op jit(solution)/shard_map/dynamic_slice | solution.py:326
  2.5 3.0 %collective-permute-start.2 = (bf16[4,13,16,256]{3,2,1,0:T(8,128)(2,1)}, bf16[4,13,16,256]{3,2,1,0:T(8,128)(2,1)S(1)}, u32[]{:S(2)}, u32[]{:S(2)}) collective-permute-start(bf16[4,13,16,256]{3,2,1,0:T(8,128)(2,1)} %constant_dynamic-slice_fusion), channel_id=1, source_target_pairs={{0,1},{1,2},{2,3},{3,4},{4,5},{5,6},{6,7},{7,0},{8,9},{9,10},{10,1... | collective-permute-start | bytes 1277960 | tf_op jit(solution)/shard_map/ppermute | solution.py:301
  5.5 1.4 %copy-done = bf16[24,16,16,128]{3,2,1,0:T(8,128)(2,1)S(1)} copy-done((bf16[24,16,16,128]{3,2,1,0:T(8,128)(2,1)S(1)}, bf16[24,16,16,128]{3,2,1,0:T(8,128)(2,1)}, u32[]{:S(2)}) %copy-start) | copy-done | bytes 1572888
  6.9 0.7 %copy-done.7 = f32[24]{0:T(128)S(1)} copy-done((f32[24]{0:T(128)S(1)}, f32[24]{0:T(128)}, u32[]{:S(2)}) %copy-start.7) | copy-done | bytes 120
  7.6 2.3 %prepare.1 = (f32[16,16,128]{2,1,0:T(8,128)S(1)}, bf16[16,24,2048]{2,1,0:T(8,128)(2,1)S(1)}, bf16[24,2,16,128]{3,2,1,0:T(8,128)(2,1)}, bf16[24,2,16,128]{3,2,1,0:T(8,128)(2,1)}) custom-call(f32[24]{0:T(128)S(1)} %copy-done.7, bf16[24,16,16,128]{3,2,1,0:T(8,128)(2,1)S(1)} %copy-done), custom_call_target="tpu_custom_call" | custom-call | flops 1000000 | bytes 2000000 | tf_op jit(solution)/shard_map/prepare/pallas_call | solution.py:339
  9.9 1.5 %collective-permute-start = (bf16[24,2,16,128]{3,2,1,0:T(8,128)(2,1)}, bf16[24,2,16,128]{3,2,1,0:T(8,128)(2,1)S(1)}, u32[]{:S(2)}, u32[]{:S(2)}) collective-permute-start(bf16[24,2,16,128]{3,2,1,0:T(8,128)(2,1)} %get-tuple-element.11), channel_id=1, source_target_pairs={{0,1},{1,2},{2,3},{3,4},{4,5},{5,6},{6,7},{7,0},{8,9},{9,10},{10,1... | collective-permute-start | bytes 589832 | tf_op jit(solution)/shard_map/ppermute | solution.py:301
  11.5 3.2 %collective-permute-start.1 = (bf16[24,2,16,128]{3,2,1,0:T(8,128)(2,1)}, bf16[24,2,16,128]{3,2,1,0:T(8,128)(2,1)S(1)}, u32[]{:S(2)}, u32[]{:S(2)}) collective-permute-start(bf16[24,2,16,128]{3,2,1,0:T(8,128)(2,1)} %get-tuple-element.12), channel_id=1, source_target_pairs={{0,7},{1,0},{2,1},{3,2},{4,3},{5,4},{6,5},{7,6},{8,15},{9,8},{10,9... | collective-permute-start | bytes 589832 | tf_op jit(solution)/shard_map/ppermute | solution.py:301
  14.7 0.1 constant_dynamic-slice_fusion.1
  14.8 2.9 %own_part.1 = (f32[24,128]{1,0:T(8,128)S(1)}, bf16[8,16,4096]{2,1,0:T(8,128)(2,1)S(1)}, f32[128,128]{1,0:T(8,128)S(1)}) custom-call(s32[2,8]{1,0:T(2,128)S(1)} %pad_add_fusion.starts, bf16[16,24,2048]{2,1,0:T(8,128)(2,1)S(1)} %get-tuple-element.13.turned_ref, bf16[8,13,16,256]{3,2,1,0:T(8,128)(2,1)S(1)} %copy-done.2, f32[13,13]{1,0:T(8,128)S(1)} %copy-done.6), custom_call_target="tpu_custom_call" | custom-call | flops 2000000 | bytes 4000000 | tf_op jit(solution)/shard_map/own_part/pallas_call | solution.py:365
  17.8 1.6 %collective-permute-start.5 = (bf16[16,16,128]{2,1,0:T(8,128)(2,1)S(1)}, bf16[16,16,128]{2,1,0:T(8,128)(2,1)S(1)}, u32[]{:S(2)}, u32[]{:S(2)}) collective-permute-start(bf16[16,16,128]{2,1,0:T(8,128)(2,1)S(1)} %add_convert_fusion), channel_id=1, source_target_pairs={{0,16},{8,24},{16,0},{24,8},{1,17},{9,25},{17,1},{25,9},{2,18},{10... | collective-permute-start | bytes 196616 | tf_op jit(solution)/shard_map/ppermute | solution.py:305
  19.4 2.8 %collective-permute-done.5 = bf16[16,16,128]{2,1,0:T(8,128)(2,1)S(1)} collective-permute-done((bf16[16,16,128]{2,1,0:T(8,128)(2,1)S(1)}, bf16[16,16,128]{2,1,0:T(8,128)(2,1)S(1)}, u32[]{:S(2)}, u32[]{:S(2)}) %collective-permute-start.5) | collective-permute-done | bytes 65568 | tf_op jit(solution)/shard_map/ppermute | solution.py:305
  22.1 0.7 %fusion.2 = (f32[]{:T(128)}, f32[16,16,128]{2,1,0:T(8,128)S(1)}) fusion(bf16[16,16,128]{2,1,0:T(8,128)(2,1)S(1)} %collective-permute-done.5, bf16[16,16,128]{2,1,0:T(8,128)(2,1)S(1)} %add_convert_fusion), kind=kLoop, calls=%fused_computation.18 | loop fusion | flops 131071 | bytes 262148 | tf_op jit(solution)/shard_map/reduce_sum | solution.py:386
  22.8 0.6 %broadcast_in_dim.3 = f32[8,128]{1,0:T(8,128)S(1)} broadcast(f32[]{:T(128)} %get-tuple-element.20), dimensions={} | broadcast | bytes 4100 | tf_op jit(solution)/shard_map/broadcast_in_dim | solution.py:386
  23.6 3.5 %collective-permute-done.8 = f32[8,128]{1,0:T(8,128)S(1)} collective-permute-done((f32[8,128]{1,0:T(8,128)S(1)}, f32[8,128]{1,0:T(8,128)S(1)}, u32[]{:S(2)}, u32[]{:S(2)}) %collective-permute-start.8) | collective-permute-done | bytes 4128 | tf_op jit(solution)/shard_map/ppermute | solution.py:305
  27.1 0.6 %broadcast_add_fusion = f32[8,128]{1,0:T(8,128)S(1)} fusion(f32[8,128]{1,0:T(8,128)S(1)} %collective-permute-done.8, f32[]{:T(128)} %get-tuple-element.20), kind=kLoop, calls=%fused_computation.8 | loop fusion | flops 1024 | bytes 8196 | tf_op jit(solution)/shard_map/add | solution.py:389
  27.8 0.1 collective-permute-start.9
  27.9 0.4 collective-permute-start.6
  28.2 3.0 %carried_part.1 = (f32[72,128]{1,0:T(8,128)S(1)}, bf16[8,16,4096]{2,1,0:T(8,128)(2,1)S(1)}) custom-call(s32[2,8]{1,0:T(2,128)S(1)} %pad_add_fusion.1.starts, s32[1]{0:T(128)} %bitcast.core, bf16[16,24,2048]{2,1,0:T(8,128)(2,1)S(1)} %get-tuple-element.13.turned_ref, bf16[4,13,16,256]{3,2,1,0:T(8,128)(2,1)S(1)} %collective-permute-done.2.mine_ref, ...), custom_call_target="tpu_custom_call" | custom-call | flops 2000000 | bytes 4000000 | tf_op jit(solution)/shard_map/carried_part/pallas_call | solution.py:405
  31.2 4.5 %collective-permute-start.7 = (f32[72,128]{1,0:T(8,128)S(1)}, f32[72,128]{1,0:T(8,128)S(1)}, u32[]{:S(2)}, u32[]{:S(2)}) collective-permute-start(f32[72,128]{1,0:T(8,128)S(1)} %get-tuple-element.16.message_ref), channel_id=1, source_target_pairs={{0,7},{1,0},{2,1},{3,2},{4,3},{5,4},{6,5},{7,6},{8,15},{9,8},{10,9... | collective-permute-start | bytes 110600 | tf_op jit(solution)/shard_map/ppermute | solution.py:301
  35.7 0.6 %fusion.3 = f32[8,128]{1,0:T(8,128)S(1)} fusion(f32[8,128]{1,0:T(8,128)S(1)} %collective-permute-done.9, f32[8,128]{1,0:T(8,128)S(1)} %collective-permute-done.8, f32[]{:T(128)} %get-tuple-element.20), kind=kLoop, calls=%fused_computation.19 | loop fusion | flops 2048 | bytes 12292 | tf_op jit(solution)/shard_map/add | solution.py:389
  36.3 0.5 collective-permute-start.10
  36.9 4.0 %collective-permute-done.10 = f32[8,128]{1,0:T(8,128)S(1)} collective-permute-done((f32[8,128]{1,0:T(8,128)S(1)}, f32[8,128]{1,0:T(8,128)S(1)}, u32[]{:S(2)}, u32[]{:S(2)}) %collective-permute-start.10) | collective-permute-done | bytes 4128 | tf_op jit(solution)/shard_map/ppermute | solution.py:305
  40.9 10.0 %local_part.1.acc_ref = f32[24,16,16,128]{3,2,1,0:T(8,128)S(1)} custom-call(s32[2,8]{1,0:T(2,128)S(1)} %pad_add_fusion.1.starts, bf16[24,16,16,128]{3,2,1,0:T(8,128)(2,1)S(1)} %copy-done.1, bf16[24,2,16,128]{3,2,1,0:T(8,128)(2,1)S(1)} %collective-permute-done.low_ref, bf16[24,2,16,128]{3,2,1,0:T(8,128)(2,1)S(1)} %collective-permute-done.1.high_ref, ...), custom_call_target="tpu_custom_call" | custom-call | flops 3000000 | bytes 6000000 | tf_op jit(solution)/shard_map/local_part/pallas_call | solution.py:419
  51.0 8.4 %final_part.1 = (bf16[24,16,16,128]{3,2,1,0:T(8,128)(2,1)}, f32[16,16,128]{2,1,0:T(8,128)}) custom-call(s32[2,8]{1,0:T(2,128)S(1)} %pad_add_fusion.starts, f32[24,16,16,128]{3,2,1,0:T(8,128)S(1)} %local_part.1.acc_ref, bf16[8,16,4096]{2,1,0:T(8,128)(2,1)S(1)} %get-tuple-element.19.shifted_ref, f32[24,128]{1,0:T(8,128)S(1)} %get-tuple-element.17.part_ref, ...), custom_call_target="tpu_custom_call" | custom-call | flops 2000000 | bytes 4000000 | tf_op jit(solution)/shard_map/final_part/pallas_call | solution.py:429
  (36 shorter events, 0.3 us)
Async XLA Ops:
  0.6 14.2 %copy-start.2 = (bf16[8,13,16,256]{3,2,1,0:T(8,128)(2,1)S(1)}, bf16[8,13,16,256]{3,2,1,0:T(8,128)(2,1)}, u32[]{:S(2)}) copy-start(bf16[8,13,16,256]{3,2,1,0:T(8,128)(2,1)} %proj_ref.1) | copy-start | bytes 2555908
  0.6 14.0 %copy-start.8 = (s32[3,64]{1,0:T(4,128)S(1)}, s32[3,64]{1,0:T(4,128)}, u32[]{:S(2)}) copy-start(s32[3,64]{1,0:T(4,128)} %param.14) | copy-start | bytes 2308
  0.7 14.1 %copy-start.6 = (f32[13,13]{1,0:T(8,128)S(1)}, f32[13,13]{1,0:T(8,128)}, u32[]{:S(2)}) copy-start(f32[13,13]{1,0:T(8,128)} %coupling_ref.1) | copy-start | bytes 2032
  2.5 21.0 %collective-permute-start.2 = (bf16[4,13,16,256]{3,2,1,0:T(8,128)(2,1)}, bf16[4,13,16,256]{3,2,1,0:T(8,128)(2,1)S(1)}, u32[]{:S(2)}, u32[]{:S(2)}) collective-permute-start(bf16[4,13,16,256]{3,2,1,0:T(8,128)(2,1)} %constant_dynamic-slice_fusion), channel_id=1, source_target_pairs={{0,1},{1,2},{2,3},{3,4},{4,5},{5,6},{6,7},{7,0},{8,9},{9,10},{10,1... | collective-permute-start | bytes 1277960 | tf_op jit(solution)/shard_map/ppermute | solution.py:301
  5.5 1.4 %copy-start = (bf16[24,16,16,128]{3,2,1,0:T(8,128)(2,1)S(1)}, bf16[24,16,16,128]{3,2,1,0:T(8,128)(2,1)}, u32[]{:S(2)}) copy-start(bf16[24,16,16,128]{3,2,1,0:T(8,128)(2,1)} %field_ref.3) | copy-start | bytes 4718596
  6.9 0.7 %copy-start.7 = (f32[24]{0:T(128)S(1)}, f32[24]{0:T(128)}, u32[]{:S(2)}) copy-start(f32[24]{0:T(128)} %occ.1) | copy-start | bytes 292
  9.9 7.8 %collective-permute-start.4 = (f32[16,16,128]{2,1,0:T(8,128)S(1)}, f32[16,16,128]{2,1,0:T(8,128)S(1)}, u32[]{:S(2)}, u32[]{:S(2)}) collective-permute-start(f32[16,16,128]{2,1,0:T(8,128)S(1)} %get-tuple-element.14), channel_id=1, source_target_pairs={{0,8},{8,0},{16,24},{24,16},{1,9},{9,1},{17,25},{25,17},{2,10},{10... | collective-permute-start | bytes 393224 | tf_op jit(solution)/shard_map/ppermute | solution.py:305
  9.9 31.0 %collective-permute-start = (bf16[24,2,16,128]{3,2,1,0:T(8,128)(2,1)}, bf16[24,2,16,128]{3,2,1,0:T(8,128)(2,1)S(1)}, u32[]{:S(2)}, u32[]{:S(2)}) collective-permute-start(bf16[24,2,16,128]{3,2,1,0:T(8,128)(2,1)} %get-tuple-element.11), channel_id=1, source_target_pairs={{0,1},{1,2},{2,3},{3,4},{4,5},{5,6},{6,7},{7,0},{8,9},{9,10},{10,1... | collective-permute-start | bytes 589832 | tf_op jit(solution)/shard_map/ppermute | solution.py:301
  11.5 29.4 %collective-permute-start.1 = (bf16[24,2,16,128]{3,2,1,0:T(8,128)(2,1)}, bf16[24,2,16,128]{3,2,1,0:T(8,128)(2,1)S(1)}, u32[]{:S(2)}, u32[]{:S(2)}) collective-permute-start(bf16[24,2,16,128]{3,2,1,0:T(8,128)(2,1)} %get-tuple-element.12), channel_id=1, source_target_pairs={{0,7},{1,0},{2,1},{3,2},{4,3},{5,4},{6,5},{7,6},{8,15},{9,8},{10,9... | collective-permute-start | bytes 589832 | tf_op jit(solution)/shard_map/ppermute | solution.py:301
  14.7 13.2 %slice-start = ((f32[16,16,128]{2,1,0:T(8,128)}), f32[2,16,128]{2,1,0:T(8,128)S(1)}, s32[]{:S(2)}) async-start(f32[16,16,128]{2,1,0:T(8,128)} %hart_ref.3), calls=%async_computation | async-start | bytes 32768 | tf_op jit(solution)/shard_map/slice | solution.py:396
  14.8 13.5 %copy-start.3 = (f32[16,16,128]{2,1,0:T(8,128)S(1)}, f32[16,16,128]{2,1,0:T(8,128)}, u32[]{:S(2)}) copy-start(f32[16,16,128]{2,1,0:T(8,128)} %hart_ref.3) | copy-start | bytes 393220
  17.8 23.1 %copy-start.1 = (bf16[24,16,16,128]{3,2,1,0:T(8,128)(2,1)S(1)}, bf16[24,16,16,128]{3,2,1,0:T(8,128)(2,1)}, u32[]{:S(2)}) copy-start(bf16[24,16,16,128]{3,2,1,0:T(8,128)(2,1)} %field_ref.3) | copy-start | bytes 4718596
  17.8 23.1 %copy-start.4 = (f32[16,16,128]{2,1,0:T(8,128)S(1)}, f32[16,16,128]{2,1,0:T(8,128)}, u32[]{:S(2)}) copy-start(f32[16,16,128]{2,1,0:T(8,128)} %pot_ref.1) | copy-start | bytes 393220
  17.8 4.3 %collective-permute-start.5 = (bf16[16,16,128]{2,1,0:T(8,128)(2,1)S(1)}, bf16[16,16,128]{2,1,0:T(8,128)(2,1)S(1)}, u32[]{:S(2)}, u32[]{:S(2)}) collective-permute-start(bf16[16,16,128]{2,1,0:T(8,128)(2,1)S(1)} %add_convert_fusion), channel_id=1, source_target_pairs={{0,16},{8,24},{16,0},{24,8},{1,17},{9,25},{17,1},{25,9},{2,18},{10... | collective-permute-start | bytes 196616 | tf_op jit(solution)/shard_map/ppermute | solution.py:305
  23.4 3.7 %collective-permute-start.8 = (f32[8,128]{1,0:T(8,128)S(1)}, f32[8,128]{1,0:T(8,128)S(1)}, u32[]{:S(2)}, u32[]{:S(2)}) collective-permute-start(f32[8,128]{1,0:T(8,128)S(1)} %broadcast_in_dim.3), channel_id=1, source_target_pairs={{0,1},{1,0},{2,3},{3,2},{4,5},{5,4},{6,7},{7,6},{8,9},{9,8},{10,11... | collective-permute-start | bytes 12296 | tf_op jit(solution)/shard_map/ppermute | solution.py:305
  23.5 4.7 %collective-permute-start.3 = (bf16[4,13,16,256]{3,2,1,0:T(8,128)(2,1)S(1)}, bf16[4,13,16,256]{3,2,1,0:T(8,128)(2,1)S(1)}, u32[]{:S(2)}, u32[]{:S(2)}) collective-permute-start(bf16[4,13,16,256]{3,2,1,0:T(8,128)(2,1)S(1)} %collective-permute-done.2.mine_ref), channel_id=1, source_target_pairs={{0,8},{8,0},{16,24},{24,16},{1,9},{9,1},{17,25},{25,17},{2,10},{10... | collective-permute-start | bytes 1277960 | tf_op jit(solution)/shard_map/ppermute | solution.py:305
  27.8 7.9 %collective-permute-start.9 = (f32[8,128]{1,0:T(8,128)S(1)}, f32[8,128]{1,0:T(8,128)S(1)}, u32[]{:S(2)}, u32[]{:S(2)}) collective-permute-start(f32[8,128]{1,0:T(8,128)S(1)} %broadcast_add_fusion), channel_id=1, source_target_pairs={{0,2},{1,3},{2,0},{3,1},{4,6},{5,7},{6,4},{7,5},{8,10},{9,11},{10,... | collective-permute-start | bytes 12296 | tf_op jit(solution)/shard_map/ppermute | solution.py:305
  27.9 13.0 %collective-permute-start.6 = (f32[72,128]{1,0:T(8,128)S(1)}, f32[72,128]{1,0:T(8,128)S(1)}, u32[]{:S(2)}, u32[]{:S(2)}) collective-permute-start(f32[72,128]{1,0:T(8,128)S(1)} %pad_maximum_fusion), channel_id=1, source_target_pairs={{0,1},{1,2},{2,3},{3,4},{4,5},{5,6},{6,7},{7,0},{8,9},{9,10},{10,1... | collective-permute-start | bytes 110600 | tf_op jit(solution)/shard_map/ppermute | solution.py:301
  31.2 19.8 %collective-permute-start.7 = (f32[72,128]{1,0:T(8,128)S(1)}, f32[72,128]{1,0:T(8,128)S(1)}, u32[]{:S(2)}, u32[]{:S(2)}) collective-permute-start(f32[72,128]{1,0:T(8,128)S(1)} %get-tuple-element.16.message_ref), channel_id=1, source_target_pairs={{0,7},{1,0},{2,1},{3,2},{4,3},{5,4},{6,5},{7,6},{8,15},{9,8},{10,9... | collective-permute-start | bytes 110600 | tf_op jit(solution)/shard_map/ppermute | solution.py:301
  36.3 4.6 %collective-permute-start.10 = (f32[8,128]{1,0:T(8,128)S(1)}, f32[8,128]{1,0:T(8,128)S(1)}, u32[]{:S(2)}, u32[]{:S(2)}) collective-permute-start(f32[8,128]{1,0:T(8,128)S(1)} %fusion.3), channel_id=1, source_target_pairs={{0,4},{1,5},{2,6},{3,7},{4,0},{5,1},{6,2},{7,3},{8,12},{9,13},{10,... | collective-permute-start | bytes 12296 | tf_op jit(solution)/shard_map/ppermute | solution.py:305
  40.9 10.1 %copy-start.5 = (f32[16,16,128]{2,1,0:T(8,128)S(1)}, f32[16,16,128]{2,1,0:T(8,128)}, u32[]{:S(2)}) copy-start(f32[16,16,128]{2,1,0:T(8,128)} %ionic_ref.1) | copy-start | bytes 393220

commit v3 on v2

v3 whole, which is shorter than its diff:
```python
import functools
import math

import jax
import jax.numpy as jnp
from jax import lax
from jax.experimental import pallas as pl
from jax.experimental.pallas import tpu as pltpu
from jax.sharding import PartitionSpec as P


LANES = 128
SLOT = 16
LIMIT = 24

screening = 0.25
four_pi = 4.0 * math.pi
f32 = jnp.float32
bf16 = jnp.bfloat16


def vmem():
    return pl.BlockSpec(memory_space=pltpu.VMEM)


def smem():
    return pl.BlockSpec(memory_space=pltpu.SMEM)


def high_hbm():
    return pl.BlockSpec(memory_space=pltpu.HBM)


def hbm():
    return pl.BlockSpec(memory_space=pl.ANY)


NT = (((1,), (1,)), ((), ()))


def start_of(starts, atom, atoms, planes, carried):
    domain = lax.axis_index("space")
    if carried:
        count = lax.axis_size("space")
        domain = lax.rem(domain + (count - 1), count)
    index = domain * atoms + atom
    return lax.rem(starts[0, index], planes), starts[2, index]


def pick_kernel(proj_ref, out_ref, sem):
    half = out_ref.shape[0]
    core = lax.rem(lax.axis_index("band"), 2)
    copy = pltpu.make_async_copy(proj_ref.at[pl.ds(core * half, half)], out_ref, sem)
    copy.start()
    copy.wait()


def prepare_kernel(
    occ, field_hbm, density_ref, turned_ref, first_ref, last_ref, field_ref, wide_ref, sems
):
    count, planes, rows, _ = field_ref.shape
    stride = rows + 1
    groups = sems.shape[0]
    size = planes // groups
    copies = [
        pltpu.make_async_copy(
            field_hbm.at[:, pl.ds(g * size, size)], field_ref.at[:, pl.ds(g * size, size)], sems.at[g]
        )
        for g in range(groups)
    ]
    for copy in copies:
        copy.start()
    for g in range(groups):
        copies[g].wait()

        def one(i):
            plane = g * size + i
            total = jnp.zeros((rows, LANES), f32)
            for o in range(count):
                cells = field_ref[o, plane].astype(f32)
                total = total + (occ[o] * cells) * cells
                wide_ref[i % 2, o * stride : o * stride + rows, :] = cells
            density_ref[plane] = total
            turned_ref[plane] = jnp.concatenate(
                [
                    pltpu.roll(
                        wide_ref[i % 2, pl.ds(r, count, stride=stride), :], (SLOT * r) % LANES, 1
                    )
                    for r in range(rows)
                ],
                axis=1,
            ).astype(bf16)

        for i in range(size):
            one(i)
    first_ref[...] = field_ref[:, :2]
    last_ref[...] = field_ref[:, planes - 2 :]


def shift_projectors(raw_ref, index, atom, column, rows_ref, shifted_ref):
    nproj, box, square = raw_ref.shape[1:]
    stride = box + 1
    tiles = square // LANES
    for p in range(SLOT):
        if p < nproj:
            cells = raw_ref[index, p].astype(f32)
        else:
            cells = jnp.zeros((box, square), f32)
        for t in range(tiles):
            rows_ref[t, p * stride : p * stride + box, :] = cells[:, t * LANES : (t + 1) * LANES]
    for j in range(box):
        for t in range(tiles):
            cells = rows_ref[t, pl.ds(j, SLOT, stride=stride), :].astype(bf16)
            k = j * tiles + t
            shifted_ref[atom, :, k * LANES : (k + 1) * LANES] = pltpu.roll(cells, column, 1)
    shifted_ref[atom, :, box * square :] = jnp.zeros((SLOT, square), bf16)


def lane_group(column, height):
    lane = lax.broadcasted_iota(jnp.int32, (height, LANES), 1)
    return lax.shift_right_logical(jnp.bitwise_and(lane - column + LANES, LANES - 1), 4)


def gather_atom(turned_ref, shifted_ref, atom, offset, column, lift, boxed_ref):
    planes, count, _ = turned_ref.shape
    box = SLOT
    tiles = boxed_ref.shape[1] // (box * LANES)
    per_tile = LANES // box
    group = lane_group(column, count)
    masks = [group == r for r in range(per_tile)]
    for j in range(box):
        plane = offset + j - lift
        valid = jnp.logical_and(plane >= 0, plane < planes)
        plane = jnp.clip(plane, 0, planes - 1)
        for t in range(tiles):
            base = t * per_tile * LANES
            cells = turned_ref[plane, :, base : base + LANES]
            for r in range(1, per_tile):
                low = base + r * LANES
                cells = jnp.where(masks[r], turned_ref[plane, :, low : low + LANES], cells)
            k = j * tiles + t
            boxed_ref[:, k * LANES : (k + 1) * LANES] = jnp.where(valid, cells, jnp.zeros_like(cells))
    shifted = shifted_ref[atom, :, : boxed_ref.shape[1]]
    return lax.dot_general(boxed_ref[...], shifted, NT, preferred_element_type=f32)


def own_kernel(
    starts, turned_ref, proj_ref, coupling_ref, partial_ref, partner_ref,
    part_ref, shifted_ref, wide_coupling_ref, pair_ref, rows_ref, boxed_ref,
):
    atoms, nproj = proj_ref.shape[:2]
    pair_ref[...] = (partial_ref[...] + partner_ref[...]).astype(pair_ref.dtype)
    planes = turned_ref.shape[0]
    for a in range(atoms):
        offset, column = start_of(starts, a, atoms, planes, False)
        shift_projectors(proj_ref, a, a, column, rows_ref.at[a % 2], shifted_ref)
    for a in range(atoms):
        offset, column = start_of(starts, a, atoms, planes, False)
        part_ref[:, a * SLOT : (a + 1) * SLOT] = gather_atom(
            turned_ref, shifted_ref, a, offset, column, 0, boxed_ref.at[a % 2]
        )
    slots = atoms * SLOT
    spread = (
        lax.broadcasted_iota(jnp.int32, (nproj, slots), 0)
        == lax.broadcasted_iota(jnp.int32, (nproj, slots), 1) % SLOT
    ).astype(f32)
    exact = dict(precision=lax.Precision.HIGHEST, preferred_element_type=f32)
    right = lax.dot_general(coupling_ref[...], spread, (((0,), (0,)), ((), ())), **exact)
    both = lax.dot_general(spread, right, (((0,), (0,)), ((), ())), **exact)
    same = (
        lax.broadcasted_iota(jnp.int32, (slots, slots), 0) // SLOT
        == lax.broadcasted_iota(jnp.int32, (slots, slots), 1) // SLOT
    )
    wide_coupling_ref[...] = jnp.where(same, both, 0.0)


def carried_kernel(
    starts, turned_ref, mine_ref, other_ref, hart_ref, dens_ref,
    message_ref, shifted_ref, rows_ref, boxed_ref,
):
    half = mine_ref.shape[0]
    planes, count, _ = turned_ref.shape
    rows = hart_ref.shape[1]
    core = lax.rem(lax.axis_index("band"), 2)
    for q in range(half):
        a = core * half + q
        offset, column = start_of(starts, a, 2 * half, planes, True)
        shift_projectors(mine_ref, q, a, column, rows_ref.at[0], shifted_ref)
        a = (1 - core) * half + q
        offset, column = start_of(starts, a, 2 * half, planes, True)
        shift_projectors(other_ref, q, a, column, rows_ref.at[1], shifted_ref)
    for a in range(2 * half):
        offset, column = start_of(starts, a, 2 * half, planes, True)
        message_ref[:count, a * SLOT : (a + 1) * SLOT] = gather_atom(
            turned_ref, shifted_ref, a, offset, column, planes, boxed_ref.at[a % 2]
        )
    message_ref[count : count + 2 * rows] = hart_ref[:2].reshape(2 * rows, LANES)
    message_ref[count + 2 * rows :] = dens_ref[0]


def weigh(coef, coupling_ref):
    return lax.dot_general(
        coef, coupling_ref[...], (((1,), (0,)), ((), ())),
        precision=lax.Precision.HIGHEST, preferred_element_type=f32,
    ).astype(bf16)


def lane_masks(starts, planes, carried, masks_ref):
    atoms, per_tile = masks_ref.shape[:2]
    for a in range(atoms):
        group = lane_group(start_of(starts, a, atoms, planes, carried)[1], SLOT)
        for r in range(per_tile):
            masks_ref[a, r] = jnp.where(group == r, 1.0, 0.0).astype(bf16)


def deposit_plane(starts, shifted_ref, masks_ref, weighted, plane, planes, carried, wide_ref):
    atoms, per_tile = masks_ref.shape[:2]
    count = weighted.shape[0]
    box = SLOT
    tiles = shifted_ref.shape[2] // ((box + 1) * LANES)
    rows = tiles * per_tile
    places = []
    for a in range(atoms):
        j = plane - start_of(starts, a, atoms, planes, carried)[0]
        if carried:
            j = j + planes
        places.append(jnp.where(jnp.logical_and(j >= 0, j < box), j, box) * (tiles * LANES))
    for t in range(tiles):
        cells = [
            shifted_ref[a, :, pl.ds(pl.multiple_of(places[a] + t * LANES, LANES), LANES)]
            for a in range(atoms)
        ]
        for r in range(per_tile):
            placed = jnp.concatenate([cells[a] * masks_ref[a, r] for a in range(atoms)], axis=0)
            update = jnp.dot(weighted, placed, preferred_element_type=f32)
            row = t * per_tile + r
            wide_ref[pl.ds(row, count, stride=rows + 1), :] = pltpu.roll(
                update, (-SLOT * row) % LANES, 1
            )


def pad_rows(padded_ref, index, cells):
    rows = cells.shape[0]
    base = index * (rows + 8)
    padded_ref[base + 2 : base + 2 + rows, :] = cells
    padded_ref[base : base + 2, :] = cells[rows - 2 :]
    padded_ref[base + 2 + rows : base + 4 + rows, :] = cells[:2]


def stencil_plane(padded_ref, index, below2, below1, c, above1, above2, potential):
    rows = c.shape[0]
    base = index * (rows + 8)
    near = below1 + above1
    near = near + padded_ref[base + 1 : base + 1 + rows, :] + padded_ref[base + 3 : base + 3 + rows, :]
    near = near + pltpu.roll(c, 1, 1) + pltpu.roll(c, LANES - 1, 1)
    far = below2 + above2
    far = far + padded_ref[base : base + rows, :] + padded_ref[base + 4 : base + 4 + rows, :]
    far = far + pltpu.roll(c, 2, 1) + pltpu.roll(c, LANES - 2, 1)
    return (potential + 3.75) * c - (2.0 / 3.0) * near + (1.0 / 24.0) * far


def inner_kernel(field_ref, pot_ref, acc_ref, padded_ref):
    count, planes, _, _ = field_ref.shape

    def one(o, _):
        cells = [field_ref[o, i].astype(f32) for i in range(planes)]
        for i in range(2, planes - 2):
            pad_rows(padded_ref, i, cells[i])
            acc_ref[o, i] = stencil_plane(padded_ref, i, *cells[i - 2 : i + 3], pot_ref[i])
        return 0

    lax.fori_loop(0, count, one, 0)


def add_kernel(one_ref, other_ref, out_ref):
    out_ref[...] = one_ref[...] + other_ref[...]


def shift_kernel(cells, pot_ref, charge_ref, out_ref):
    scale = 1.0 / (6.0 + screening)
    shift = charge_ref[0:1, 0:1] * (four_pi * scale * (1.0 + 6.0 * scale) / cells)
    out_ref[...] = pot_ref[...] - shift[None]


def join_kernel(pair_ref, partner_ref, part_ref, hart_ref, density_ref, charge_ref, message_ref):
    planes, rows, _ = density_ref.shape
    count = part_ref.shape[0]
    density = pair_ref[...].astype(f32) + partner_ref[...].astype(f32)
    density_ref[...] = density
    charge_ref[...] = jnp.full(charge_ref.shape, jnp.sum(density), f32)
    message_ref[:count] = part_ref[...]
    message_ref[count : count + 2 * rows] = hart_ref[planes - 2 :].reshape(2 * rows, LANES)
    message_ref[count + 2 * rows :] = density[planes - 1]


def local_kernel(
    starts, inner_ref, field_ref, low_ref, high_ref, shifted_ref, message_ref, below_ref,
    coupling_ref, pot_ref, acc_ref, masks_ref, wide_ref, padded_ref,
):
    count, planes, rows, _ = field_ref.shape
    lane_masks(starts, planes, True, masks_ref)
    weighted = weigh(message_ref[:count] + below_ref[:count], coupling_ref)

    def one(o, _):
        cells = {i: field_ref[o, i].astype(f32) for i in (0, 1, 2, 3)}
        cells.update({i: field_ref[o, i].astype(f32) for i in range(planes - 4, planes)})
        for i in range(2):
            cells[i - 2] = low_ref[o, i].astype(f32)
            cells[planes + i] = high_ref[o, i].astype(f32)
        for k, i in enumerate((0, 1, planes - 2, planes - 1)):
            pad_rows(padded_ref, k, cells[i])
            acc_ref[o, i] = stencil_plane(
                padded_ref, k, *[cells[i + d] for d in range(-2, 3)], pot_ref[i]
            )
        return 0

    lax.fori_loop(0, count, one, 0)

    def two(pair, _):
        for half in range(2):
            plane = 2 * pair + half
            deposit_plane(
                starts, shifted_ref, masks_ref, weighted, plane, planes, True, wide_ref.at[half]
            )
            for o in range(count):
                low = o * (rows + 1)
                acc_ref[o, plane] += wide_ref[half, low : low + rows, :]
        return 0

    lax.fori_loop(0, planes // 2, two, 0)


def final_kernel(
    starts, acc_ref, shifted_ref, part_ref, above_ref, coupling_ref,
    dens_ref, hart_ref, ionic_ref, below_ref,
    out_ref, pot_ref, masks_ref, wide_ref, done_ref, sems,
):
    count, planes, rows, _ = done_ref.shape
    lane_masks(starts, planes, False, masks_ref)
    weighted = weigh(part_ref[...] + above_ref[:count], coupling_ref)
    groups = sems.shape[0]
    size = planes // groups
    copies = []
    for group in range(groups):
        def two(pair, _):
            for half in range(2):
                plane = group * size + 2 * pair + half
                deposit_plane(
                    starts, shifted_ref, masks_ref, weighted, plane, planes, False, wide_ref.at[half]
                )
                for o in range(count):
                    low = o * (rows + 1)
                    done_ref[o, plane] = (
                        acc_ref[o, plane] + wide_ref[half, low : low + rows, :]
                    ).astype(bf16)
            return 0

        lax.fori_loop(0, size // 2, two, 0)
        part = pl.ds(group * size, size)
        copies.append(
            pltpu.make_async_copy(done_ref.at[:, part], out_ref.at[:, part], sems.at[group])
        )
        copies[-1].start()

    field = jnp.concatenate(
        [
            below_ref[count : count + 2 * rows].reshape(2, rows, LANES),
            hart_ref[...],
            above_ref[count : count + 2 * rows].reshape(2, rows, LANES),
        ],
        axis=0,
    )
    dens = jnp.concatenate(
        [
            below_ref[count + 2 * rows :].reshape(1, rows, LANES),
            dens_ref[...],
            above_ref[count + 2 * rows :].reshape(1, rows, LANES),
        ],
        axis=0,
    )
    source = four_pi * dens
    scale = 1.0 / (6.0 + screening)

    def relax(h, s):
        inner = h[1:-1]
        size = inner.shape
        flat = inner.reshape(size[0] * rows, LANES)
        across = pltpu.roll(flat, 1, 1) + pltpu.roll(flat, LANES - 1, 1)
        total = h[2:] + h[:-2] + across.reshape(size)
        total = total + pltpu.roll(inner, 1, 1) + pltpu.roll(inner, rows - 1, 1)
        return (total + s) * scale

    once = relax(field, source)
    twice = relax(once, source[1:-1])
    third = (3.0 / math.pi) * dens_ref[...]
    root = jnp.exp(jnp.log(jnp.maximum(third, 1e-37)) * (1.0 / 3.0))
    root = (2.0 * root + third / jnp.maximum(root * root, 1e-30)) * (1.0 / 3.0)
    root = jnp.where(third > 0.0, root, 0.0)
    pot_ref[...] = ionic_ref[...] + twice - root
    for copy in copies:
        copy.wait()


def around(block, axis, distance):
    count = lax.axis_size(axis)
    return lax.ppermute(block, axis, [(i, (i + distance) % count) for i in range(count)])


def swap(block, axis, mask):
    return lax.ppermute(block, axis, [(i, i ^ mask) for i in range(lax.axis_size(axis))])


def local(
    orbitals, occupations, potential_in, ionic_potential, hartree_prev, projectors, box_start, coupling
):
    count, planes, rows, lanes = orbitals.shape
    atoms, nproj, box, square = projectors.shape
    n_space = lax.axis_size("space")
    n_band = lax.axis_size("band")
    half = atoms // 2
    slots = atoms * SLOT
    cells = planes * rows * lanes
    params = pltpu.CompilerParams(vmem_limit_bytes=LIMIT << 20)

    def call(kernel, work, **kwargs):
        cost = pl.CostEstimate(flops=work * 500000, bytes_accessed=work * 1000000, transcendentals=0)
        return pl.pallas_call(kernel, compiler_params=params, cost_estimate=cost, **kwargs)

    picked = call(
        pick_kernel, 1,
        in_specs=[high_hbm()],
        out_specs=vmem(),
        out_shape=jax.ShapeDtypeStruct((half, nproj, box, square), projectors.dtype),
        scratch_shapes=[pltpu.SemaphoreType.DMA],
    )(projectors)
    mine = around(picked, "space", 1)
    other = swap(mine, "band", 1)

    groups = 4
    stride = rows + 1
    partial, turned, first, last = call(
        prepare_kernel, 2,
        in_specs=[smem(), high_hbm()],
        out_specs=(vmem(),) * 4,
        out_shape=(
            jax.ShapeDtypeStruct((planes, rows, lanes), f32),
            jax.ShapeDtypeStruct((planes, count, rows * lanes), bf16),
            jax.ShapeDtypeStruct((count, 2, rows, lanes), bf16),
            jax.ShapeDtypeStruct((count, 2, rows, lanes), bf16),
        ),
        scratch_shapes=[
            pltpu.VMEM((count, planes, rows, lanes), bf16),
            pltpu.VMEM((2, count * stride, lanes), f32),
            pltpu.SemaphoreType.DMA((groups,)),
        ],
    )(occupations, orbitals)
    low = around(last, "space", 1)
    high = around(first, "space", -1)

    shifted_shape = jax.ShapeDtypeStruct((atoms, SLOT, (box + 1) * square), bf16)
    gather_scratch = [
        pltpu.VMEM((2, square // lanes, SLOT * (box + 1), lanes), f32),
        pltpu.VMEM((2, count, box * square), bf16),
    ]
    own_part, own_shifted, wide_coupling, pair = call(
        own_kernel, 4,
        in_specs=[smem()] + [vmem()] * 5,
        out_specs=(vmem(),) * 4,
        out_shape=(
            jax.ShapeDtypeStruct((count, slots), f32),
            shifted_shape,
            jax.ShapeDtypeStruct((slots, slots), f32),
            jax.ShapeDtypeStruct((planes, rows, lanes), bf16),
        ),
        scratch_shapes=gather_scratch,
    )(box_start, turned, projectors, coupling, partial, swap(partial, "band", 1))

    inner = call(
        inner_kernel, 3,
        in_specs=[vmem(), vmem()],
        out_specs=vmem(),
        out_shape=jax.ShapeDtypeStruct((count, planes, rows, lanes), f32),
        scratch_shapes=[pltpu.VMEM((planes * (rows + 8), lanes), f32)],
    )(orbitals, potential_in)

    mask = 2
    while 2 * mask < n_band:
        pair = (pair.astype(f32) + swap(pair, "band", mask).astype(f32)).astype(bf16)
        mask *= 2
    message_shape = jax.ShapeDtypeStruct((count + 3 * rows, lanes), f32)
    density, charge, message = call(
        join_kernel, 1,
        in_specs=[vmem()] * 4,
        out_specs=(vmem(),) * 3,
        out_shape=(
            jax.ShapeDtypeStruct((planes, rows, lanes), f32),
            jax.ShapeDtypeStruct((8, lanes), f32),
            message_shape,
        ),
    )(pair, swap(pair, "band", mask), own_part, hartree_prev)
    below = around(message, "space", 1)
    mask = 1
    while mask < n_space:
        charge = call(
            add_kernel, 1,
            in_specs=[vmem(), vmem()],
            out_specs=vmem(),
            out_shape=jax.ShapeDtypeStruct((8, lanes), f32),
        )(charge, swap(charge, "space", mask))
        mask *= 2

    message, prev_shifted = call(
        carried_kernel, 4,
        in_specs=[smem()] + [vmem()] * 5,
        out_specs=(vmem(), vmem()),
        out_shape=(message_shape, shifted_shape),
        scratch_shapes=gather_scratch,
    )(box_start, turned, mine, other, hartree_prev, density)

    above = around(message, "space", -1)

    deposit_scratch = [
        pltpu.VMEM((atoms, lanes // SLOT, SLOT, lanes), bf16),
        pltpu.VMEM((2, count * stride, lanes), f32),
    ]
    acc = call(
        local_kernel, 4,
        in_specs=[smem()] + [vmem()] * 9,
        out_specs=vmem(),
        out_shape=jax.ShapeDtypeStruct((count, planes, rows, lanes), f32),
        scratch_shapes=deposit_scratch + [pltpu.VMEM((4 * (rows + 8), lanes), f32)],
        input_output_aliases={1: 0},
    )(
        box_start, inner, orbitals, low, high, prev_shifted, message, below, wide_coupling,
        potential_in,
    )

    applied, potential = call(
        final_kernel, 4,
        in_specs=[smem()] + [vmem()] * 9,
        out_specs=(hbm(), vmem()),
        out_shape=(
            jax.ShapeDtypeStruct((count, planes, rows, lanes), bf16),
            jax.ShapeDtypeStruct((planes, rows, lanes), f32),
        ),
        scratch_shapes=deposit_scratch
        + [
            pltpu.VMEM((count, planes, rows, lanes), bf16),
            pltpu.SemaphoreType.DMA((4,)),
        ],
    )(
        box_start, acc, own_shifted, own_part, above, wide_coupling,
        density, hartree_prev, ionic_potential, below,
    )
    potential = call(
        functools.partial(shift_kernel, float(cells * n_space)), 1,
        in_specs=[vmem(), vmem()],
        out_specs=vmem(),
        out_shape=jax.ShapeDtypeStruct((planes, rows, lanes), f32),
    )(potential, charge)
    return applied, potential


def solution(mesh):
    placed = (
        P("band", "space", None, None),
        P("band"),
        P("space", None, None),
        P("space", None, None),
        P("space", None, None),
        P("space", None, None, None),
        P(),
        P(),
    )

    return jax.shard_map(
        local,
        mesh=mesh,
        in_specs=placed,
        out_specs=(P("band", "space", None, None), P("space", None, None)),
        check_vma=False,
    )
```

time: 59.6 us -> 68 us (1.14)
  waiting for transfers between devices: 10.3 us -> 24.3 us
  other arithmetic: 1.99 us -> 0 us
  Pallas kernels: 26.7 us -> 24.8 us
  local copies, waits for them, and re-layouts: 4.68 us -> 3.25 us
    ppermute x5, waiting for transfers between devices: 0.01 us -> 12.9 us  [around(): lax.ppermute(block, axis, [(i, (i + distance) % count) for i in range(cou...]
    dynamic_slice x2 -> x0, local copies, waits for them, and re-layouts: 1.94 us -> none  [the longest x1 1.86 us: local(): lax.dynamic_slice_in_dim(projectors, core * half, half, 0)]
    pallas_call x5 -> x12, Pallas kernels: 26.7 us -> 24.8 us  [the longest x1 7.05 us: local(): call(local_kernel, 4, in_specs=[smem()] + [vmem()] * 9, out_specs=vmem(),...]
    add x3 -> x0, other arithmetic: 1.28 us -> none  [local(): charge = charge + swap(charge, 'space', mask)]
    unnamed x18 -> x20, local copies, waits for them, and re-layouts: 2.1 us -> 3.25 us
    ppermute x6, waiting for transfers between devices: 10.3 us -> 11.4 us  [swap(): lax.ppermute(block, axis, [(i, i ^ mask) for i in range(lax.axis_size(axi...]
  transfers between devices with their start and end apart: 11 -> 11, of which waited for: 3 -> 5; matrix products, arithmetic and copies ran while one was open for 5% -> 0% of each run, Pallas kernels for 31% -> 27%
where the time goes in v3:
time: 68 us; the launch traced here: 67.8 us
  Pallas kernels  24.8 us (36%)
  waiting for transfers between devices  24.3 us (36%)
  starting transfers between devices  14.7 us (22%)
  local copies, waits for them, and re-layouts  3.25 us (5%)
  between operations  0.8 us (1%)
    ppermute x5, waiting for transfers between devices, around(): lax.ppermute(block, axis, [(i, (i + distance) % count) for i in range(cou...  12.9 us
    ppermute x5, starting transfers between devices, around(): lax.ppermute(block, axis, [(i, (i + distance) % count) for i in range(cou...  12.6 us
    ppermute x6, waiting for transfers between devices, swap(): lax.ppermute(block, axis, [(i, i ^ mask) for i in range(lax.axis_size(axi...  11.4 us
    pallas_call x1, Pallas kernels, local(): call(local_kernel, 4, in_specs=[smem()] + [vmem()] * 9, out_specs=vmem(),...  7.05 us
    pallas_call x1, Pallas kernels, local(): call(final_kernel, 4, in_specs=[smem()] + [vmem()] * 9, out_specs=(hbm(),...  5.8 us
    unnamed x20, local copies, waits for them, and re-layouts  3.25 us
    pallas_call x1, Pallas kernels, local(): call(inner_kernel, 3, in_specs=[vmem(), vmem()], out_specs=vmem(), out_sh...  3.06 us
    pallas_call x1, Pallas kernels, local(): call(own_kernel, 4, in_specs=[smem()] + [vmem()] * 5, out_specs=(vmem(),)...  3.05 us
  transfers between devices with their start and end apart: 11, of which 5 were waited for; matrix products, arithmetic and copies ran while one was open for 0% of the time, Pallas kernels for 27%

profile of v3, /device:TPU:0, one launch (start us, length us, event | category | flops | bytes accessed | tf_op | source)
XLA Modules:
  0.0 67.8 jit_solution(8941217999715567102)
XLA Ops:
  0.6 1.1 %copy-done.2 = bf16[8,13,16,256]{3,2,1,0:T(8,128)(2,1)S(1)} copy-done((bf16[8,13,16,256]{3,2,1,0:T(8,128)(2,1)S(1)}, bf16[8,13,16,256]{3,2,1,0:T(8,128)(2,1)}, u32[]{:S(2)}) %copy-start.2) | copy-done | bytes 851992
  1.8 0.2 shard_map.97
  2.0 3.0 %collective-permute-start.2 = (bf16[4,13,16,256]{3,2,1,0:T(8,128)(2,1)S(1)}, bf16[4,13,16,256]{3,2,1,0:T(8,128)(2,1)S(1)}, u32[]{:S(2)}, u32[]{:S(2)}) collective-permute-start(bf16[4,13,16,256]{3,2,1,0:T(8,128)(2,1)S(1)} %shard_map.97), channel_id=1, source_target_pairs={{0,1},{1,2},{2,3},{3,4},{4,5},{5,6},{6,7},{7,0},{8,9},{9,10},{10,1... | collective-permute-start | bytes 1277960 | tf_op jit(solution)/shard_map/ppermute | solution.py:406
  5.1 12.9 %collective-permute-done.2.mine_ref = bf16[4,13,16,256]{3,2,1,0:T(8,128)(2,1)S(1)} collective-permute-done((bf16[4,13,16,256]{3,2,1,0:T(8,128)(2,1)S(1)}, bf16[4,13,16,256]{3,2,1,0:T(8,128)(2,1)S(1)}, u32[]{:S(2)}, u32[]{:S(2)}) %collective-permute-start.2) | collective-permute-done | bytes 426016 | tf_op jit(solution)/shard_map/ppermute | solution.py:406
  17.9 1.4 %copy-done = bf16[24,16,16,128]{3,2,1,0:T(8,128)(2,1)S(1)} copy-done((bf16[24,16,16,128]{3,2,1,0:T(8,128)(2,1)S(1)}, bf16[24,16,16,128]{3,2,1,0:T(8,128)(2,1)}, u32[]{:S(2)}) %copy-start) | copy-done | bytes 1572888
  19.4 0.7 copy-done.9
  20.0 1.7 %shard_map.96 = (f32[16,16,128]{2,1,0:T(8,128)S(1)}, bf16[16,24,2048]{2,1,0:T(8,128)(2,1)S(1)}, bf16[24,2,16,128]{3,2,1,0:T(8,128)(2,1)S(1)}, bf16[24,2,16,128]{3,2,1,0:T(8,128)(2,1)S(1)}) custom-call(f32[24]{0:T(128)S(1)} %copy-done.9, bf16[24,16,16,128]{3,2,1,0:T(8,128)(2,1)S(1)} %copy-done), custom_call_target="tpu_custom_call" | custom-call | flops 1000000 | bytes 2000000 | tf_op jit(solution)/shard_map/pallas_call | solution.py:441
  21.8 0.0 copy-start.4
  21.8 0.6 collective-permute-start.4
  22.4 4.7 %collective-permute-start.1 = (bf16[24,2,16,128]{3,2,1,0:T(8,128)(2,1)S(1)}, bf16[24,2,16,128]{3,2,1,0:T(8,128)(2,1)S(1)}, u32[]{:S(2)}, u32[]{:S(2)}) collective-permute-start(bf16[24,2,16,128]{3,2,1,0:T(8,128)(2,1)S(1)} %get-tuple-element.18), channel_id=1, source_target_pairs={{0,7},{1,0},{2,1},{3,2},{4,3},{5,4},{6,5},{7,6},{8,15},{9,8},{10,9... | collective-permute-start | bytes 589832 | tf_op jit(solution)/shard_map/ppermute | solution.py:406
  27.1 3.0 %shard_map.98 = (f32[24,128]{1,0:T(8,128)S(1)}, bf16[8,16,4352]{2,1,0:T(8,128)(2,1)S(1)}, f32[128,128]{1,0:T(8,128)S(1)}, bf16[16,16,128]{2,1,0:T(8,128)(2,1)S(1)}) custom-call(s32[3,64]{1,0:T(4,128)S(1)} %copy-done.7, bf16[16,24,2048]{2,1,0:T(8,128)(2,1)S(1)} %get-tuple-element.19.turned_ref, bf16[8,13,16,256]{3,2,1,0:T(8,128)(2,1)S(1)} %copy-done.3, ...), custom_call_target="tpu_custom_call" | custom-call | flops 2000000 | bytes 4000000 | tf_op jit(solution)/shard_map/pallas_call | solution.py:465
  30.2 1.6 %collective-permute-start.5 = (bf16[16,16,128]{2,1,0:T(8,128)(2,1)S(1)}, bf16[16,16,128]{2,1,0:T(8,128)(2,1)S(1)}, u32[]{:S(2)}, u32[]{:S(2)}) collective-permute-start(bf16[16,16,128]{2,1,0:T(8,128)(2,1)S(1)} %get-tuple-element.21.pair_ref), channel_id=1, source_target_pairs={{0,16},{8,24},{16,0},{24,8},{1,17},{9,25},{17,1},{25,9},{2,18},{10... | collective-permute-start | bytes 196616 | tf_op jit(solution)/shard_map/ppermute | solution.py:410
  31.7 2.8 %collective-permute-done.5.partner_ref = bf16[16,16,128]{2,1,0:T(8,128)(2,1)S(1)} collective-permute-done((bf16[16,16,128]{2,1,0:T(8,128)(2,1)S(1)}, bf16[16,16,128]{2,1,0:T(8,128)(2,1)S(1)}, u32[]{:S(2)}, u32[]{:S(2)}) %collective-permute-start.5) | collective-permute-done | bytes 65568 | tf_op jit(solution)/shard_map/ppermute | solution.py:410
  34.5 0.2 shard_map.99
  34.7 0.1 collective-permute-start.6
  34.8 3.0 %shard_map.100 = (f32[72,128]{1,0:T(8,128)S(1)}, bf16[8,16,4352]{2,1,0:T(8,128)(2,1)S(1)}) custom-call(s32[3,64]{1,0:T(4,128)S(1)} %copy-done.7, bf16[16,24,2048]{2,1,0:T(8,128)(2,1)S(1)} %get-tuple-element.19.turned_ref, bf16[4,13,16,256]{3,2,1,0:T(8,128)(2,1)S(1)} %collective-permute-done.2.mine_ref, ...), custom_call_target="tpu_custom_call" | custom-call | flops 2000000 | bytes 4000000 | tf_op jit(solution)/shard_map/pallas_call | solution.py:512
  37.7 4.7 %collective-permute-start.7 = (f32[72,128]{1,0:T(8,128)S(1)}, f32[72,128]{1,0:T(8,128)S(1)}, u32[]{:S(2)}, u32[]{:S(2)}) collective-permute-start(f32[72,128]{1,0:T(8,128)S(1)} %get-tuple-element.25.message_ref), channel_id=1, source_target_pairs={{0,7},{1,0},{2,1},{3,2},{4,3},{5,4},{6,5},{7,6},{8,15},{9,8},{10,9... | collective-permute-start | bytes 110600 | tf_op jit(solution)/shard_map/ppermute | solution.py:406
  42.4 3.6 %collective-permute-done.8.other_ref = f32[8,128]{1,0:T(8,128)S(1)} collective-permute-done((f32[8,128]{1,0:T(8,128)S(1)}, f32[8,128]{1,0:T(8,128)S(1)}, u32[]{:S(2)}, u32[]{:S(2)}) %collective-permute-start.8) | collective-permute-done | bytes 4128 | tf_op jit(solution)/shard_map/ppermute | solution.py:410
  46.1 3.6 %collective-permute-done.9.other_ref = f32[8,128]{1,0:T(8,128)S(1)} collective-permute-done((f32[8,128]{1,0:T(8,128)S(1)}, f32[8,128]{1,0:T(8,128)S(1)}, u32[]{:S(2)}, u32[]{:S(2)}) %collective-permute-start.9) | collective-permute-done | bytes 4128 | tf_op jit(solution)/shard_map/ppermute | solution.py:410
  49.7 3.1 %shard_map.95.inner_ref = f32[24,16,16,128]{3,2,1,0:T(8,128)S(1)} custom-call(bf16[24,16,16,128]{3,2,1,0:T(8,128)(2,1)S(1)} %copy-done.1, f32[16,16,128]{2,1,0:T(8,128)S(1)} %copy-done.5), custom_call_target="tpu_custom_call" | custom-call | flops 1500000 | bytes 3000000 | tf_op jit(solution)/shard_map/pallas_call | solution.py:478
  52.7 1.4 %collective-permute-done.10.other_ref = f32[8,128]{1,0:T(8,128)S(1)} collective-permute-done((f32[8,128]{1,0:T(8,128)S(1)}, f32[8,128]{1,0:T(8,128)S(1)}, u32[]{:S(2)}, u32[]{:S(2)}) %collective-permute-start.10) | collective-permute-done | bytes 4128 | tf_op jit(solution)/shard_map/ppermute | solution.py:410
  54.2 7.1 %shard_map.101.acc_ref = f32[24,16,16,128]{3,2,1,0:T(8,128)S(1)} custom-call(s32[3,64]{1,0:T(4,128)S(1)} %copy-done.7, f32[24,16,16,128]{3,2,1,0:T(8,128)S(1)} %shard_map.95.inner_ref, bf16[24,16,16,128]{3,2,1,0:T(8,128)(2,1)S(1)} %copy-done.1, bf16[24,2,16,128]{3,2,1,0:T(8,128)(2,1)S(1)} %collective-permute-done.low_ref, ...), custom_call_target="tpu_custom_call", output_to_operand_aliasing={{}: (1, {})} | custom-call | flops 2000000 | bytes 4000000 | tf_op jit(solution)/shard_map/pallas_call | solution.py:526
  61.3 5.8 %shard_map.102 = (bf16[24,16,16,128]{3,2,1,0:T(8,128)(2,1)}, f32[16,16,128]{2,1,0:T(8,128)S(1)}) custom-call(s32[3,64]{1,0:T(4,128)S(1)} %copy-done.7, f32[24,16,16,128]{3,2,1,0:T(8,128)S(1)} %shard_map.101.acc_ref, bf16[8,16,4352]{2,1,0:T(8,128)(2,1)S(1)} %get-tuple-element.28.shifted_ref, f32[24,128]{1,0:T(8,128)S(1)} %get-tuple-element.22.part_ref, ...), custom_call_target="tpu_custom_call" | custom-call | flops 2000000 | bytes 4000000 | tf_op jit(solution)/shard_map/pallas_call | solution.py:538
  67.1 0.7 %shard_map.106 = f32[16,16,128]{2,1,0:T(8,128)} custom-call(f32[16,16,128]{2,1,0:T(8,128)S(1)} %get-tuple-element.30.pot_ref, f32[8,128]{1,0:T(8,128)S(1)} %shard_map.105.charge_ref), custom_call_target="tpu_custom_call" | custom-call | flops 500000 | bytes 1000000 | tf_op jit(solution)/shard_map/pallas_call | solution.py:555
  (30 shorter events, 0.1 us)
Async XLA Ops:
  0.6 1.2 %copy-start.2 = (bf16[8,13,16,256]{3,2,1,0:T(8,128)(2,1)S(1)}, bf16[8,13,16,256]{3,2,1,0:T(8,128)(2,1)}, u32[]{:S(2)}) copy-start(bf16[8,13,16,256]{3,2,1,0:T(8,128)(2,1)} %proj_ref.3) | copy-start | bytes 2555908
  1.8 25.3 %copy-start.3 = (bf16[8,13,16,256]{3,2,1,0:T(8,128)(2,1)S(1)}, bf16[8,13,16,256]{3,2,1,0:T(8,128)(2,1)}, u32[]{:S(2)}) copy-start(bf16[8,13,16,256]{3,2,1,0:T(8,128)(2,1)} %proj_ref.3) | copy-start | bytes 2555908
  1.8 25.3 %copy-start.7 = (s32[3,64]{1,0:T(4,128)S(1)}, s32[3,64]{1,0:T(4,128)}, u32[]{:S(2)}) copy-start(s32[3,64]{1,0:T(4,128)} %starts.7) | copy-start | bytes 2308
  1.8 25.3 %copy-start.8 = (f32[13,13]{1,0:T(8,128)S(1)}, f32[13,13]{1,0:T(8,128)}, u32[]{:S(2)}) copy-start(f32[13,13]{1,0:T(8,128)} %coupling_ref.1) | copy-start | bytes 2032
  2.0 15.9 %collective-permute-start.2 = (bf16[4,13,16,256]{3,2,1,0:T(8,128)(2,1)S(1)}, bf16[4,13,16,256]{3,2,1,0:T(8,128)(2,1)S(1)}, u32[]{:S(2)}, u32[]{:S(2)}) collective-permute-start(bf16[4,13,16,256]{3,2,1,0:T(8,128)(2,1)S(1)} %shard_map.97), channel_id=1, source_target_pairs={{0,1},{1,2},{2,3},{3,4},{4,5},{5,6},{6,7},{7,0},{8,9},{9,10},{10,1... | collective-permute-start | bytes 1277960 | tf_op jit(solution)/shard_map/ppermute | solution.py:406
  17.9 16.8 %collective-permute-start.3 = (bf16[4,13,16,256]{3,2,1,0:T(8,128)(2,1)S(1)}, bf16[4,13,16,256]{3,2,1,0:T(8,128)(2,1)S(1)}, u32[]{:S(2)}, u32[]{:S(2)}) collective-permute-start(bf16[4,13,16,256]{3,2,1,0:T(8,128)(2,1)S(1)} %collective-permute-done.2.mine_ref), channel_id=1, source_target_pairs={{0,8},{8,0},{16,24},{24,16},{1,9},{9,1},{17,25},{25,17},{2,10},{10... | collective-permute-start | bytes 1277960 | tf_op jit(solution)/shard_map/ppermute | solution.py:410
  17.9 1.4 %copy-start = (bf16[24,16,16,128]{3,2,1,0:T(8,128)(2,1)S(1)}, bf16[24,16,16,128]{3,2,1,0:T(8,128)(2,1)}, u32[]{:S(2)}) copy-start(bf16[24,16,16,128]{3,2,1,0:T(8,128)(2,1)} %field_ref.3) | copy-start | bytes 4718596
  19.4 0.7 copy-start.9
  21.8 12.7 %copy-start.4 = (f32[16,16,128]{2,1,0:T(8,128)S(1)}, f32[16,16,128]{2,1,0:T(8,128)}, u32[]{:S(2)}) copy-start(f32[16,16,128]{2,1,0:T(8,128)} %hart_ref.5) | copy-start | bytes 393220
  21.8 5.3 %collective-permute-start.4 = (f32[16,16,128]{2,1,0:T(8,128)S(1)}, f32[16,16,128]{2,1,0:T(8,128)S(1)}, u32[]{:S(2)}, u32[]{:S(2)}) collective-permute-start(f32[16,16,128]{2,1,0:T(8,128)S(1)} %get-tuple-element.20.partial_ref), channel_id=1, source_target_pairs={{0,8},{8,0},{16,24},{24,16},{1,9},{9,1},{17,25},{25,17},{2,10},{10... | collective-permute-start | bytes 393224 | tf_op jit(solution)/shard_map/ppermute | solution.py:410
  22.3 31.8 %collective-permute-start = (bf16[24,2,16,128]{3,2,1,0:T(8,128)(2,1)S(1)}, bf16[24,2,16,128]{3,2,1,0:T(8,128)(2,1)S(1)}, u32[]{:S(2)}, u32[]{:S(2)}) collective-permute-start(bf16[24,2,16,128]{3,2,1,0:T(8,128)(2,1)S(1)} %get-tuple-element.17), channel_id=1, source_target_pairs={{0,1},{1,2},{2,3},{3,4},{4,5},{5,6},{6,7},{7,0},{8,9},{9,10},{10,1... | collective-permute-start | bytes 589832 | tf_op jit(solution)/shard_map/ppermute | solution.py:406
  22.4 31.8 %collective-permute-start.1 = (bf16[24,2,16,128]{3,2,1,0:T(8,128)(2,1)S(1)}, bf16[24,2,16,128]{3,2,1,0:T(8,128)(2,1)S(1)}, u32[]{:S(2)}, u32[]{:S(2)}) collective-permute-start(bf16[24,2,16,128]{3,2,1,0:T(8,128)(2,1)S(1)} %get-tuple-element.18), channel_id=1, source_target_pairs={{0,7},{1,0},{2,1},{3,2},{4,3},{5,4},{6,5},{7,6},{8,15},{9,8},{10,9... | collective-permute-start | bytes 589832 | tf_op jit(solution)/shard_map/ppermute | solution.py:406
  30.1 19.5 %copy-start.1 = (bf16[24,16,16,128]{3,2,1,0:T(8,128)(2,1)S(1)}, bf16[24,16,16,128]{3,2,1,0:T(8,128)(2,1)}, u32[]{:S(2)}) copy-start(bf16[24,16,16,128]{3,2,1,0:T(8,128)(2,1)} %field_ref.3) | copy-start | bytes 4718596
  30.2 19.5 %copy-start.5 = (f32[16,16,128]{2,1,0:T(8,128)S(1)}, f32[16,16,128]{2,1,0:T(8,128)}, u32[]{:S(2)}) copy-start(f32[16,16,128]{2,1,0:T(8,128)} %pot_ref.3) | copy-start | bytes 393220
  30.2 4.3 %collective-permute-start.5 = (bf16[16,16,128]{2,1,0:T(8,128)(2,1)S(1)}, bf16[16,16,128]{2,1,0:T(8,128)(2,1)S(1)}, u32[]{:S(2)}, u32[]{:S(2)}) collective-permute-start(bf16[16,16,128]{2,1,0:T(8,128)(2,1)S(1)} %get-tuple-element.21.pair_ref), channel_id=1, source_target_pairs={{0,16},{8,24},{16,0},{24,8},{1,17},{9,25},{17,1},{25,9},{2,18},{10... | collective-permute-start | bytes 196616 | tf_op jit(solution)/shard_map/ppermute | solution.py:410
  34.7 19.5 %collective-permute-start.6 = (f32[72,128]{1,0:T(8,128)S(1)}, f32[72,128]{1,0:T(8,128)S(1)}, u32[]{:S(2)}, u32[]{:S(2)}) collective-permute-start(f32[72,128]{1,0:T(8,128)S(1)} %get-tuple-element.26), channel_id=1, source_target_pairs={{0,1},{1,2},{2,3},{3,4},{4,5},{5,6},{6,7},{7,0},{8,9},{9,10},{10,1... | collective-permute-start | bytes 110600 | tf_op jit(solution)/shard_map/ppermute | solution.py:406
  37.7 23.6 %collective-permute-start.7 = (f32[72,128]{1,0:T(8,128)S(1)}, f32[72,128]{1,0:T(8,128)S(1)}, u32[]{:S(2)}, u32[]{:S(2)}) collective-permute-start(f32[72,128]{1,0:T(8,128)S(1)} %get-tuple-element.25.message_ref), channel_id=1, source_target_pairs={{0,7},{1,0},{2,1},{3,2},{4,3},{5,4},{6,5},{7,6},{8,15},{9,8},{10,9... | collective-permute-start | bytes 110600 | tf_op jit(solution)/shard_map/ppermute | solution.py:406
  42.4 3.6 %collective-permute-start.8 = (f32[8,128]{1,0:T(8,128)S(1)}, f32[8,128]{1,0:T(8,128)S(1)}, u32[]{:S(2)}, u32[]{:S(2)}) collective-permute-start(f32[8,128]{1,0:T(8,128)S(1)} %get-tuple-element.31.one_ref), channel_id=1, source_target_pairs={{0,1},{1,0},{2,3},{3,2},{4,5},{5,4},{6,7},{7,6},{8,9},{9,8},{10,11... | collective-permute-start | bytes 12296 | tf_op jit(solution)/shard_map/ppermute | solution.py:410
  46.1 3.6 %collective-permute-start.9 = (f32[8,128]{1,0:T(8,128)S(1)}, f32[8,128]{1,0:T(8,128)S(1)}, u32[]{:S(2)}, u32[]{:S(2)}) collective-permute-start(f32[8,128]{1,0:T(8,128)S(1)} %shard_map.103.one_ref), channel_id=1, source_target_pairs={{0,2},{1,3},{2,0},{3,1},{4,6},{5,7},{6,4},{7,5},{8,10},{9,11},{10,... | collective-permute-start | bytes 12296 | tf_op jit(solution)/shard_map/ppermute | solution.py:410
  49.7 4.5 %collective-permute-start.10 = (f32[8,128]{1,0:T(8,128)S(1)}, f32[8,128]{1,0:T(8,128)S(1)}, u32[]{:S(2)}, u32[]{:S(2)}) collective-permute-start(f32[8,128]{1,0:T(8,128)S(1)} %shard_map.104.one_ref), channel_id=1, source_target_pairs={{0,4},{1,5},{2,6},{3,7},{4,0},{5,1},{6,2},{7,3},{8,12},{9,13},{10,... | collective-permute-start | bytes 12296 | tf_op jit(solution)/shard_map/ppermute | solution.py:410
  54.2 7.1 %copy-start.6 = (f32[16,16,128]{2,1,0:T(8,128)S(1)}, f32[16,16,128]{2,1,0:T(8,128)}, u32[]{:S(2)}) copy-start(f32[16,16,128]{2,1,0:T(8,128)} %ionic_ref.1) | copy-start | bytes 393220

commit v4 on v3

--- a/solution.py
+++ b/solution.py
@@ -146,7 +146,7 @@
 
 def own_kernel(
     starts, turned_ref, proj_ref, coupling_ref, partial_ref, partner_ref,
-    part_ref, shifted_ref, wide_coupling_ref, pair_ref, rows_ref, boxed_ref,
+    part_ref, shifted_ref, wide_coupling_ref, pair_ref, masks_ref, rows_ref, boxed_ref,
 ):
     atoms, nproj = proj_ref.shape[:2]
     pair_ref[...] = (partial_ref[...] + partner_ref[...]).astype(pair_ref.dtype)
@@ -159,6 +159,7 @@
         part_ref[:, a * SLOT : (a + 1) * SLOT] = gather_atom(
             turned_ref, shifted_ref, a, offset, column, 0, boxed_ref.at[a % 2]
         )
+    lane_masks([start_of(starts, a, atoms, planes, False) for a in range(atoms)], masks_ref)
     slots = atoms * SLOT
     spread = (
         lax.broadcasted_iota(jnp.int32, (nproj, slots), 0)
@@ -174,26 +175,41 @@
     wide_coupling_ref[...] = jnp.where(same, both, 0.0)
 
 
-def carried_kernel(
-    starts, turned_ref, mine_ref, other_ref, hart_ref, dens_ref,
+def carried_half(first, starts, turned_ref, proj_ref, out_ref, shifted_ref, rows_ref, boxed_ref):
+    half = proj_ref.shape[0]
+    planes, count, _ = turned_ref.shape
+    core = lax.rem(lax.axis_index("band"), 2)
+    block = core if first else 1 - core
+    base = 0 if first else half
+    for q in range(half):
+        offset, column = start_of(starts, block * half + q, 2 * half, planes, True)
+        shift_projectors(proj_ref, q, q, column, rows_ref.at[q % 2], shifted_ref)
+    for q in range(half):
+        offset, column = start_of(starts, block * half + q, 2 * half, planes, True)
+        out_ref[:count, (base + q) * SLOT : (base + q + 1) * SLOT] = gather_atom(
+            turned_ref, shifted_ref, q, offset, column, planes, boxed_ref.at[q % 2]
+        )
+
+
+def by_slot(table):
+    core = lax.rem(lax.axis_index("band"), 2)
+    return jnp.where(core == 1, pltpu.roll(table, table.shape[1] // 2, 1), table)
+
+
+def first_kernel(starts, turned_ref, mine_ref, part_ref, shifted_ref, rows_ref, boxed_ref):
+    part_ref[...] = jnp.zeros(part_ref.shape, f32)
+    carried_half(True, starts, turned_ref, mine_ref, part_ref, shifted_ref, rows_ref, boxed_ref)
+
+
+def second_kernel(
+    starts, turned_ref, other_ref, half_ref, hart_ref, dens_ref,
     message_ref, shifted_ref, rows_ref, boxed_ref,
 ):
-    half = mine_ref.shape[0]
-    planes, count, _ = turned_ref.shape
+    count = half_ref.shape[0]
     rows = hart_ref.shape[1]
-    core = lax.rem(lax.axis_index("band"), 2)
-    for q in range(half):
-        a = core * half + q
-        offset, column = start_of(starts, a, 2 * half, planes, True)
-        shift_projectors(mine_ref, q, a, column, rows_ref.at[0], shifted_ref)
-        a = (1 - core) * half + q
-        offset, column = start_of(starts, a, 2 * half, planes, True)
-        shift_projectors(other_ref, q, a, column, rows_ref.at[1], shifted_ref)
-    for a in range(2 * half):
-        offset, column = start_of(starts, a, 2 * half, planes, True)
-        message_ref[:count, a * SLOT : (a + 1) * SLOT] = gather_atom(
-            turned_ref, shifted_ref, a, offset, column, planes, boxed_ref.at[a % 2]
-        )
+    message_ref[:count] = half_ref[...]
+    carried_half(False, starts, turned_ref, other_ref, message_ref, shifted_ref, rows_ref, boxed_ref)
+    message_ref[:count] = by_slot(message_ref[:count])
     message_ref[count : count + 2 * rows] = hart_ref[:2].reshape(2 * rows, LANES)
     message_ref[count + 2 * rows :] = dens_ref[0]
 
@@ -205,33 +221,32 @@
     ).astype(bf16)
 
 
-def lane_masks(starts, planes, carried, masks_ref):
-    atoms, per_tile = masks_ref.shape[:2]
-    for a in range(atoms):
-        group = lane_group(start_of(starts, a, atoms, planes, carried)[1], SLOT)
-        for r in range(per_tile):
-            masks_ref[a, r] = jnp.where(group == r, 1.0, 0.0).astype(bf16)
-
-
-def deposit_plane(starts, shifted_ref, masks_ref, weighted, plane, planes, carried, wide_ref):
-    atoms, per_tile = masks_ref.shape[:2]
+def lane_masks(spots, masks_ref):
+    for slot, (_, column) in enumerate(spots):
+        group = lane_group(column, SLOT)
+        for r in range(masks_ref.shape[1]):
+            masks_ref[slot, r] = jnp.where(group == r, 1.0, 0.0).astype(bf16)
+
+
+def deposit_plane(spots, tables, masks, weighted, plane, wide_ref):
+    per_tile = masks[0][0].shape[1]
     count = weighted.shape[0]
     box = SLOT
-    tiles = shifted_ref.shape[2] // ((box + 1) * LANES)
+    tiles = tables[0][0].shape[2] // ((box + 1) * LANES)
     rows = tiles * per_tile
     places = []
-    for a in range(atoms):
-        j = plane - start_of(starts, a, atoms, planes, carried)[0]
-        if carried:
-            j = j + planes
+    for first, _ in spots:
+        j = plane - first
         places.append(jnp.where(jnp.logical_and(j >= 0, j < box), j, box) * (tiles * LANES))
     for t in range(tiles):
         cells = [
-            shifted_ref[a, :, pl.ds(pl.multiple_of(places[a] + t * LANES, LANES), LANES)]
-            for a in range(atoms)
+            table[index, :, pl.ds(pl.multiple_of(place + t * LANES, LANES), LANES)]
+            for (table, index), place in zip(tables, places)
         ]
         for r in range(per_tile):
-            placed = jnp.concatenate([cells[a] * masks_ref[a, r] for a in range(atoms)], axis=0)
+            placed = jnp.concatenate(
+                [cell * ref[slot, r] for cell, (ref, slot) in zip(cells, masks)], axis=0
+            )
             update = jnp.dot(weighted, placed, preferred_element_type=f32)
             row = t * per_tile + r
             wide_ref[pl.ds(row, count, stride=rows + 1), :] = pltpu.roll(
@@ -259,14 +274,32 @@
     return (potential + 3.75) * c - (2.0 / 3.0) * near + (1.0 / 24.0) * far
 
 
-def inner_kernel(field_ref, pot_ref, acc_ref, padded_ref):
+def carried_spots(starts, atoms, planes):
+    core = lax.rem(lax.axis_index("band"), 2)
+    half = atoms // 2
+    spots = []
+    for block in (core, 1 - core):
+        for q in range(half):
+            offset, column = start_of(starts, block * half + q, atoms, planes, True)
+            spots.append((offset - planes, column))
+    return spots
+
+
+def stencil_kernel(
+    starts, field_ref, low_ref, high_ref, pot_ref, acc_ref, masks_ref, padded_ref
+):
     count, planes, _, _ = field_ref.shape
+    lane_masks(carried_spots(starts, masks_ref.shape[0], planes), masks_ref)
 
     def one(o, _):
-        cells = [field_ref[o, i].astype(f32) for i in range(planes)]
-        for i in range(2, planes - 2):
-            pad_rows(padded_ref, i, cells[i])
-            acc_ref[o, i] = stencil_plane(padded_ref, i, *cells[i - 2 : i + 3], pot_ref[i])
+        cells = (
+            [low_ref[o, i].astype(f32) for i in range(2)]
+            + [field_ref[o, i].astype(f32) for i in range(planes)]
+            + [high_ref[o, i].astype(f32) for i in range(2)]
+        )
+        for i in range(planes):
+            pad_rows(padded_ref, i, cells[i + 2])
+            acc_ref[o, i] = stencil_plane(padded_ref, i, *cells[i : i + 5], pot_ref[i])
         return 0
 
     lax.fori_loop(0, count, one, 0)
@@ -282,7 +315,9 @@
     out_ref[...] = pot_ref[...] - shift[None]
 
 
-def join_kernel(pair_ref, partner_ref, part_ref, hart_ref, density_ref, charge_ref, message_ref):
+def join_kernel(
+    pair_ref, partner_ref, part_ref, hart_ref, density_ref, charge_ref, message_ref
+):
     planes, rows, _ = density_ref.shape
     count = part_ref.shape[0]
     density = pair_ref[...].astype(f32) + partner_ref[...].astype(f32)
@@ -293,74 +328,27 @@
     message_ref[count + 2 * rows :] = density[planes - 1]
 
 
-def local_kernel(
-    starts, inner_ref, field_ref, low_ref, high_ref, shifted_ref, message_ref, below_ref,
-    coupling_ref, pot_ref, acc_ref, masks_ref, wide_ref, padded_ref,
-):
-    count, planes, rows, _ = field_ref.shape
-    lane_masks(starts, planes, True, masks_ref)
-    weighted = weigh(message_ref[:count] + below_ref[:count], coupling_ref)
-
-    def one(o, _):
-        cells = {i: field_ref[o, i].astype(f32) for i in (0, 1, 2, 3)}
-        cells.update({i: field_ref[o, i].astype(f32) for i in range(planes - 4, planes)})
-        for i in range(2):
-            cells[i - 2] = low_ref[o, i].astype(f32)
-            cells[planes + i] = high_ref[o, i].astype(f32)
-        for k, i in enumerate((0, 1, planes - 2, planes - 1)):
-            pad_rows(padded_ref, k, cells[i])
-            acc_ref[o, i] = stencil_plane(
-                padded_ref, k, *[cells[i + d] for d in range(-2, 3)], pot_ref[i]
-            )
-        return 0
-
-    lax.fori_loop(0, count, one, 0)
-
-    def two(pair, _):
-        for half in range(2):
-            plane = 2 * pair + half
-            deposit_plane(
-                starts, shifted_ref, masks_ref, weighted, plane, planes, True, wide_ref.at[half]
-            )
-            for o in range(count):
-                low = o * (rows + 1)
-                acc_ref[o, plane] += wide_ref[half, low : low + rows, :]
-        return 0
-
-    lax.fori_loop(0, planes // 2, two, 0)
-
-
 def final_kernel(
-    starts, acc_ref, shifted_ref, part_ref, above_ref, coupling_ref,
-    dens_ref, hart_ref, ionic_ref, below_ref,
-    out_ref, pot_ref, masks_ref, wide_ref, done_ref, sems,
+    starts, acc_ref, own_ref, mine_ref, other_ref, own_masks, prev_masks,
+    part_ref, above_ref, message_ref, below_ref,
+    coupling_ref, dens_ref, hart_ref, ionic_ref,
+    out_ref, pot_ref, wide_ref, done_ref, sems,
 ):
     count, planes, rows, _ = done_ref.shape
-    lane_masks(starts, planes, False, masks_ref)
-    weighted = weigh(part_ref[...] + above_ref[:count], coupling_ref)
-    groups = sems.shape[0]
-    size = planes // groups
-    copies = []
-    for group in range(groups):
-        def two(pair, _):
-            for half in range(2):
-                plane = group * size + 2 * pair + half
-                deposit_plane(
-                    starts, shifted_ref, masks_ref, weighted, plane, planes, False, wide_ref.at[half]
-                )
-                for o in range(count):
-                    low = o * (rows + 1)
-                    done_ref[o, plane] = (
-                        acc_ref[o, plane] + wide_ref[half, low : low + rows, :]
-                    ).astype(bf16)
-            return 0
-
-        lax.fori_loop(0, size // 2, two, 0)
-        part = pl.ds(group * size, size)
-        copies.append(
-            pltpu.make_async_copy(done_ref.at[:, part], out_ref.at[:, part], sems.at[group])
-        )
-        copies[-1].start()
+    atoms = own_ref.shape[0]
+    half = atoms // 2
+    spots = [start_of(starts, a, atoms, planes, False) for a in range(atoms)]
+    spots = spots + carried_spots(starts, atoms, planes)
+    tables = [(own_ref, a) for a in range(atoms)]
+    tables = tables + [(table, q) for table in (mine_ref, other_ref) for q in range(half)]
+    masks = [(ref, a) for ref in (own_masks, prev_masks) for a in range(atoms)]
+    weighted = jnp.concatenate(
+        [
+            weigh(part_ref[...] + above_ref[:count], coupling_ref),
+            weigh(by_slot(message_ref[:count] + below_ref[:count]), coupling_ref),
+        ],
+        axis=1,
+    )
 
     field = jnp.concatenate(
         [
@@ -397,6 +385,28 @@
     root = (2.0 * root + third / jnp.maximum(root * root, 1e-30)) * (1.0 / 3.0)
     root = jnp.where(third > 0.0, root, 0.0)
     pot_ref[...] = ionic_ref[...] + twice - root
+    copies = []
+    sizes = [planes // 8 * k for k in (3, 3, 1, 1)]
+    base = 0
+    for group, size in enumerate(sizes):
+        def two(pair, _, base=base):
+            for turn in range(2):
+                plane = base + 2 * pair + turn
+                deposit_plane(spots, tables, masks, weighted, plane, wide_ref.at[turn])
+                for o in range(count):
+                    low = o * (rows + 1)
+                    done_ref[o, plane] = (
+                        acc_ref[o, plane] + wide_ref[turn, low : low + rows, :]
+                    ).astype(bf16)
+            return 0
+
+        lax.fori_loop(0, size // 2, two, 0)
+        part = pl.ds(base, size)
+        copies.append(
+            pltpu.make_async_copy(done_ref.at[:, part], out_ref.at[:, part], sems.at[group])
+        )
+        copies[-1].start()
+        base += size
     for copy in copies:
         copy.wait()
 
@@ -438,6 +448,7 @@
 
     groups = 4
     stride = rows + 1
+    edge_shape = jax.ShapeDtypeStruct((count, 2, rows, lanes), bf16)
     partial, turned, first, last = call(
         prepare_kernel, 2,
         in_specs=[smem(), high_hbm()],
@@ -445,8 +456,8 @@
         out_shape=(
             jax.ShapeDtypeStruct((planes, rows, lanes), f32),
             jax.ShapeDtypeStruct((planes, count, rows * lanes), bf16),
-            jax.ShapeDtypeStruct((count, 2, rows, lanes), bf16),
-            jax.ShapeDtypeStruct((count, 2, rows, lanes), bf16),
+            edge_shape,
+            edge_shape,
         ),
         scratch_shapes=[
             pltpu.VMEM((count, planes, rows, lanes), bf16),
@@ -454,41 +465,33 @@
             pltpu.SemaphoreType.DMA((groups,)),
         ],
     )(occupations, orbitals)
-    low = around(last, "space", 1)
-    high = around(first, "space", -1)
 
     shifted_shape = jax.ShapeDtypeStruct((atoms, SLOT, (box + 1) * square), bf16)
     gather_scratch = [
         pltpu.VMEM((2, square // lanes, SLOT * (box + 1), lanes), f32),
         pltpu.VMEM((2, count, box * square), bf16),
     ]
-    own_part, own_shifted, wide_coupling, pair = call(
+    mask_shape = jax.ShapeDtypeStruct((atoms, lanes // SLOT, SLOT, lanes), bf16)
+    own_part, own_shifted, wide_coupling, pair, own_masks = call(
         own_kernel, 4,
         in_specs=[smem()] + [vmem()] * 5,
-        out_specs=(vmem(),) * 4,
+        out_specs=(vmem(),) * 5,
         out_shape=(
             jax.ShapeDtypeStruct((count, slots), f32),
             shifted_shape,
             jax.ShapeDtypeStruct((slots, slots), f32),
             jax.ShapeDtypeStruct((planes, rows, lanes), bf16),
+            mask_shape,
         ),
         scratch_shapes=gather_scratch,
     )(box_start, turned, projectors, coupling, partial, swap(partial, "band", 1))
-
-    inner = call(
-        inner_kernel, 3,
-        in_specs=[vmem(), vmem()],
-        out_specs=vmem(),
-        out_shape=jax.ShapeDtypeStruct((count, planes, rows, lanes), f32),
-        scratch_shapes=[pltpu.VMEM((planes * (rows + 8), lanes), f32)],
-    )(orbitals, potential_in)
 
     mask = 2
     while 2 * mask < n_band:
         pair = (pair.astype(f32) + swap(pair, "band", mask).astype(f32)).astype(bf16)
         mask *= 2
     message_shape = jax.ShapeDtypeStruct((count + 3 * rows, lanes), f32)
-    density, charge, message = call(
+    density, charge, below = call(
         join_kernel, 1,
         in_specs=[vmem()] * 4,
         out_specs=(vmem(),) * 3,
@@ -498,7 +501,9 @@
             message_shape,
         ),
     )(pair, swap(pair, "band", mask), own_part, hartree_prev)
-    below = around(message, "space", 1)
+    below = around(below, "space", 1)
+    low = around(last, "space", 1)
+    high = around(first, "space", -1)
     mask = 1
     while mask < n_space:
         charge = call(
@@ -509,48 +514,48 @@
         )(charge, swap(charge, "space", mask))
         mask *= 2
 
-    message, prev_shifted = call(
-        carried_kernel, 4,
+    half_shape = jax.ShapeDtypeStruct((half, SLOT, (box + 1) * square), bf16)
+    prev_half, mine_shifted = call(
+        first_kernel, 2,
+        in_specs=[smem()] + [vmem()] * 2,
+        out_specs=(vmem(), vmem()),
+        out_shape=(jax.ShapeDtypeStruct((count, slots), f32), half_shape),
+        scratch_shapes=gather_scratch,
+    )(box_start, turned, mine)
+    message, other_shifted = call(
+        second_kernel, 2,
         in_specs=[smem()] + [vmem()] * 5,
         out_specs=(vmem(), vmem()),
-        out_shape=(message_shape, shifted_shape),
+        out_shape=(message_shape, half_shape),
         scratch_shapes=gather_scratch,
-    )(box_start, turned, mine, other, hartree_prev, density)
+    )(box_start, turned, other, prev_half, hartree_prev, density)
 
     above = around(message, "space", -1)
 
-    deposit_scratch = [
-        pltpu.VMEM((atoms, lanes // SLOT, SLOT, lanes), bf16),
-        pltpu.VMEM((2, count * stride, lanes), f32),
-    ]
-    acc = call(
-        local_kernel, 4,
-        in_specs=[smem()] + [vmem()] * 9,
-        out_specs=vmem(),
-        out_shape=jax.ShapeDtypeStruct((count, planes, rows, lanes), f32),
-        scratch_shapes=deposit_scratch + [pltpu.VMEM((4 * (rows + 8), lanes), f32)],
-        input_output_aliases={1: 0},
-    )(
-        box_start, inner, orbitals, low, high, prev_shifted, message, below, wide_coupling,
-        potential_in,
-    )
+    acc, prev_masks = call(
+        stencil_kernel, 4,
+        in_specs=[smem()] + [vmem()] * 4,
+        out_specs=(vmem(), vmem()),
+        out_shape=(jax.ShapeDtypeStruct((count, planes, rows, lanes), f32), mask_shape),
+        scratch_shapes=[pltpu.VMEM((planes * (rows + 8), lanes), f32)],
+    )(box_start, orbitals, low, high, potential_in)
 
     applied, potential = call(
-        final_kernel, 4,
-        in_specs=[smem()] + [vmem()] * 9,
+        final_kernel, 6,
+        in_specs=[smem()] + [vmem()] * 14,
         out_specs=(hbm(), vmem()),
         out_shape=(
             jax.ShapeDtypeStruct((count, planes, rows, lanes), bf16),
             jax.ShapeDtypeStruct((planes, rows, lanes), f32),
         ),
-        scratch_shapes=deposit_scratch
-        + [
+        scratch_shapes=[
+            pltpu.VMEM((2, count * stride, lanes), f32),
             pltpu.VMEM((count, planes, rows, lanes), bf16),
-            pltpu.SemaphoreType.DMA((4,)),
+            pltpu.SemaphoreType.DMA((groups,)),
         ],
     )(
-        box_start, acc, own_shifted, own_part, above, wide_coupling,
-        density, hartree_prev, ionic_potential, below,
+        box_start, acc, own_shifted, mine_shifted, other_shifted, own_masks, prev_masks, own_part, above, message, below,
+        wide_coupling, density, hartree_prev, ionic_potential,
     )
     potential = call(
         functools.partial(shift_kernel, float(cells * n_space)), 1,

time: 68 us -> 62.2 us (0.915)
  Pallas kernels: 24.8 us -> 20 us
  waiting for transfers between devices: 24.3 us -> 23.2 us
    pallas_call x4, Pallas kernels: 18.9 us -> 14.1 us  [the longest x1 6.31 us: local(): call(final_kernel, 6, in_specs=[smem()] + [vmem()] * 14, out_specs=(hbm()...]
    ppermute x6, waiting for transfers between devices: 11.4 us -> 10.4 us  [swap(): lax.ppermute(block, axis, [(i, i ^ mask) for i in range(lax.axis_size(axi...]
  transfers between devices with their start and end apart: 11 -> 11, of which waited for: 5 -> 5; matrix products, arithmetic and copies ran while one was open for 0% -> 0% of each run, Pallas kernels for 27% -> 21%
where the time goes in v4:
time: 62.2 us; the launch traced here: 62 us
  waiting for transfers between devices  23.2 us (37%)
  Pallas kernels  20 us (32%)
  starting transfers between devices  14.7 us (24%)
  local copies, waits for them, and re-layouts  3.26 us (5%)
  between operations  0.78 us (1%)
    ppermute x5, waiting for transfers between devices, around(): lax.ppermute(block, axis, [(i, (i + distance) % count) for i in range(cou...  12.9 us
    ppermute x5, starting transfers between devices, around(): lax.ppermute(block, axis, [(i, (i + distance) % count) for i in range(cou...  12.6 us
    ppermute x6, waiting for transfers between devices, swap(): lax.ppermute(block, axis, [(i, i ^ mask) for i in range(lax.axis_size(axi...  10.4 us
    pallas_call x1, Pallas kernels, local(): call(final_kernel, 6, in_specs=[smem()] + [vmem()] * 14, out_specs=(hbm()...  6.31 us
    pallas_call x1, Pallas kernels, local(): call(stencil_kernel, 4, in_specs=[smem()] + [vmem()] * 4, out_specs=(vmem...  4.07 us
    unnamed x20, local copies, waits for them, and re-layouts  3.26 us
    pallas_call x1, Pallas kernels, local(): call(own_kernel, 4, in_specs=[smem()] + [vmem()] * 5, out_specs=(vmem(),)...  3.07 us
    ppermute x6, starting transfers between devices, swap(): lax.ppermute(block, axis, [(i, i ^ mask) for i in range(lax.axis_size(axi...  2.13 us
  transfers between devices with their start and end apart: 11, of which 5 were waited for; matrix products, arithmetic and copies ran while one was open for 0% of the time, Pallas kernels for 21%

profile of v4, /device:TPU:0, one launch (start us, length us, event | category | flops | bytes accessed | tf_op | source)
XLA Modules:
  0.0 62.0 jit_solution(7378466120137594363)
XLA Ops:
  0.6 1.1 %copy-done.2 = bf16[8,13,16,256]{3,2,1,0:T(8,128)(2,1)S(1)} copy-done((bf16[8,13,16,256]{3,2,1,0:T(8,128)(2,1)S(1)}, bf16[8,13,16,256]{3,2,1,0:T(8,128)(2,1)}, u32[]{:S(2)}) %copy-start.2) | copy-done | bytes 851992
  1.8 0.2 shard_map.98
  2.0 3.0 %collective-permute-start.3 = (bf16[4,13,16,256]{3,2,1,0:T(8,128)(2,1)S(1)}, bf16[4,13,16,256]{3,2,1,0:T(8,128)(2,1)S(1)}, u32[]{:S(2)}, u32[]{:S(2)}) collective-permute-start(bf16[4,13,16,256]{3,2,1,0:T(8,128)(2,1)S(1)} %shard_map.98), channel_id=1, source_target_pairs={{0,1},{1,2},{2,3},{3,4},{4,5},{5,6},{6,7},{7,0},{8,9},{9,10},{10,1... | collective-permute-start | bytes 1277960 | tf_op jit(solution)/shard_map/ppermute | solution.py:416
  5.1 12.9 %collective-permute-done.3.mine_ref = bf16[4,13,16,256]{3,2,1,0:T(8,128)(2,1)S(1)} collective-permute-done((bf16[4,13,16,256]{3,2,1,0:T(8,128)(2,1)S(1)}, bf16[4,13,16,256]{3,2,1,0:T(8,128)(2,1)S(1)}, u32[]{:S(2)}, u32[]{:S(2)}) %collective-permute-start.3) | collective-permute-done | bytes 426016 | tf_op jit(solution)/shard_map/ppermute | solution.py:416
  17.9 1.4 %copy-done = bf16[24,16,16,128]{3,2,1,0:T(8,128)(2,1)S(1)} copy-done((bf16[24,16,16,128]{3,2,1,0:T(8,128)(2,1)S(1)}, bf16[24,16,16,128]{3,2,1,0:T(8,128)(2,1)}, u32[]{:S(2)}) %copy-start) | copy-done | bytes 1572888
  19.4 0.7 %copy-done.9 = f32[24]{0:T(128)S(1)} copy-done((f32[24]{0:T(128)S(1)}, f32[24]{0:T(128)}, u32[]{:S(2)}) %copy-start.9) | copy-done | bytes 120
  20.0 1.7 %shard_map.95 = (f32[16,16,128]{2,1,0:T(8,128)S(1)}, bf16[16,24,2048]{2,1,0:T(8,128)(2,1)S(1)}, bf16[24,2,16,128]{3,2,1,0:T(8,128)(2,1)S(1)}, bf16[24,2,16,128]{3,2,1,0:T(8,128)(2,1)S(1)}) custom-call(f32[24]{0:T(128)S(1)} %copy-done.9, bf16[24,16,16,128]{3,2,1,0:T(8,128)(2,1)S(1)} %copy-done), custom_call_target="tpu_custom_call" | custom-call | flops 1000000 | bytes 2000000 | tf_op jit(solution)/shard_map/pallas_call | solution.py:452
  21.8 0.6 collective-permute-start.2
  22.3 4.7 %collective-permute-start.1 = (bf16[24,2,16,128]{3,2,1,0:T(8,128)(2,1)S(1)}, bf16[24,2,16,128]{3,2,1,0:T(8,128)(2,1)S(1)}, u32[]{:S(2)}, u32[]{:S(2)}) collective-permute-start(bf16[24,2,16,128]{3,2,1,0:T(8,128)(2,1)S(1)} %get-tuple-element.23), channel_id=1, source_target_pairs={{0,7},{1,0},{2,1},{3,2},{4,3},{5,4},{6,5},{7,6},{8,15},{9,8},{10,9... | collective-permute-start | bytes 589832 | tf_op jit(solution)/shard_map/ppermute | solution.py:416
  27.1 3.1 %shard_map.97 = (f32[24,128]{1,0:T(8,128)S(1)}, bf16[8,16,4352]{2,1,0:T(8,128)(2,1)S(1)}, f32[128,128]{1,0:T(8,128)S(1)}, bf16[16,16,128]{2,1,0:T(8,128)(2,1)S(1)}, bf16[8,8,16,128]{3,2,1,0:T(8,128)(2,1)S(1)}) custom-call(s32[3,64]{1,0:T(4,128)S(1)} %copy-done.7, bf16[16,24,2048]{2,1,0:T(8,128)(2,1)S(1)} %get-tuple-element.25.turned_ref, ...), custom_call_target="tpu_custom_call" | custom-call | flops 2000000 | bytes 4000000 | tf_op jit(solution)/shard_map/pallas_call | solution.py:475
  30.2 1.6 %collective-permute-start.5 = (bf16[16,16,128]{2,1,0:T(8,128)(2,1)S(1)}, bf16[16,16,128]{2,1,0:T(8,128)(2,1)S(1)}, u32[]{:S(2)}, u32[]{:S(2)}) collective-permute-start(bf16[16,16,128]{2,1,0:T(8,128)(2,1)S(1)} %get-tuple-element.30.pair_ref), channel_id=1, source_target_pairs={{0,16},{8,24},{16,0},{24,8},{1,17},{9,25},{17,1},{25,9},{2,18},{10... | collective-permute-start | bytes 196616 | tf_op jit(solution)/shard_map/ppermute | solution.py:420
  31.7 2.8 %collective-permute-done.5.partner_ref = bf16[16,16,128]{2,1,0:T(8,128)(2,1)S(1)} collective-permute-done((bf16[16,16,128]{2,1,0:T(8,128)(2,1)S(1)}, bf16[16,16,128]{2,1,0:T(8,128)(2,1)S(1)}, u32[]{:S(2)}, u32[]{:S(2)}) %collective-permute-start.5) | collective-permute-done | bytes 65568 | tf_op jit(solution)/shard_map/ppermute | solution.py:420
  34.5 0.2 shard_map.100
  34.7 0.1 collective-permute-start.7
  34.7 1.8 %shard_map.99 = (f32[24,128]{1,0:T(8,128)S(1)}, bf16[4,16,4352]{2,1,0:T(8,128)(2,1)S(1)}) custom-call(s32[3,64]{1,0:T(4,128)S(1)} %copy-done.7, bf16[16,24,2048]{2,1,0:T(8,128)(2,1)S(1)} %get-tuple-element.25.turned_ref, bf16[4,13,16,256]{3,2,1,0:T(8,128)(2,1)S(1)} %collective-permute-done.3.mine_ref), custom_call_target="tpu_custom_call" | custom-call | flops 1000000 | bytes 2000000 | tf_op jit(solution)/shard_map/pallas_call | solution.py:518
  36.6 0.0 copy-start.5
  36.6 1.9 %shard_map.101 = (f32[72,128]{1,0:T(8,128)S(1)}, bf16[4,16,4352]{2,1,0:T(8,128)(2,1)S(1)}) custom-call(s32[3,64]{1,0:T(4,128)S(1)} %copy-done.7, bf16[16,24,2048]{2,1,0:T(8,128)(2,1)S(1)} %get-tuple-element.25.turned_ref, bf16[4,13,16,256]{3,2,1,0:T(8,128)(2,1)S(1)} %collective-permute-done.4.other_ref, f32[24,128]{1,0:T(8,128)S(1)} %get-tuple-element.29.half_ref, ...), custom_call_target="tpu_custom_call" | custom-call | flops 1000000 | bytes 2000000 | tf_op jit(solution)/shard_map/pallas_call | solution.py:525
  38.5 4.7 %collective-permute-start.6 = (f32[72,128]{1,0:T(8,128)S(1)}, f32[72,128]{1,0:T(8,128)S(1)}, u32[]{:S(2)}, u32[]{:S(2)}) collective-permute-start(f32[72,128]{1,0:T(8,128)S(1)} %get-tuple-element.36.message_ref), channel_id=1, source_target_pairs={{0,7},{1,0},{2,1},{3,2},{4,3},{5,4},{6,5},{7,6},{8,15},{9,8},{10,9... | collective-permute-start | bytes 110600 | tf_op jit(solution)/shard_map/ppermute | solution.py:416
  43.2 3.6 %collective-permute-done.8.other_ref = f32[8,128]{1,0:T(8,128)S(1)} collective-permute-done((f32[8,128]{1,0:T(8,128)S(1)}, f32[8,128]{1,0:T(8,128)S(1)}, u32[]{:S(2)}, u32[]{:S(2)}) %collective-permute-start.8) | collective-permute-done | bytes 4128 | tf_op jit(solution)/shard_map/ppermute | solution.py:420
  46.9 3.6 %collective-permute-done.9.other_ref = f32[8,128]{1,0:T(8,128)S(1)} collective-permute-done((f32[8,128]{1,0:T(8,128)S(1)}, f32[8,128]{1,0:T(8,128)S(1)}, u32[]{:S(2)}, u32[]{:S(2)}) %collective-permute-start.9) | collective-permute-done | bytes 4128 | tf_op jit(solution)/shard_map/ppermute | solution.py:420
  50.5 4.1 %shard_map.96 = (f32[24,16,16,128]{3,2,1,0:T(8,128)S(1)}, bf16[8,8,16,128]{3,2,1,0:T(8,128)(2,1)S(1)}) custom-call(s32[3,64]{1,0:T(4,128)S(1)} %copy-done.7, bf16[24,16,16,128]{3,2,1,0:T(8,128)(2,1)S(1)} %copy-done.1, bf16[24,2,16,128]{3,2,1,0:T(8,128)(2,1)S(1)} %collective-permute-done.low_ref, ...), custom_call_target="tpu_custom_call" | custom-call | flops 2000000 | bytes 4000000 | tf_op jit(solution)/shard_map/pallas_call | solution.py:535
  54.6 0.4 collective-permute-done.10.other_ref
  55.0 6.3 %shard_map.102 = (bf16[24,16,16,128]{3,2,1,0:T(8,128)(2,1)}, f32[16,16,128]{2,1,0:T(8,128)S(1)}) custom-call(s32[3,64]{1,0:T(4,128)S(1)} %copy-done.7, f32[24,16,16,128]{3,2,1,0:T(8,128)S(1)} %get-tuple-element.24.acc_ref, bf16[8,16,4352]{2,1,0:T(8,128)(2,1)S(1)} %get-tuple-element.27.own_ref, bf16[4,16,4352]{2,1,0:T(8,128)(2,1)S(1)} %get-tuple-element.28.mine_ref, ...), custom_call_target="tpu_custom_call" | custom-call | flops 3000000 | bytes 6000000 | tf_op jit(solution)/shard_map/pallas_call | solution.py:543
  61.3 0.7 %shard_map.106 = f32[16,16,128]{2,1,0:T(8,128)} custom-call(f32[16,16,128]{2,1,0:T(8,128)S(1)} %get-tuple-element.40.pot_ref, f32[8,128]{1,0:T(8,128)S(1)} %shard_map.105.charge_ref), custom_call_target="tpu_custom_call" | custom-call | flops 500000 | bytes 1000000 | tf_op jit(solution)/shard_map/pallas_call | solution.py:560
  (30 shorter events, 0.1 us)
Async XLA Ops:
  0.6 1.2 %copy-start.2 = (bf16[8,13,16,256]{3,2,1,0:T(8,128)(2,1)S(1)}, bf16[8,13,16,256]{3,2,1,0:T(8,128)(2,1)}, u32[]{:S(2)}) copy-start(bf16[8,13,16,256]{3,2,1,0:T(8,128)(2,1)} %proj_ref.3) | copy-start | bytes 2555908
  1.8 25.3 %copy-start.3 = (bf16[8,13,16,256]{3,2,1,0:T(8,128)(2,1)S(1)}, bf16[8,13,16,256]{3,2,1,0:T(8,128)(2,1)}, u32[]{:S(2)}) copy-start(bf16[8,13,16,256]{3,2,1,0:T(8,128)(2,1)} %proj_ref.3) | copy-start | bytes 2555908
  1.8 25.3 %copy-start.7 = (s32[3,64]{1,0:T(4,128)S(1)}, s32[3,64]{1,0:T(4,128)}, u32[]{:S(2)}) copy-start(s32[3,64]{1,0:T(4,128)} %starts.9) | copy-start | bytes 2308
  1.8 25.3 %copy-start.8 = (f32[13,13]{1,0:T(8,128)S(1)}, f32[13,13]{1,0:T(8,128)}, u32[]{:S(2)}) copy-start(f32[13,13]{1,0:T(8,128)} %coupling_ref.1) | copy-start | bytes 2032
  2.0 15.9 %collective-permute-start.3 = (bf16[4,13,16,256]{3,2,1,0:T(8,128)(2,1)S(1)}, bf16[4,13,16,256]{3,2,1,0:T(8,128)(2,1)S(1)}, u32[]{:S(2)}, u32[]{:S(2)}) collective-permute-start(bf16[4,13,16,256]{3,2,1,0:T(8,128)(2,1)S(1)} %shard_map.98), channel_id=1, source_target_pairs={{0,1},{1,2},{2,3},{3,4},{4,5},{5,6},{6,7},{7,0},{8,9},{9,10},{10,1... | collective-permute-start | bytes 1277960 | tf_op jit(solution)/shard_map/ppermute | solution.py:416
  17.9 18.7 %collective-permute-start.4 = (bf16[4,13,16,256]{3,2,1,0:T(8,128)(2,1)S(1)}, bf16[4,13,16,256]{3,2,1,0:T(8,128)(2,1)S(1)}, u32[]{:S(2)}, u32[]{:S(2)}) collective-permute-start(bf16[4,13,16,256]{3,2,1,0:T(8,128)(2,1)S(1)} %collective-permute-done.3.mine_ref), channel_id=1, source_target_pairs={{0,8},{8,0},{16,24},{24,16},{1,9},{9,1},{17,25},{25,17},{2,10},{10... | collective-permute-start | bytes 1277960 | tf_op jit(solution)/shard_map/ppermute | solution.py:420
  17.9 1.4 %copy-start = (bf16[24,16,16,128]{3,2,1,0:T(8,128)(2,1)S(1)}, bf16[24,16,16,128]{3,2,1,0:T(8,128)(2,1)}, u32[]{:S(2)}) copy-start(bf16[24,16,16,128]{3,2,1,0:T(8,128)(2,1)} %field_ref.1) | copy-start | bytes 4718596
  19.4 0.7 %copy-start.9 = (f32[24]{0:T(128)S(1)}, f32[24]{0:T(128)}, u32[]{:S(2)}) copy-start(f32[24]{0:T(128)} %occ.1) | copy-start | bytes 292
  21.7 12.7 %copy-start.4 = (f32[16,16,128]{2,1,0:T(8,128)S(1)}, f32[16,16,128]{2,1,0:T(8,128)}, u32[]{:S(2)}) copy-start(f32[16,16,128]{2,1,0:T(8,128)} %hart_ref.5) | copy-start | bytes 393220
  21.8 5.3 %collective-permute-start.2 = (f32[16,16,128]{2,1,0:T(8,128)S(1)}, f32[16,16,128]{2,1,0:T(8,128)S(1)}, u32[]{:S(2)}, u32[]{:S(2)}) collective-permute-start(f32[16,16,128]{2,1,0:T(8,128)S(1)} %get-tuple-element.26.partial_ref), channel_id=1, source_target_pairs={{0,8},{8,0},{16,24},{24,16},{1,9},{9,1},{17,25},{25,17},{2,10},{10... | collective-permute-start | bytes 393224 | tf_op jit(solution)/shard_map/ppermute | solution.py:420
  22.3 28.1 %collective-permute-start = (bf16[24,2,16,128]{3,2,1,0:T(8,128)(2,1)S(1)}, bf16[24,2,16,128]{3,2,1,0:T(8,128)(2,1)S(1)}, u32[]{:S(2)}, u32[]{:S(2)}) collective-permute-start(bf16[24,2,16,128]{3,2,1,0:T(8,128)(2,1)S(1)} %get-tuple-element.22), channel_id=1, source_target_pairs={{0,1},{1,2},{2,3},{3,4},{4,5},{5,6},{6,7},{7,0},{8,9},{9,10},{10,1... | collective-permute-start | bytes 589832 | tf_op jit(solution)/shard_map/ppermute | solution.py:416
  22.3 28.1 %collective-permute-start.1 = (bf16[24,2,16,128]{3,2,1,0:T(8,128)(2,1)S(1)}, bf16[24,2,16,128]{3,2,1,0:T(8,128)(2,1)S(1)}, u32[]{:S(2)}, u32[]{:S(2)}) collective-permute-start(bf16[24,2,16,128]{3,2,1,0:T(8,128)(2,1)S(1)} %get-tuple-element.23), channel_id=1, source_target_pairs={{0,7},{1,0},{2,1},{3,2},{4,3},{5,4},{6,5},{7,6},{8,15},{9,8},{10,9... | collective-permute-start | bytes 589832 | tf_op jit(solution)/shard_map/ppermute | solution.py:416
  30.2 4.3 %collective-permute-start.5 = (bf16[16,16,128]{2,1,0:T(8,128)(2,1)S(1)}, bf16[16,16,128]{2,1,0:T(8,128)(2,1)S(1)}, u32[]{:S(2)}, u32[]{:S(2)}) collective-permute-start(bf16[16,16,128]{2,1,0:T(8,128)(2,1)S(1)} %get-tuple-element.30.pair_ref), channel_id=1, source_target_pairs={{0,16},{8,24},{16,0},{24,8},{1,17},{9,25},{17,1},{25,9},{2,18},{10... | collective-permute-start | bytes 196616 | tf_op jit(solution)/shard_map/ppermute | solution.py:420
  34.7 20.3 %collective-permute-start.7 = (f32[72,128]{1,0:T(8,128)S(1)}, f32[72,128]{1,0:T(8,128)S(1)}, u32[]{:S(2)}, u32[]{:S(2)}) collective-permute-start(f32[72,128]{1,0:T(8,128)S(1)} %get-tuple-element.37), channel_id=1, source_target_pairs={{0,1},{1,2},{2,3},{3,4},{4,5},{5,6},{6,7},{7,0},{8,9},{9,10},{10,1... | collective-permute-start | bytes 110600 | tf_op jit(solution)/shard_map/ppermute | solution.py:416
  36.6 13.9 %copy-start.1 = (bf16[24,16,16,128]{3,2,1,0:T(8,128)(2,1)S(1)}, bf16[24,16,16,128]{3,2,1,0:T(8,128)(2,1)}, u32[]{:S(2)}) copy-start(bf16[24,16,16,128]{3,2,1,0:T(8,128)(2,1)} %field_ref.1) | copy-start | bytes 4718596
  36.6 13.9 %copy-start.5 = (f32[16,16,128]{2,1,0:T(8,128)S(1)}, f32[16,16,128]{2,1,0:T(8,128)}, u32[]{:S(2)}) copy-start(f32[16,16,128]{2,1,0:T(8,128)} %pot_ref.1) | copy-start | bytes 393220
  38.5 16.5 %copy-start.6 = (f32[16,16,128]{2,1,0:T(8,128)S(1)}, f32[16,16,128]{2,1,0:T(8,128)}, u32[]{:S(2)}) copy-start(f32[16,16,128]{2,1,0:T(8,128)} %ionic_ref.1) | copy-start | bytes 393220
  38.5 16.5 %collective-permute-start.6 = (f32[72,128]{1,0:T(8,128)S(1)}, f32[72,128]{1,0:T(8,128)S(1)}, u32[]{:S(2)}, u32[]{:S(2)}) collective-permute-start(f32[72,128]{1,0:T(8,128)S(1)} %get-tuple-element.36.message_ref), channel_id=1, source_target_pairs={{0,7},{1,0},{2,1},{3,2},{4,3},{5,4},{6,5},{7,6},{8,15},{9,8},{10,9... | collective-permute-start | bytes 110600 | tf_op jit(solution)/shard_map/ppermute | solution.py:416
  43.2 3.6 %collective-permute-start.8 = (f32[8,128]{1,0:T(8,128)S(1)}, f32[8,128]{1,0:T(8,128)S(1)}, u32[]{:S(2)}, u32[]{:S(2)}) collective-permute-start(f32[8,128]{1,0:T(8,128)S(1)} %get-tuple-element.41.one_ref), channel_id=1, source_target_pairs={{0,1},{1,0},{2,3},{3,2},{4,5},{5,4},{6,7},{7,6},{8,9},{9,8},{10,11... | collective-permute-start | bytes 12296 | tf_op jit(solution)/shard_map/ppermute | solution.py:420
  46.9 3.6 %collective-permute-start.9 = (f32[8,128]{1,0:T(8,128)S(1)}, f32[8,128]{1,0:T(8,128)S(1)}, u32[]{:S(2)}, u32[]{:S(2)}) collective-permute-start(f32[8,128]{1,0:T(8,128)S(1)} %shard_map.103.one_ref), channel_id=1, source_target_pairs={{0,2},{1,3},{2,0},{3,1},{4,6},{5,7},{6,4},{7,5},{8,10},{9,11},{10,... | collective-permute-start | bytes 12296 | tf_op jit(solution)/shard_map/ppermute | solution.py:420
  50.5 4.5 %collective-permute-start.10 = (f32[8,128]{1,0:T(8,128)S(1)}, f32[8,128]{1,0:T(8,128)S(1)}, u32[]{:S(2)}, u32[]{:S(2)}) collective-permute-start(f32[8,128]{1,0:T(8,128)S(1)} %shard_map.104.one_ref), channel_id=1, source_target_pairs={{0,4},{1,5},{2,6},{3,7},{4,0},{5,1},{6,2},{7,3},{8,12},{9,13},{10,... | collective-permute-start | bytes 12296 | tf_op jit(solution)/shard_map/ppermute | solution.py:420

commit v5 on v4

--- a/solution.py
+++ b/solution.py
@@ -55,44 +55,36 @@
     copy.wait()
 
 
-def prepare_kernel(
-    occ, field_hbm, density_ref, turned_ref, first_ref, last_ref, field_ref, wide_ref, sems
-):
+def density_kernel(occ, field_ref, _, density_ref):
+    count, planes, rows, _ = field_ref.shape
+    for plane in range(planes):
+        total = jnp.zeros((rows, LANES), f32)
+        for o in range(count):
+            cells = field_ref[o, plane].astype(f32)
+            total = total + (occ[o] * cells) * cells
+        density_ref[plane] = total
+
+
+def pair_kernel(partial_ref, partner_ref, pair_ref):
+    pair_ref[...] = (partial_ref[...] + partner_ref[...]).astype(pair_ref.dtype)
+
+
+def turn_kernel(field_ref, turned_ref, first_ref, last_ref, wide_ref):
     count, planes, rows, _ = field_ref.shape
     stride = rows + 1
-    groups = sems.shape[0]
-    size = planes // groups
-    copies = [
-        pltpu.make_async_copy(
-            field_hbm.at[:, pl.ds(g * size, size)], field_ref.at[:, pl.ds(g * size, size)], sems.at[g]
-        )
-        for g in range(groups)
-    ]
-    for copy in copies:
-        copy.start()
-    for g in range(groups):
-        copies[g].wait()
-
-        def one(i):
-            plane = g * size + i
-            total = jnp.zeros((rows, LANES), f32)
-            for o in range(count):
-                cells = field_ref[o, plane].astype(f32)
-                total = total + (occ[o] * cells) * cells
-                wide_ref[i % 2, o * stride : o * stride + rows, :] = cells
-            density_ref[plane] = total
-            turned_ref[plane] = jnp.concatenate(
-                [
-                    pltpu.roll(
-                        wide_ref[i % 2, pl.ds(r, count, stride=stride), :], (SLOT * r) % LANES, 1
-                    )
-                    for r in range(rows)
-                ],
-                axis=1,
-            ).astype(bf16)
-
-        for i in range(size):
-            one(i)
+    for plane in range(planes):
+        turn = plane % 2
+        for o in range(count):
+            wide_ref[turn, o * stride : o * stride + rows, :] = field_ref[o, plane].astype(f32)
+        turned_ref[plane] = jnp.concatenate(
+            [
+                pltpu.roll(
+                    wide_ref[turn, pl.ds(r, count, stride=stride), :], (SLOT * r) % LANES, 1
+                )
+                for r in range(rows)
+            ],
+            axis=1,
+        ).astype(bf16)
     first_ref[...] = field_ref[:, :2]
     last_ref[...] = field_ref[:, planes - 2 :]
 
@@ -145,11 +137,10 @@
 
 
 def own_kernel(
-    starts, turned_ref, proj_ref, coupling_ref, partial_ref, partner_ref,
-    part_ref, shifted_ref, wide_coupling_ref, pair_ref, masks_ref, rows_ref, boxed_ref,
+    starts, turned_ref, proj_ref, coupling_ref,
+    part_ref, shifted_ref, wide_coupling_ref, masks_ref, rows_ref, boxed_ref,
 ):
     atoms, nproj = proj_ref.shape[:2]
-    pair_ref[...] = (partial_ref[...] + partner_ref[...]).astype(pair_ref.dtype)
     planes = turned_ref.shape[0]
     for a in range(atoms):
         offset, column = start_of(starts, a, atoms, planes, False)
@@ -449,22 +440,23 @@
     groups = 4
     stride = rows + 1
     edge_shape = jax.ShapeDtypeStruct((count, 2, rows, lanes), bf16)
-    partial, turned, first, last = call(
-        prepare_kernel, 2,
-        in_specs=[smem(), high_hbm()],
-        out_specs=(vmem(),) * 4,
+    turned, first, last = call(
+        turn_kernel, 2,
+        in_specs=[vmem()],
+        out_specs=(vmem(),) * 3,
         out_shape=(
-            jax.ShapeDtypeStruct((planes, rows, lanes), f32),
             jax.ShapeDtypeStruct((planes, count, rows * lanes), bf16),
             edge_shape,
             edge_shape,
         ),
-        scratch_shapes=[
-            pltpu.VMEM((count, planes, rows, lanes), bf16),
-            pltpu.VMEM((2, count * stride, lanes), f32),
-            pltpu.SemaphoreType.DMA((groups,)),
-        ],
-    )(occupations, orbitals)
+        scratch_shapes=[pltpu.VMEM((2, count * stride, lanes), f32)],
+    )(orbitals)
+    partial = call(
+        density_kernel, 1,
+        in_specs=[smem(), vmem(), hbm()],
+        out_specs=vmem(),
+        out_shape=jax.ShapeDtypeStruct((planes, rows, lanes), f32),
+    )(occupations, orbitals, last)
 
     shifted_shape = jax.ShapeDtypeStruct((atoms, SLOT, (box + 1) * square), bf16)
     gather_scratch = [
@@ -472,19 +464,24 @@
         pltpu.VMEM((2, count, box * square), bf16),
     ]
     mask_shape = jax.ShapeDtypeStruct((atoms, lanes // SLOT, SLOT, lanes), bf16)
-    own_part, own_shifted, wide_coupling, pair, own_masks = call(
+    own_part, own_shifted, wide_coupling, own_masks = call(
         own_kernel, 4,
-        in_specs=[smem()] + [vmem()] * 5,
-        out_specs=(vmem(),) * 5,
+        in_specs=[smem()] + [vmem()] * 3,
+        out_specs=(vmem(),) * 4,
         out_shape=(
             jax.ShapeDtypeStruct((count, slots), f32),
             shifted_shape,
             jax.ShapeDtypeStruct((slots, slots), f32),
-            jax.ShapeDtypeStruct((planes, rows, lanes), bf16),
             mask_shape,
         ),
         scratch_shapes=gather_scratch,
-    )(box_start, turned, projectors, coupling, partial, swap(partial, "band", 1))
+    )(box_start, turned, projectors, coupling)
+    pair = call(
+        pair_kernel, 1,
+        in_specs=[vmem(), vmem()],
+        out_specs=vmem(),
+        out_shape=jax.ShapeDtypeStruct((planes, rows, lanes), bf16),
+    )(partial, swap(partial, "band", 1))
 
     mask = 2
     while 2 * mask < n_band:

time: 62.2 us -> 56 us (0.900)
  starting transfers between devices: 14.7 us -> 12 us
  waiting for transfers between devices: 23.2 us -> 20.5 us
  local copies, waits for them, and re-layouts: 3.26 us -> 2.6 us
    ppermute x6, waiting for transfers between devices: 10.4 us -> 7.61 us  [swap(): lax.ppermute(block, axis, [(i, i ^ mask) for i in range(lax.axis_size(axi...]
    ppermute x5, starting transfers between devices: 12.6 us -> 9.85 us  [around(): lax.ppermute(block, axis, [(i, (i + distance) % count) for i in range(cou...]
    unnamed x20, local copies, waits for them, and re-layouts: 3.26 us -> 2.6 us
    pallas_call x2 -> x4, Pallas kernels: 4.8 us -> 4.65 us  [the longest x1 3.08 us: local(): call(own_kernel, 4, in_specs=[smem()] + [vmem()] * 3, out_specs=(vmem(),)...]
  transfers between devices with their start and end apart: 11 -> 11, of which waited for: 5 -> 4; matrix products, arithmetic and copies ran while one was open for 0% -> 0% of each run, Pallas kernels for 21% -> 23%
where the time goes in v5:
time: 56 us; the launch traced here: 55.8 us
  waiting for transfers between devices  20.5 us (37%)
  Pallas kernels  19.9 us (36%)
  starting transfers between devices  12 us (21%)
  local copies, waits for them, and re-layouts  2.6 us (5%)
  between operations  0.8 us (1%)
    ppermute x5, waiting for transfers between devices, around(): lax.ppermute(block, axis, [(i, (i + distance) % count) for i in range(cou...  12.9 us
    ppermute x5, starting transfers between devices, around(): lax.ppermute(block, axis, [(i, (i + distance) % count) for i in range(cou...  9.85 us
    ppermute x6, waiting for transfers between devices, swap(): lax.ppermute(block, axis, [(i, i ^ mask) for i in range(lax.axis_size(axi...  7.61 us
    pallas_call x1, Pallas kernels, local(): call(final_kernel, 6, in_specs=[smem()] + [vmem()] * 14, out_specs=(hbm()...  6.31 us
    pallas_call x1, Pallas kernels, local(): call(stencil_kernel, 4, in_specs=[smem()] + [vmem()] * 4, out_specs=(vmem...  4.07 us
    pallas_call x1, Pallas kernels, local(): call(own_kernel, 4, in_specs=[smem()] + [vmem()] * 3, out_specs=(vmem(),)...  3.08 us
    unnamed x20, local copies, waits for them, and re-layouts  2.6 us
    ppermute x6, starting transfers between devices, swap(): lax.ppermute(block, axis, [(i, i ^ mask) for i in range(lax.axis_size(axi...  2.14 us
  transfers between devices with their start and end apart: 11, of which 4 were waited for; matrix products, arithmetic and copies ran while one was open for 0% of the time, Pallas kernels for 23%

profile of v5, /device:TPU:0, one launch (start us, length us, event | category | flops | bytes accessed | tf_op | source)
XLA Modules:
  0.0 55.8 jit_solution(10301582107070013293)
XLA Ops:
  0.6 1.1 %copy-done.2 = bf16[8,13,16,256]{3,2,1,0:T(8,128)(2,1)S(1)} copy-done((bf16[8,13,16,256]{3,2,1,0:T(8,128)(2,1)S(1)}, bf16[8,13,16,256]{3,2,1,0:T(8,128)(2,1)}, u32[]{:S(2)}) %copy-start.2) | copy-done | bytes 851992
  1.8 0.3 shard_map.98
  2.1 3.0 %collective-permute-start.2 = (bf16[4,13,16,256]{3,2,1,0:T(8,128)(2,1)S(1)}, bf16[4,13,16,256]{3,2,1,0:T(8,128)(2,1)S(1)}, u32[]{:S(2)}, u32[]{:S(2)}) collective-permute-start(bf16[4,13,16,256]{3,2,1,0:T(8,128)(2,1)S(1)} %shard_map.98), channel_id=1, source_target_pairs={{0,1},{1,2},{2,3},{3,4},{4,5},{5,6},{6,7},{7,0},{8,9},{9,10},{10,1... | collective-permute-start | bytes 1277960 | tf_op jit(solution)/shard_map/ppermute | solution.py:407
  5.1 12.9 %collective-permute-done.2.mine_ref = bf16[4,13,16,256]{3,2,1,0:T(8,128)(2,1)S(1)} collective-permute-done((bf16[4,13,16,256]{3,2,1,0:T(8,128)(2,1)S(1)}, bf16[4,13,16,256]{3,2,1,0:T(8,128)(2,1)S(1)}, u32[]{:S(2)}, u32[]{:S(2)}) %collective-permute-start.2) | collective-permute-done | bytes 426016 | tf_op jit(solution)/shard_map/ppermute | solution.py:407
  18.0 1.4 %copy-done = bf16[24,16,16,128]{3,2,1,0:T(8,128)(2,1)S(1)} copy-done((bf16[24,16,16,128]{3,2,1,0:T(8,128)(2,1)S(1)}, bf16[24,16,16,128]{3,2,1,0:T(8,128)(2,1)}, u32[]{:S(2)}) %copy-start) | copy-done | bytes 1572888
  19.4 0.6 %shard_map.95 = (bf16[16,24,2048]{2,1,0:T(8,128)(2,1)S(1)}, bf16[24,2,16,128]{3,2,1,0:T(8,128)(2,1)S(1)}, bf16[24,2,16,128]{3,2,1,0:T(8,128)(2,1)S(1)}) custom-call(bf16[24,16,16,128]{3,2,1,0:T(8,128)(2,1)S(1)} %copy-done), custom_call_target="tpu_custom_call" | custom-call | flops 1000000 | bytes 2000000 | tf_op jit(solution)/shard_map/pallas_call | solution.py:443
  20.0 1.0 %shard_map.100.partial_ref = f32[16,16,128]{2,1,0:T(8,128)S(1)} custom-call(f32[24]{0:T(128)S(1)} %copy-done.9, bf16[24,16,16,128]{3,2,1,0:T(8,128)(2,1)S(1)} %copy-done, bf16[24,2,16,128]{3,2,1,0:T(8,128)(2,1)S(1)} %get-tuple-element.20._), custom_call_target="tpu_custom_call" | custom-call | flops 500000 | bytes 1000000 | tf_op jit(solution)/shard_map/pallas_call | solution.py:454
  21.0 0.6 %collective-permute-start.4 = (f32[16,16,128]{2,1,0:T(8,128)S(1)}, f32[16,16,128]{2,1,0:T(8,128)S(1)}, u32[]{:S(2)}, u32[]{:S(2)}) collective-permute-start(f32[16,16,128]{2,1,0:T(8,128)S(1)} %shard_map.100.partial_ref), channel_id=1, source_target_pairs={{0,8},{8,0},{16,24},{24,16},{1,9},{9,1},{17,25},{25,17},{2,10},{10... | collective-permute-start | bytes 393224 | tf_op jit(solution)/shard_map/ppermute | solution.py:411
  21.5 1.7 %collective-permute-start.1 = (bf16[24,2,16,128]{3,2,1,0:T(8,128)(2,1)S(1)}, bf16[24,2,16,128]{3,2,1,0:T(8,128)(2,1)S(1)}, u32[]{:S(2)}, u32[]{:S(2)}) collective-permute-start(bf16[24,2,16,128]{3,2,1,0:T(8,128)(2,1)S(1)} %get-tuple-element.21), channel_id=1, source_target_pairs={{0,7},{1,0},{2,1},{3,2},{4,3},{5,4},{6,5},{7,6},{8,15},{9,8},{10,9... | collective-permute-start | bytes 589832 | tf_op jit(solution)/shard_map/ppermute | solution.py:407
  23.3 0.3 collective-permute-start
  23.6 1.6 %collective-permute-start.5 = (bf16[16,16,128]{2,1,0:T(8,128)(2,1)S(1)}, bf16[16,16,128]{2,1,0:T(8,128)(2,1)S(1)}, u32[]{:S(2)}, u32[]{:S(2)}) collective-permute-start(bf16[16,16,128]{2,1,0:T(8,128)(2,1)S(1)} %shard_map.101.pair_ref), channel_id=1, source_target_pairs={{0,16},{8,24},{16,0},{24,8},{1,17},{9,25},{17,1},{25,9},{2,18},{10... | collective-permute-start | bytes 196616 | tf_op jit(solution)/shard_map/ppermute | solution.py:411
  25.2 3.1 %shard_map.97 = (f32[24,128]{1,0:T(8,128)S(1)}, bf16[8,16,4352]{2,1,0:T(8,128)(2,1)S(1)}, f32[128,128]{1,0:T(8,128)S(1)}, bf16[8,8,16,128]{3,2,1,0:T(8,128)(2,1)S(1)}) custom-call(s32[3,64]{1,0:T(4,128)S(1)} %copy-done.7, bf16[16,24,2048]{2,1,0:T(8,128)(2,1)S(1)} %get-tuple-element.23.turned_ref, bf16[8,13,16,256]{3,2,1,0:T(8,128)(2,1)S(1)} %copy-done.3, ...), custom_call_target="tpu_custom_call" | custom-call | flops 2000000 | bytes 4000000 | tf_op jit(solution)/shard_map/pallas_call | solution.py:467
  28.3 0.2 shard_map.102
  28.4 0.1 collective-permute-start.7
  28.5 1.8 %shard_map.99 = (f32[24,128]{1,0:T(8,128)S(1)}, bf16[4,16,4352]{2,1,0:T(8,128)(2,1)S(1)}) custom-call(s32[3,64]{1,0:T(4,128)S(1)} %copy-done.7, bf16[16,24,2048]{2,1,0:T(8,128)(2,1)S(1)} %get-tuple-element.23.turned_ref, bf16[4,13,16,256]{3,2,1,0:T(8,128)(2,1)S(1)} %collective-permute-done.2.mine_ref), custom_call_target="tpu_custom_call" | custom-call | flops 1000000 | bytes 2000000 | tf_op jit(solution)/shard_map/pallas_call | solution.py:515
  30.3 0.0 copy-start.5
  30.4 1.9 %shard_map.103 = (f32[72,128]{1,0:T(8,128)S(1)}, bf16[4,16,4352]{2,1,0:T(8,128)(2,1)S(1)}) custom-call(s32[3,64]{1,0:T(4,128)S(1)} %copy-done.7, bf16[16,24,2048]{2,1,0:T(8,128)(2,1)S(1)} %get-tuple-element.23.turned_ref, bf16[4,13,16,256]{3,2,1,0:T(8,128)(2,1)S(1)} %collective-permute-done.3.other_ref, f32[24,128]{1,0:T(8,128)S(1)} %get-tuple-element.26.half_ref, ...), custom_call_target="tpu_custom_call" | custom-call | flops 1000000 | bytes 2000000 | tf_op jit(solution)/shard_map/pallas_call | solution.py:522
  32.3 4.7 %collective-permute-start.6 = (f32[72,128]{1,0:T(8,128)S(1)}, f32[72,128]{1,0:T(8,128)S(1)}, u32[]{:S(2)}, u32[]{:S(2)}) collective-permute-start(f32[72,128]{1,0:T(8,128)S(1)} %get-tuple-element.32.message_ref), channel_id=1, source_target_pairs={{0,7},{1,0},{2,1},{3,2},{4,3},{5,4},{6,5},{7,6},{8,15},{9,8},{10,9... | collective-permute-start | bytes 110600 | tf_op jit(solution)/shard_map/ppermute | solution.py:407
  37.0 3.6 %collective-permute-done.8.other_ref = f32[8,128]{1,0:T(8,128)S(1)} collective-permute-done((f32[8,128]{1,0:T(8,128)S(1)}, f32[8,128]{1,0:T(8,128)S(1)}, u32[]{:S(2)}, u32[]{:S(2)}) %collective-permute-start.8) | collective-permute-done | bytes 4128 | tf_op jit(solution)/shard_map/ppermute | solution.py:411
  40.6 3.6 %collective-permute-done.9.other_ref = f32[8,128]{1,0:T(8,128)S(1)} collective-permute-done((f32[8,128]{1,0:T(8,128)S(1)}, f32[8,128]{1,0:T(8,128)S(1)}, u32[]{:S(2)}, u32[]{:S(2)}) %collective-permute-start.9) | collective-permute-done | bytes 4128 | tf_op jit(solution)/shard_map/ppermute | solution.py:411
  44.3 4.1 %shard_map.96 = (f32[24,16,16,128]{3,2,1,0:T(8,128)S(1)}, bf16[8,8,16,128]{3,2,1,0:T(8,128)(2,1)S(1)}) custom-call(s32[3,64]{1,0:T(4,128)S(1)} %copy-done.7, bf16[24,16,16,128]{3,2,1,0:T(8,128)(2,1)S(1)} %copy-done.1, bf16[24,2,16,128]{3,2,1,0:T(8,128)(2,1)S(1)} %collective-permute-done.low_ref, ...), custom_call_target="tpu_custom_call" | custom-call | flops 2000000 | bytes 4000000 | tf_op jit(solution)/shard_map/pallas_call | solution.py:532
  48.4 0.4 collective-permute-done.10.other_ref
  48.8 6.3 %shard_map.104 = (bf16[24,16,16,128]{3,2,1,0:T(8,128)(2,1)}, f32[16,16,128]{2,1,0:T(8,128)S(1)}) custom-call(s32[3,64]{1,0:T(4,128)S(1)} %copy-done.7, f32[24,16,16,128]{3,2,1,0:T(8,128)S(1)} %get-tuple-element.22.acc_ref, bf16[8,16,4352]{2,1,0:T(8,128)(2,1)S(1)} %get-tuple-element.24.own_ref, bf16[4,16,4352]{2,1,0:T(8,128)(2,1)S(1)} %get-tuple-element.25.mine_ref, ...), custom_call_target="tpu_custom_call" | custom-call | flops 3000000 | bytes 6000000 | tf_op jit(solution)/shard_map/pallas_call | solution.py:540
  55.1 0.7 %shard_map.108 = f32[16,16,128]{2,1,0:T(8,128)} custom-call(f32[16,16,128]{2,1,0:T(8,128)S(1)} %get-tuple-element.36.pot_ref, f32[8,128]{1,0:T(8,128)S(1)} %shard_map.107.charge_ref), custom_call_target="tpu_custom_call" | custom-call | flops 500000 | bytes 1000000 | tf_op jit(solution)/shard_map/pallas_call | solution.py:557
  (32 shorter events, 0.1 us)
Async XLA Ops:
  0.6 1.2 %copy-start.2 = (bf16[8,13,16,256]{3,2,1,0:T(8,128)(2,1)S(1)}, bf16[8,13,16,256]{3,2,1,0:T(8,128)(2,1)}, u32[]{:S(2)}) copy-start(bf16[8,13,16,256]{3,2,1,0:T(8,128)(2,1)} %proj_ref.3) | copy-start | bytes 2555908
  1.8 18.2 %copy-start.9 = (f32[24]{0:T(128)S(1)}, f32[24]{0:T(128)}, u32[]{:S(2)}) copy-start(f32[24]{0:T(128)} %occ.1) | copy-start | bytes 292
  1.8 23.4 %copy-start.3 = (bf16[8,13,16,256]{3,2,1,0:T(8,128)(2,1)S(1)}, bf16[8,13,16,256]{3,2,1,0:T(8,128)(2,1)}, u32[]{:S(2)}) copy-start(bf16[8,13,16,256]{3,2,1,0:T(8,128)(2,1)} %proj_ref.3) | copy-start | bytes 2555908
  1.8 23.4 %copy-start.7 = (s32[3,64]{1,0:T(4,128)S(1)}, s32[3,64]{1,0:T(4,128)}, u32[]{:S(2)}) copy-start(s32[3,64]{1,0:T(4,128)} %starts.9) | copy-start | bytes 2308
  1.8 23.4 %copy-start.8 = (f32[13,13]{1,0:T(8,128)S(1)}, f32[13,13]{1,0:T(8,128)}, u32[]{:S(2)}) copy-start(f32[13,13]{1,0:T(8,128)} %coupling_ref.1) | copy-start | bytes 2032
  2.1 15.9 %collective-permute-start.2 = (bf16[4,13,16,256]{3,2,1,0:T(8,128)(2,1)S(1)}, bf16[4,13,16,256]{3,2,1,0:T(8,128)(2,1)S(1)}, u32[]{:S(2)}, u32[]{:S(2)}) collective-permute-start(bf16[4,13,16,256]{3,2,1,0:T(8,128)(2,1)S(1)} %shard_map.98), channel_id=1, source_target_pairs={{0,1},{1,2},{2,3},{3,4},{4,5},{5,6},{6,7},{7,0},{8,9},{9,10},{10,1... | collective-permute-start | bytes 1277960 | tf_op jit(solution)/shard_map/ppermute | solution.py:407
  18.0 12.4 %collective-permute-start.3 = (bf16[4,13,16,256]{3,2,1,0:T(8,128)(2,1)S(1)}, bf16[4,13,16,256]{3,2,1,0:T(8,128)(2,1)S(1)}, u32[]{:S(2)}, u32[]{:S(2)}) collective-permute-start(bf16[4,13,16,256]{3,2,1,0:T(8,128)(2,1)S(1)} %collective-permute-done.2.mine_ref), channel_id=1, source_target_pairs={{0,8},{8,0},{16,24},{24,16},{1,9},{9,1},{17,25},{25,17},{2,10},{10... | collective-permute-start | bytes 1277960 | tf_op jit(solution)/shard_map/ppermute | solution.py:411
  18.0 1.4 %copy-start = (bf16[24,16,16,128]{3,2,1,0:T(8,128)(2,1)S(1)}, bf16[24,16,16,128]{3,2,1,0:T(8,128)(2,1)}, u32[]{:S(2)}) copy-start(bf16[24,16,16,128]{3,2,1,0:T(8,128)(2,1)} %field_ref.5) | copy-start | bytes 4718596
  21.0 7.3 %copy-start.4 = (f32[16,16,128]{2,1,0:T(8,128)S(1)}, f32[16,16,128]{2,1,0:T(8,128)}, u32[]{:S(2)}) copy-start(f32[16,16,128]{2,1,0:T(8,128)} %hart_ref.5) | copy-start | bytes 393220
  21.0 2.6 %collective-permute-start.4 = (f32[16,16,128]{2,1,0:T(8,128)S(1)}, f32[16,16,128]{2,1,0:T(8,128)S(1)}, u32[]{:S(2)}, u32[]{:S(2)}) collective-permute-start(f32[16,16,128]{2,1,0:T(8,128)S(1)} %shard_map.100.partial_ref), channel_id=1, source_target_pairs={{0,8},{8,0},{16,24},{24,16},{1,9},{9,1},{17,25},{25,17},{2,10},{10... | collective-permute-start | bytes 393224 | tf_op jit(solution)/shard_map/ppermute | solution.py:411
  21.5 22.7 %collective-permute-start.1 = (bf16[24,2,16,128]{3,2,1,0:T(8,128)(2,1)S(1)}, bf16[24,2,16,128]{3,2,1,0:T(8,128)(2,1)S(1)}, u32[]{:S(2)}, u32[]{:S(2)}) collective-permute-start(bf16[24,2,16,128]{3,2,1,0:T(8,128)(2,1)S(1)} %get-tuple-element.21), channel_id=1, source_target_pairs={{0,7},{1,0},{2,1},{3,2},{4,3},{5,4},{6,5},{7,6},{8,15},{9,8},{10,9... | collective-permute-start | bytes 589832 | tf_op jit(solution)/shard_map/ppermute | solution.py:407
  23.3 21.0 %collective-permute-start = (bf16[24,2,16,128]{3,2,1,0:T(8,128)(2,1)S(1)}, bf16[24,2,16,128]{3,2,1,0:T(8,128)(2,1)S(1)}, u32[]{:S(2)}, u32[]{:S(2)}) collective-permute-start(bf16[24,2,16,128]{3,2,1,0:T(8,128)(2,1)S(1)} %get-tuple-element.20._), channel_id=1, source_target_pairs={{0,1},{1,2},{2,3},{3,4},{4,5},{5,6},{6,7},{7,0},{8,9},{9,10},{10,1... | collective-permute-start | bytes 589832 | tf_op jit(solution)/shard_map/ppermute | solution.py:407
  23.6 4.7 %collective-permute-start.5 = (bf16[16,16,128]{2,1,0:T(8,128)(2,1)S(1)}, bf16[16,16,128]{2,1,0:T(8,128)(2,1)S(1)}, u32[]{:S(2)}, u32[]{:S(2)}) collective-permute-start(bf16[16,16,128]{2,1,0:T(8,128)(2,1)S(1)} %shard_map.101.pair_ref), channel_id=1, source_target_pairs={{0,16},{8,24},{16,0},{24,8},{1,17},{9,25},{17,1},{25,9},{2,18},{10... | collective-permute-start | bytes 196616 | tf_op jit(solution)/shard_map/ppermute | solution.py:411
  28.4 20.3 %collective-permute-start.7 = (f32[72,128]{1,0:T(8,128)S(1)}, f32[72,128]{1,0:T(8,128)S(1)}, u32[]{:S(2)}, u32[]{:S(2)}) collective-permute-start(f32[72,128]{1,0:T(8,128)S(1)} %get-tuple-element.33), channel_id=1, source_target_pairs={{0,1},{1,2},{2,3},{3,4},{4,5},{5,6},{6,7},{7,0},{8,9},{9,10},{10,1... | collective-permute-start | bytes 110600 | tf_op jit(solution)/shard_map/ppermute | solution.py:407
  30.3 13.9 %copy-start.1 = (bf16[24,16,16,128]{3,2,1,0:T(8,128)(2,1)S(1)}, bf16[24,16,16,128]{3,2,1,0:T(8,128)(2,1)}, u32[]{:S(2)}) copy-start(bf16[24,16,16,128]{3,2,1,0:T(8,128)(2,1)} %field_ref.5) | copy-start | bytes 4718596
  30.3 13.9 %copy-start.5 = (f32[16,16,128]{2,1,0:T(8,128)S(1)}, f32[16,16,128]{2,1,0:T(8,128)}, u32[]{:S(2)}) copy-start(f32[16,16,128]{2,1,0:T(8,128)} %pot_ref.1) | copy-start | bytes 393220
  32.3 16.5 %copy-start.6 = (f32[16,16,128]{2,1,0:T(8,128)S(1)}, f32[16,16,128]{2,1,0:T(8,128)}, u32[]{:S(2)}) copy-start(f32[16,16,128]{2,1,0:T(8,128)} %ionic_ref.1) | copy-start | bytes 393220
  32.3 16.5 %collective-permute-start.6 = (f32[72,128]{1,0:T(8,128)S(1)}, f32[72,128]{1,0:T(8,128)S(1)}, u32[]{:S(2)}, u32[]{:S(2)}) collective-permute-start(f32[72,128]{1,0:T(8,128)S(1)} %get-tuple-element.32.message_ref), channel_id=1, source_target_pairs={{0,7},{1,0},{2,1},{3,2},{4,3},{5,4},{6,5},{7,6},{8,15},{9,8},{10,9... | collective-permute-start | bytes 110600 | tf_op jit(solution)/shard_map/ppermute | solution.py:407
  37.0 3.6 %collective-permute-start.8 = (f32[8,128]{1,0:T(8,128)S(1)}, f32[8,128]{1,0:T(8,128)S(1)}, u32[]{:S(2)}, u32[]{:S(2)}) collective-permute-start(f32[8,128]{1,0:T(8,128)S(1)} %get-tuple-element.37.one_ref), channel_id=1, source_target_pairs={{0,1},{1,0},{2,3},{3,2},{4,5},{5,4},{6,7},{7,6},{8,9},{9,8},{10,11... | collective-permute-start | bytes 12296 | tf_op jit(solution)/shard_map/ppermute | solution.py:411
  40.6 3.6 %collective-permute-start.9 = (f32[8,128]{1,0:T(8,128)S(1)}, f32[8,128]{1,0:T(8,128)S(1)}, u32[]{:S(2)}, u32[]{:S(2)}) collective-permute-start(f32[8,128]{1,0:T(8,128)S(1)} %shard_map.105.one_ref), channel_id=1, source_target_pairs={{0,2},{1,3},{2,0},{3,1},{4,6},{5,7},{6,4},{7,5},{8,10},{9,11},{10,... | collective-permute-start | bytes 12296 | tf_op jit(solution)/shard_map/ppermute | solution.py:411
  44.2 4.5 %collective-permute-start.10 = (f32[8,128]{1,0:T(8,128)S(1)}, f32[8,128]{1,0:T(8,128)S(1)}, u32[]{:S(2)}, u32[]{:S(2)}) collective-permute-start(f32[8,128]{1,0:T(8,128)S(1)} %shard_map.106.one_ref), channel_id=1, source_target_pairs={{0,4},{1,5},{2,6},{3,7},{4,0},{5,1},{6,2},{7,3},{8,12},{9,13},{10,... | collective-permute-start | bytes 12296 | tf_op jit(solution)/shard_map/ppermute | solution.py:411
